TPU v7x, 32 devices: a whole 2x2x4 slice. The times are simulated.
32 devices in a mesh: star: 2 (over core), dev: 16 (over z, y, x).
Axes of the slice: x: 2, y: 2, z: 4, core: 2. Of those that a mesh axis runs over, the one named last changes fastest.
Arguments:
- screens: bfloat16 [3, 32, 256, 8192], P(None, None, 'dev', 'star'), may hold values from -4 to 4
- foot_rows: int32 [3, 2], replicated, may hold values from 0 to 8191
- foot_cols: int32 [3, 2], replicated, may hold values from 0 to 6784
- wind: int32 [3, 3, 2], replicated, may hold values from 0 to 15
- amplitude: float32 [256, 1280], P('dev'), may hold values from 0.5 to 1.5
- owner: int32 [2, 16], P('star', 'dev'), may hold values from 0 to 5
- refs: float32 [6, 16, 16], replicated, may hold values from 0.1 to 1
Outputs:
- correlation: float32 [3, 2, 16, 80, 256], P(None, 'star', 'dev')
All inputs are finite; a program needn't handle non-finite values.
Results may differ from a plain program's by a relative error of at most 0.0003.
Values may be sent and summed in bfloat16 or wider, within the bound.
No kernel may reach another device: no remote copies, remote signals or barrier semaphores. Data moves between devices by JAX's collectives and lax.ppermute only.
A program may use at most 128 MiB of HBM per device.

v0:
```python
import math

import jax
import jax.numpy as jnp
from jax import lax
from jax.sharding import PartitionSpec as P

BIN = 4
MARGIN = 128
STEPS = 3


def from_behind(array, axis, by):
    size = lax.axis_size(axis)
    return lax.ppermute(array, axis, [(i, (i + by) % size) for i in range(size)])


def dft_tables(length, count, offset):
    freq = jnp.arange(length, dtype=jnp.int32)
    place = jnp.arange(count, dtype=jnp.int32)
    index = ((freq + offset) % length)[:, None] * place[None, :] % length
    angle = index.astype(jnp.float32) * (2.0 * math.pi / length)
    return (jnp.cos(angle), -jnp.sin(angle))


def contract(form, left, right):
    return jnp.einsum(
        form, left, right, precision=lax.Precision.HIGHEST, preferred_element_type=jnp.float32
    )


def spectra(image, real_tab, imag_tab):
    first_real = contract("km,bmn->bkn", real_tab, image)
    first_imag = contract("km,bmn->bkn", imag_tab, image)
    out_real = contract("bkn,ln->bkl", first_real, real_tab) - contract(
        "bkn,ln->bkl", first_imag, imag_tab
    )
    out_imag = contract("bkn,ln->bkl", first_real, imag_tab) + contract(
        "bkn,ln->bkl", first_imag, real_tab
    )
    return (out_real, out_imag)


def spot_rows(phase, amplitude, ref_real, ref_imag):
    side = phase.shape[0]
    across = phase.shape[1] // side
    blocks = phase.reshape(side, across, side).transpose(1, 0, 2)
    amps = amplitude.reshape(side, across, side).transpose(1, 0, 2)
    field_real = amps * jnp.cos(blocks)
    field_imag = amps * jnp.sin(blocks)
    length = BIN * side
    shift_real, shift_imag = dft_tables(length, side, length // 2)
    left_real = contract("kn,bnm->bkm", shift_real, field_real) - contract(
        "kn,bnm->bkm", shift_imag, field_imag
    )
    left_imag = contract("kn,bnm->bkm", shift_real, field_imag) + contract(
        "kn,bnm->bkm", shift_imag, field_real
    )
    full_real = contract("bkm,lm->bkl", left_real, shift_real) - contract(
        "bkm,lm->bkl", left_imag, shift_imag
    )
    full_imag = contract("bkm,lm->bkl", left_real, shift_imag) + contract(
        "bkm,lm->bkl", left_imag, shift_real
    )
    power = full_real * full_real + full_imag * full_imag
    pixels = length // BIN
    binned = power.reshape(across, pixels, BIN, pixels, BIN).sum(axis=(2, 4))
    image = binned / jnp.sum(binned, axis=(1, 2), keepdims=True)
    grid_real, grid_imag = dft_tables(pixels, pixels, 0)
    spec_real, spec_imag = spectra(image, grid_real, grid_imag)
    prod_real = spec_real * ref_real + spec_imag * ref_imag
    prod_imag = spec_imag * ref_real - spec_real * ref_imag
    inner_real = contract("km,bmn->bkn", grid_real, prod_real) + contract(
        "km,bmn->bkn", grid_imag, prod_imag
    )
    inner_imag = contract("km,bmn->bkn", grid_real, prod_imag) - contract(
        "km,bmn->bkn", grid_imag, prod_real
    )
    result = contract("bkn,ln->bkl", inner_real, grid_real) + contract(
        "bkn,ln->bkl", inner_imag, grid_imag
    )
    result = result / float(pixels * pixels)
    return result.reshape(across, pixels * pixels)


def cut_phase(stacked, tops, lefts, side, across):

    def cut_one_layer(block, top, left):
        return lax.dynamic_slice(block, (top, left), (side, across))

    pieces = jax.vmap(cut_one_layer)(stacked, tops, lefts)
    return jnp.sum(pieces.astype(jnp.float32), axis=0)


def candidates(window, first, bands):
    ids = (first[:, None] + jnp.arange(3, dtype=jnp.int32)[None, :]) % bands

    def candidates_one_layer(block, wanted):
        return jnp.take(block, wanted, axis=0)

    return jax.vmap(candidates_one_layer)(window, ids)


def pick_band(stack, index):

    def pick_one_layer(block, which):
        return lax.dynamic_index_in_dim(block, which, 0, keepdims=False)

    return jax.vmap(pick_one_layer)(stack, index)


def shards(screens, foot_rows, foot_cols, wind, amplitude, owner, refs):
    star = lax.axis_index("star")
    place = lax.axis_index("dev")
    bands = screens.shape[1]
    side = screens.shape[2]
    across = amplitude.shape[1]
    span = across + MARGIN
    devices = lax.axis_size("dev")
    total_rows = bands * side * devices
    bits = devices.bit_length() - 1
    panels = lax.all_gather(screens, "star", axis=3, tiled=True)
    row_base = lax.dynamic_index_in_dim(foot_rows, star, 1, keepdims=False)
    col_base = lax.dynamic_index_in_dim(foot_cols, star, 1, keepdims=False)

    def crop(block, start):
        return lax.dynamic_slice_in_dim(block, start, span, 2)

    window = jax.vmap(crop)(panels, col_base)
    camera = owner[0, 0]
    refer = lax.dynamic_index_in_dim(refs, camera, 0, keepdims=True)
    pixels = refs.shape[1]
    grid_real, grid_imag = dft_tables(pixels, pixels, 0)
    ref_real, ref_imag = spectra(refer, grid_real, grid_imag)
    last_one = (place == devices - 1).astype(jnp.int32)
    results = []
    for step in range(STEPS):
        offset = (row_base + wind[step, :, 0]) % total_rows
        strip = offset // side
        first = strip // devices
        turn = strip % devices
        lows = offset % side
        cand = candidates(window, first, bands)
        own_pos = (place < turn).astype(jnp.int32)
        following = from_behind(cand, "dev", -1)
        current = jnp.concatenate(
            [pick_band(cand, own_pos), pick_band(following, own_pos + last_one)], axis=1
        )
        for bit in range(bits):
            moved = from_behind(current, "dev", -(1 << bit))
            flags = turn >> bit & 1 == 1
            current = jnp.where(flags[:, None, None], moved, current)
        phase = cut_phase(current, lows, wind[step, :, 1], side, across)
        results.append(spot_rows(phase, amplitude, ref_real, ref_imag))
    return jnp.stack(results)[:, None, None]


def solution(mesh):
    in_specs = (P(None, None, "dev", "star"), P(), P(), P(), P("dev", None), P("star", "dev"), P())
    out_specs = P(None, "star", "dev", None, None)
    return jax.shard_map(shards, mesh=mesh, in_specs=in_specs, out_specs=out_specs, check_vma=False)
```

profile of v0, /device:TPU:0, one launch (start us, length us, event | category | flops | bytes accessed | tf_op | source)
XLA Modules:
  0.0 270.2 jit_solution(3464391387708898479)
XLA Ops:
  11.0 41.0 %all-gather.2.cloned.1.call-done = bf16[3,32,16,8192]{3,2,1,0:T(8,128)(2,1)} async-done(((bf16[3,32,16,4096]{3,2,1,0:T(8,128)(2,1)}), bf16[3,32,16,8192]{3,2,1,0:T(8,128)(2,1)}) %all-gather.2.cloned.1.call-update) | async-done | bytes 25165840 | tf_op jit(solution)/shard_map/all_gather | solution.py:122
  52.0 16.5 %while.4 = (s32[]{:T(128)}, bf16[3,32,16,8192]{3,2,1,0:T(8,128)(2,1)}, s32[3,4]{1,0:T(4,128)S(1)}, bf16[3,32,16,1408]{3,2,1,0:T(8,128)(2,1)}, s32[]{:T(128)}) while((s32[]{:T(128)}, bf16[3,32,16,8192]{3,2,1,0:T(8,128)(2,1)}, s32[3,4]{1,0:T(4,128)S(1)}, bf16[3,32,16,1408]{3,2,1,0:T(8,128)(2,1)}, s32[]{:T(128)}) %tuple.126), condition=%wide.while_cond, body=%wide.while_body.sunk | while | flops 2 | bytes 2884733 | solution.py:127
  52.7 4.9 %dynamic-slice_dynamic-update-slice_fusion.8 = bf16[3,32,16,1408]{3,2,1,0:T(8,128)(2,1)} fusion(bf16[3,32,16,1408]{3,2,1,0:T(8,128)(2,1)} %get-tuple-element.331, s32[]{:T(128)S(6)} %copy.265, bf16[3,32,16,8192]{3,2,1,0:T(8,128)(2,1)} %get-tuple-element.334, s32[]{:T(128)} %bitcast.326, s32[]{:T(128)} %bitcast.327), kind=kLoop, calls=%fused_computation.9.clone.1 | loop fusion | bytes 2884612 | tf_op jit(solution)/shard_map/vmap()/gather
  58.2 4.8 %dynamic-slice_dynamic-update-slice_fusion.8 = bf16[3,32,16,1408]{3,2,1,0:T(8,128)(2,1)} fusion(bf16[3,32,16,1408]{3,2,1,0:T(8,128)(2,1)} %get-tuple-element.331, s32[]{:T(128)S(6)} %copy.265, bf16[3,32,16,8192]{3,2,1,0:T(8,128)(2,1)} %get-tuple-element.334, s32[]{:T(128)} %bitcast.326, s32[]{:T(128)} %bitcast.327), kind=kLoop, calls=%fused_computation.9.clone.1 | loop fusion | bytes 2884612 | tf_op jit(solution)/shard_map/vmap()/gather
  63.6 4.9 %dynamic-slice_dynamic-update-slice_fusion.8 = bf16[3,32,16,1408]{3,2,1,0:T(8,128)(2,1)} fusion(bf16[3,32,16,1408]{3,2,1,0:T(8,128)(2,1)} %get-tuple-element.331, s32[]{:T(128)S(6)} %copy.265, bf16[3,32,16,8192]{3,2,1,0:T(8,128)(2,1)} %get-tuple-element.334, s32[]{:T(128)} %bitcast.326, s32[]{:T(128)} %bitcast.327), kind=kLoop, calls=%fused_computation.9.clone.1 | loop fusion | bytes 2884612 | tf_op jit(solution)/shard_map/vmap()/gather
  68.5 2.9 %gather_fusion.6 = bf16[9,16,1408]{2,1,0:T(8,128)(2,1)S(1)} fusion(bf16[3,32,16,1408]{3,2,1,0:T(8,128)(2,1)} %get-tuple-element.13, s32[9]{0:T(128)S(1)} %reshape.589), kind=kCustom, calls=%fused_computation.clone | custom fusion | bytes 811080 | tf_op jit(solution)/shard_map/vmap(jit(_take))/gather | solution.py:99
  71.5 5.5 %collective-permute-start = (bf16[3,3,16,1408]{3,2,1,0:T(8,128)(2,1)S(1)}, bf16[3,3,16,1408]{3,2,1,0:T(8,128)(2,1)}, u32[]{:S(2)}, u32[]{:S(2)}) collective-permute-start(bf16[3,3,16,1408]{3,2,1,0:T(8,128)(2,1)S(1)} %broadcast_select_fusion.2), channel_id=1, source_target_pairs={{0,15},{1,0},{2,1},{3,2},{4,3},{5,4},{6,5},{7,6},{8,7},{9,8},{10,9... | collective-permute-start | bytes 1216520 | tf_op jit(solution)/shard_map/ppermute | solution.py:15
  77.5 2.9 %gather_fusion.7 = bf16[9,16,1408]{2,1,0:T(8,128)(2,1)S(1)} fusion(bf16[3,32,16,1408]{3,2,1,0:T(8,128)(2,1)} %get-tuple-element.13, s32[9]{0:T(128)S(1)} %reshape.594), kind=kCustom, calls=%fused_computation.1.clone | custom fusion | bytes 811080 | tf_op jit(solution)/shard_map/vmap(jit(_take))/gather | solution.py:99
  81.7 2.9 %gather_fusion.8 = bf16[9,16,1408]{2,1,0:T(8,128)(2,1)S(1)} fusion(bf16[3,32,16,1408]{3,2,1,0:T(8,128)(2,1)} %get-tuple-element.13, s32[9]{0:T(128)S(1)} %reshape.599), kind=kCustom, calls=%fused_computation.2.clone | custom fusion | bytes 811080 | tf_op jit(solution)/shard_map/vmap(jit(_take))/gather | solution.py:99
  88.5 6.0 %collective-permute-start.1 = (bf16[3,32,1408]{2,1,0:T(8,128)(2,1)S(1)}, bf16[3,32,1408]{2,1,0:T(8,128)(2,1)S(1)}, u32[]{:S(2)}, u32[]{:S(2)}) collective-permute-start(bf16[3,32,1408]{2,1,0:T(8,128)(2,1)S(1)} %constant_dynamic-update-slice_fusion), channel_id=1, source_target_pairs={{0,15},{1,0},{2,1},{3,2},{4,3},{5,4},{6,5},{7,6},{8,7},{9,8},{10,9... | collective-permute-start | bytes 811016 | tf_op jit(solution)/shard_map/ppermute | solution.py:15
  96.0 6.1 %collective-permute-start.6 = (bf16[3,32,1408]{2,1,0:T(8,128)(2,1)S(1)}, bf16[3,32,1408]{2,1,0:T(8,128)(2,1)S(1)}, u32[]{:S(2)}, u32[]{:S(2)}) collective-permute-start(bf16[3,32,1408]{2,1,0:T(8,128)(2,1)S(1)} %constant_dynamic-update-slice_fusion.2), channel_id=1, source_target_pairs={{0,15},{1,0},{2,1},{3,2},{4,3},{5,4},{6,5},{7,6},{8,7},{9,8},{10,9... | collective-permute-start | bytes 811016 | tf_op jit(solution)/shard_map/ppermute | solution.py:15
  102.1 2.0 collective-permute-done.10
  104.6 6.1 %collective-permute-start.11 = (bf16[3,32,1408]{2,1,0:T(8,128)(2,1)S(1)}, bf16[3,32,1408]{2,1,0:T(8,128)(2,1)S(1)}, u32[]{:S(2)}, u32[]{:S(2)}) collective-permute-start(bf16[3,32,1408]{2,1,0:T(8,128)(2,1)S(1)} %constant_dynamic-update-slice_fusion.4), channel_id=1, source_target_pairs={{0,15},{1,0},{2,1},{3,2},{4,3},{5,4},{6,5},{7,6},{8,7},{9,8},{10,9... | collective-permute-start | bytes 811016 | tf_op jit(solution)/shard_map/ppermute | solution.py:15
  111.6 4.1 %collective-permute-done.6 = bf16[3,32,1408]{2,1,0:T(8,128)(2,1)S(1)} collective-permute-done((bf16[3,32,1408]{2,1,0:T(8,128)(2,1)S(1)}, bf16[3,32,1408]{2,1,0:T(8,128)(2,1)S(1)}, u32[]{:S(2)}, u32[]{:S(2)}) %collective-permute-start.6) | collective-permute-done | bytes 270368 | tf_op jit(solution)/shard_map/ppermute | solution.py:15
  117.4 7.1 %collective-permute-done.11 = bf16[3,32,1408]{2,1,0:T(8,128)(2,1)S(1)} collective-permute-done((bf16[3,32,1408]{2,1,0:T(8,128)(2,1)S(1)}, bf16[3,32,1408]{2,1,0:T(8,128)(2,1)S(1)}, u32[]{:S(2)}, u32[]{:S(2)}) %collective-permute-start.11) | collective-permute-done | bytes 270368 | tf_op jit(solution)/shard_map/ppermute | solution.py:15
  124.6 6.2 %collective-permute-done.2 = bf16[3,32,1408]{2,1,0:T(8,128)(2,1)S(1)} collective-permute-done((bf16[3,32,1408]{2,1,0:T(8,128)(2,1)S(1)}, bf16[3,32,1408]{2,1,0:T(8,128)(2,1)S(1)}, u32[]{:S(2)}, u32[]{:S(2)}) %collective-permute-start.2) | collective-permute-done | bytes 270368 | tf_op jit(solution)/shard_map/ppermute | solution.py:15
  132.7 3.9 %collective-permute-done.7 = bf16[3,32,1408]{2,1,0:T(8,128)(2,1)S(1)} collective-permute-done((bf16[3,32,1408]{2,1,0:T(8,128)(2,1)S(1)}, bf16[3,32,1408]{2,1,0:T(8,128)(2,1)S(1)}, u32[]{:S(2)}, u32[]{:S(2)}) %collective-permute-start.7) | collective-permute-done | bytes 270368 | tf_op jit(solution)/shard_map/ppermute | solution.py:15
  138.5 3.9 %collective-permute-done.12 = bf16[3,32,1408]{2,1,0:T(8,128)(2,1)S(1)} collective-permute-done((bf16[3,32,1408]{2,1,0:T(8,128)(2,1)S(1)}, bf16[3,32,1408]{2,1,0:T(8,128)(2,1)S(1)}, u32[]{:S(2)}, u32[]{:S(2)}) %collective-permute-start.12) | collective-permute-done | bytes 270368 | tf_op jit(solution)/shard_map/ppermute | solution.py:15
  144.3 4.2 %collective-permute-done.3 = bf16[3,32,1408]{2,1,0:T(8,128)(2,1)S(1)} collective-permute-done((bf16[3,32,1408]{2,1,0:T(8,128)(2,1)S(1)}, bf16[3,32,1408]{2,1,0:T(8,128)(2,1)S(1)}, u32[]{:S(2)}, u32[]{:S(2)}) %collective-permute-start.3) | collective-permute-done | bytes 270368 | tf_op jit(solution)/shard_map/ppermute | solution.py:15
  148.7 2.5 collective-permute-start.4
  151.1 3.2 %collective-permute-done.8 = bf16[3,32,1408]{2,1,0:T(8,128)(2,1)S(1)} collective-permute-done((bf16[3,32,1408]{2,1,0:T(8,128)(2,1)S(1)}, bf16[3,32,1408]{2,1,0:T(8,128)(2,1)S(1)}, u32[]{:S(2)}, u32[]{:S(2)}) %collective-permute-start.8) | collective-permute-done | bytes 270368 | tf_op jit(solution)/shard_map/ppermute | solution.py:15
  154.5 2.5 collective-permute-start.9
  156.9 3.0 %collective-permute-done.13 = bf16[3,32,1408]{2,1,0:T(8,128)(2,1)S(1)} collective-permute-done((bf16[3,32,1408]{2,1,0:T(8,128)(2,1)S(1)}, bf16[3,32,1408]{2,1,0:T(8,128)(2,1)S(1)}, u32[]{:S(2)}, u32[]{:S(2)}) %collective-permute-start.13) | collective-permute-done | bytes 270368 | tf_op jit(solution)/shard_map/ppermute | solution.py:15
  160.0 2.7 %collective-permute-start.14 = (bf16[3,32,1408]{2,1,0:T(8,128)(2,1)S(1)}, bf16[3,32,1408]{2,1,0:T(8,128)(2,1)S(1)}, u32[]{:S(2)}, u32[]{:S(2)}) collective-permute-start(bf16[3,32,1408]{2,1,0:T(8,128)(2,1)S(1)} %broadcast_select_fusion.5), channel_id=1, source_target_pairs={{0,8},{1,9},{2,10},{3,11},{4,12},{5,13},{6,14},{7,15},{8,0},{9,1},... | collective-permute-start | bytes 811016 | tf_op jit(solution)/shard_map/ppermute | solution.py:15
  162.7 21.5 %collective-permute-done.4 = bf16[3,32,1408]{2,1,0:T(8,128)(2,1)S(1)} collective-permute-done((bf16[3,32,1408]{2,1,0:T(8,128)(2,1)S(1)}, bf16[3,32,1408]{2,1,0:T(8,128)(2,1)S(1)}, u32[]{:S(2)}, u32[]{:S(2)}) %collective-permute-start.4) | collective-permute-done | bytes 270368 | tf_op jit(solution)/shard_map/ppermute | solution.py:15
  184.4 7.9 %while.5 = (s32[]{:T(128)}, bf16[3,32,1408]{2,1,0:T(8,128)(2,1)S(1)}, s32[3,3]{1,0:T(4,128)S(1)}, bf16[3,16,1280]{2,1,0:T(8,128)(2,1)S(1)}, s32[]{:T(128)}) while((s32[]{:T(128)}, bf16[3,32,1408]{2,1,0:T(8,128)(2,1)S(1)}, s32[3,3]{1,0:T(4,128)S(1)}, bf16[3,16,1280]{2,1,0:T(8,128)(2,1)S(1)}, s32[]{:T(128)}) %tuple.129), condition=%wide.while_cond.1, body=%wide.while_body.1.sunk | while | flops 2 | bytes 82057 | solution.py:89
  185.0 2.0 dynamic-slice_dynamic-update-slice_fusion.9
  187.7 2.0 dynamic-slice_dynamic-update-slice_fusion.9
  190.3 2.0 dynamic-slice_dynamic-update-slice_fusion.9
  192.4 7.9 %while.6 = (s32[]{:T(128)}, bf16[3,32,1408]{2,1,0:T(8,128)(2,1)S(1)}, s32[3,3]{1,0:T(4,128)S(1)}, bf16[3,16,1280]{2,1,0:T(8,128)(2,1)S(1)}, s32[]{:T(128)}) while((s32[]{:T(128)}, bf16[3,32,1408]{2,1,0:T(8,128)(2,1)S(1)}, s32[3,3]{1,0:T(4,128)S(1)}, bf16[3,16,1280]{2,1,0:T(8,128)(2,1)S(1)}, s32[]{:T(128)}) %tuple.132), condition=%wide.while_cond.2, body=%wide.while_body.2.sunk | while | flops 2 | bytes 82057 | solution.py:89
  193.1 2.0 dynamic-slice_dynamic-update-slice_fusion.10
  195.7 2.0 dynamic-slice_dynamic-update-slice_fusion.10
  198.3 2.0 dynamic-slice_dynamic-update-slice_fusion.10
  200.5 8.3 %while.7 = (s32[]{:T(128)}, bf16[3,32,1408]{2,1,0:T(8,128)(2,1)S(1)}, s32[3,3]{1,0:T(4,128)S(1)}, bf16[3,16,1280]{2,1,0:T(8,128)(2,1)S(1)}, s32[]{:T(128)}) while((s32[]{:T(128)}, bf16[3,32,1408]{2,1,0:T(8,128)(2,1)S(1)}, s32[3,3]{1,0:T(4,128)S(1)}, bf16[3,16,1280]{2,1,0:T(8,128)(2,1)S(1)}, s32[]{:T(128)}) %tuple.135), condition=%wide.while_cond.3, body=%wide.while_body.3.sunk | while | flops 2 | bytes 82057 | solution.py:89
  201.1 2.0 dynamic-slice_dynamic-update-slice_fusion.11
  203.8 2.0 dynamic-slice_dynamic-update-slice_fusion.11
  206.4 2.0 dynamic-slice_dynamic-update-slice_fusion.11
  212.8 1.9 fusion.32
  217.3 1.9 fusion.30
  219.3 2.4 fusion.517
  226.3 1.9 fusion.25
  228.3 1.9 fusion.27
  230.9 1.9 fusion.23
  232.9 2.4 fusion.518
  240.7 1.9 fusion.18
  242.7 1.9 fusion.20
  245.3 1.9 fusion.16
  247.2 2.7 fusion.519
  (196 shorter events, 58.6 us)
Async XLA Ops:
  6.5 2.9 %copy-start = (f32[6,16,16]{2,1,0:T(8,128)S(1)}, f32[6,16,16]{2,1,0:T(8,128)}, u32[]{:S(2)}) copy-start(f32[6,16,16]{2,1,0:T(8,128)} %param.15) | copy-start | bytes 18436
  6.5 0.8 copy-start.3
  6.5 0.8 copy-start.4
  6.5 0.8 copy-start.5
  6.5 45.5 %all-gather.2.cloned.1.call-start = ((), (), s32[]{:S(2)}) async-start(), calls=%async_computation | async-start | bytes 37748736 | tf_op jit(solution)/shard_map/all_gather | solution.py:122
  71.5 15.4 %collective-permute-start = (bf16[3,3,16,1408]{3,2,1,0:T(8,128)(2,1)S(1)}, bf16[3,3,16,1408]{3,2,1,0:T(8,128)(2,1)}, u32[]{:S(2)}, u32[]{:S(2)}) collective-permute-start(bf16[3,3,16,1408]{3,2,1,0:T(8,128)(2,1)S(1)} %broadcast_select_fusion.2), channel_id=1, source_target_pairs={{0,15},{1,0},{2,1},{3,2},{4,3},{5,4},{6,5},{7,6},{8,7},{9,8},{10,9... | collective-permute-start | bytes 1216520 | tf_op jit(solution)/shard_map/ppermute | solution.py:15
  80.5 14.8 %collective-permute-start.5 = (bf16[3,3,16,1408]{3,2,1,0:T(8,128)(2,1)S(1)}, bf16[3,3,16,1408]{3,2,1,0:T(8,128)(2,1)S(1)}, u32[]{:S(2)}, u32[]{:S(2)}) collective-permute-start(bf16[3,3,16,1408]{3,2,1,0:T(8,128)(2,1)S(1)} %broadcast_select_fusion.1), channel_id=1, source_target_pairs={{0,15},{1,0},{2,1},{3,2},{4,3},{5,4},{6,5},{7,6},{8,7},{9,8},{10,9... | collective-permute-start | bytes 1216520 | tf_op jit(solution)/shard_map/ppermute | solution.py:15
  84.7 19.3 %collective-permute-start.10 = (bf16[3,3,16,1408]{3,2,1,0:T(8,128)(2,1)S(1)}, bf16[3,3,16,1408]{3,2,1,0:T(8,128)(2,1)S(1)}, u32[]{:S(2)}, u32[]{:S(2)}) collective-permute-start(bf16[3,3,16,1408]{3,2,1,0:T(8,128)(2,1)S(1)} %broadcast_select_fusion), channel_id=1, source_target_pairs={{0,15},{1,0},{2,1},{3,2},{4,3},{5,4},{6,5},{7,6},{8,7},{9,8},{10,9... | collective-permute-start | bytes 1216520 | tf_op jit(solution)/shard_map/ppermute | solution.py:15
  88.5 22.3 %collective-permute-start.1 = (bf16[3,32,1408]{2,1,0:T(8,128)(2,1)S(1)}, bf16[3,32,1408]{2,1,0:T(8,128)(2,1)S(1)}, u32[]{:S(2)}, u32[]{:S(2)}) collective-permute-start(bf16[3,32,1408]{2,1,0:T(8,128)(2,1)S(1)} %constant_dynamic-update-slice_fusion), channel_id=1, source_target_pairs={{0,15},{1,0},{2,1},{3,2},{4,3},{5,4},{6,5},{7,6},{8,7},{9,8},{10,9... | collective-permute-start | bytes 811016 | tf_op jit(solution)/shard_map/ppermute | solution.py:15
  96.0 19.7 %collective-permute-start.6 = (bf16[3,32,1408]{2,1,0:T(8,128)(2,1)S(1)}, bf16[3,32,1408]{2,1,0:T(8,128)(2,1)S(1)}, u32[]{:S(2)}, u32[]{:S(2)}) collective-permute-start(bf16[3,32,1408]{2,1,0:T(8,128)(2,1)S(1)} %constant_dynamic-update-slice_fusion.2), channel_id=1, source_target_pairs={{0,15},{1,0},{2,1},{3,2},{4,3},{5,4},{6,5},{7,6},{8,7},{9,8},{10,9... | collective-permute-start | bytes 811016 | tf_op jit(solution)/shard_map/ppermute | solution.py:15
  104.6 19.8 %collective-permute-start.11 = (bf16[3,32,1408]{2,1,0:T(8,128)(2,1)S(1)}, bf16[3,32,1408]{2,1,0:T(8,128)(2,1)S(1)}, u32[]{:S(2)}, u32[]{:S(2)}) collective-permute-start(bf16[3,32,1408]{2,1,0:T(8,128)(2,1)S(1)} %constant_dynamic-update-slice_fusion.4), channel_id=1, source_target_pairs={{0,15},{1,0},{2,1},{3,2},{4,3},{5,4},{6,5},{7,6},{8,7},{9,8},{10,9... | collective-permute-start | bytes 811016 | tf_op jit(solution)/shard_map/ppermute | solution.py:15
  110.9 19.9 %collective-permute-start.2 = (bf16[3,32,1408]{2,1,0:T(8,128)(2,1)S(1)}, bf16[3,32,1408]{2,1,0:T(8,128)(2,1)S(1)}, u32[]{:S(2)}, u32[]{:S(2)}) collective-permute-start(bf16[3,32,1408]{2,1,0:T(8,128)(2,1)S(1)} %broadcast_select_fusion.11), channel_id=1, source_target_pairs={{0,14},{1,15},{2,0},{3,1},{4,2},{5,3},{6,4},{7,5},{8,6},{9,7},{10,... | collective-permute-start | bytes 811016 | tf_op jit(solution)/shard_map/ppermute | solution.py:15
  115.7 20.9 %collective-permute-start.7 = (bf16[3,32,1408]{2,1,0:T(8,128)(2,1)S(1)}, bf16[3,32,1408]{2,1,0:T(8,128)(2,1)S(1)}, u32[]{:S(2)}, u32[]{:S(2)}) collective-permute-start(bf16[3,32,1408]{2,1,0:T(8,128)(2,1)S(1)} %broadcast_select_fusion.7), channel_id=1, source_target_pairs={{0,14},{1,15},{2,0},{3,1},{4,2},{5,3},{6,4},{7,5},{8,6},{9,7},{10,... | collective-permute-start | bytes 811016 | tf_op jit(solution)/shard_map/ppermute | solution.py:15
  124.6 17.9 %collective-permute-start.12 = (bf16[3,32,1408]{2,1,0:T(8,128)(2,1)S(1)}, bf16[3,32,1408]{2,1,0:T(8,128)(2,1)S(1)}, u32[]{:S(2)}, u32[]{:S(2)}) collective-permute-start(bf16[3,32,1408]{2,1,0:T(8,128)(2,1)S(1)} %broadcast_select_fusion.3), channel_id=1, source_target_pairs={{0,14},{1,15},{2,0},{3,1},{4,2},{5,3},{6,4},{7,5},{8,6},{9,7},{10,... | collective-permute-start | bytes 811016 | tf_op jit(solution)/shard_map/ppermute | solution.py:15
  130.9 17.6 %collective-permute-start.3 = (bf16[3,32,1408]{2,1,0:T(8,128)(2,1)S(1)}, bf16[3,32,1408]{2,1,0:T(8,128)(2,1)S(1)}, u32[]{:S(2)}, u32[]{:S(2)}) collective-permute-start(bf16[3,32,1408]{2,1,0:T(8,128)(2,1)S(1)} %broadcast_select_fusion.12), channel_id=1, source_target_pairs={{0,12},{1,13},{2,14},{3,15},{4,0},{5,1},{6,2},{7,3},{8,4},{9,5},{1... | collective-permute-start | bytes 811016 | tf_op jit(solution)/shard_map/ppermute | solution.py:15
  136.7 17.6 %collective-permute-start.8 = (bf16[3,32,1408]{2,1,0:T(8,128)(2,1)S(1)}, bf16[3,32,1408]{2,1,0:T(8,128)(2,1)S(1)}, u32[]{:S(2)}, u32[]{:S(2)}) collective-permute-start(bf16[3,32,1408]{2,1,0:T(8,128)(2,1)S(1)} %broadcast_select_fusion.8), channel_id=1, source_target_pairs={{0,12},{1,13},{2,14},{3,15},{4,0},{5,1},{6,2},{7,3},{8,4},{9,5},{1... | collective-permute-start | bytes 811016 | tf_op jit(solution)/shard_map/ppermute | solution.py:15
  142.5 17.4 %collective-permute-start.13 = (bf16[3,32,1408]{2,1,0:T(8,128)(2,1)S(1)}, bf16[3,32,1408]{2,1,0:T(8,128)(2,1)S(1)}, u32[]{:S(2)}, u32[]{:S(2)}) collective-permute-start(bf16[3,32,1408]{2,1,0:T(8,128)(2,1)S(1)} %broadcast_select_fusion.4), channel_id=1, source_target_pairs={{0,12},{1,13},{2,14},{3,15},{4,0},{5,1},{6,2},{7,3},{8,4},{9,5},{1... | collective-permute-start | bytes 811016 | tf_op jit(solution)/shard_map/ppermute | solution.py:15
  148.7 35.6 %collective-permute-start.4 = (bf16[3,32,1408]{2,1,0:T(8,128)(2,1)S(1)}, bf16[3,32,1408]{2,1,0:T(8,128)(2,1)S(1)}, u32[]{:S(2)}, u32[]{:S(2)}) collective-permute-start(bf16[3,32,1408]{2,1,0:T(8,128)(2,1)S(1)} %broadcast_select_fusion.13), channel_id=1, source_target_pairs={{0,8},{1,9},{2,10},{3,11},{4,12},{5,13},{6,14},{7,15},{8,0},{9,1},... | collective-permute-start | bytes 811016 | tf_op jit(solution)/shard_map/ppermute | solution.py:15
  154.5 37.8 %collective-permute-start.9 = (bf16[3,32,1408]{2,1,0:T(8,128)(2,1)S(1)}, bf16[3,32,1408]{2,1,0:T(8,128)(2,1)S(1)}, u32[]{:S(2)}, u32[]{:S(2)}) collective-permute-start(bf16[3,32,1408]{2,1,0:T(8,128)(2,1)S(1)} %broadcast_select_fusion.9), channel_id=1, source_target_pairs={{0,8},{1,9},{2,10},{3,11},{4,12},{5,13},{6,14},{7,15},{8,0},{9,1},... | collective-permute-start | bytes 811016 | tf_op jit(solution)/shard_map/ppermute | solution.py:15
  160.0 40.4 %collective-permute-start.14 = (bf16[3,32,1408]{2,1,0:T(8,128)(2,1)S(1)}, bf16[3,32,1408]{2,1,0:T(8,128)(2,1)S(1)}, u32[]{:S(2)}, u32[]{:S(2)}) collective-permute-start(bf16[3,32,1408]{2,1,0:T(8,128)(2,1)S(1)} %broadcast_select_fusion.5), channel_id=1, source_target_pairs={{0,8},{1,9},{2,10},{3,11},{4,12},{5,13},{6,14},{7,15},{8,0},{9,1},... | collective-permute-start | bytes 811016 | tf_op jit(solution)/shard_map/ppermute | solution.py:15
  184.4 24.5 %copy-start.2 = (f32[16,1280]{1,0:T(8,128)S(1)}, f32[16,1280]{1,0:T(8,128)}, u32[]{:S(2)}) copy-start(f32[16,1280]{1,0:T(8,128)} %param.13) | copy-start | bytes 245764
  257.9 5.1 %copy-start.1 = (f32[6,16,16]{2,1,0:T(8,128)S(1)}, f32[6,16,16]{2,1,0:T(8,128)}, u32[]{:S(2)}) copy-start(f32[6,16,16]{2,1,0:T(8,128)} %param.15) | copy-start | bytes 18436
Sparse Core Ops, SparseCore 0:
  8.9 43.0 all-gather.1
where the time goes:
time: 275 us; the launch traced here: 270 us
  waiting for transfers between devices  102 us (37%)
  local copies, waits for them, and re-layouts  57 us (21%)
  matrix products  47.9 us (17%)
  starting transfers between devices  41.3 us (15%)
  between operations  15.5 us (6%)
  other arithmetic  6.5 us (2%)
    ppermute x15, waiting for transfers between devices, from_behind(): lax.ppermute(array, axis, [(i, (i + by) % size) for i in range(size)])  59.9 us
    dot_general x66, matrix products, contract(): jnp.einsum(form, left, right, precision=lax.Precision.HIGHEST, preferred_...  47.9 us
    ppermute x15, starting transfers between devices, from_behind(): lax.ppermute(array, axis, [(i, (i + by) % size) for i in range(size)])  41.2 us
    all_gather x1, waiting for transfers between devices, shards(): panels = lax.all_gather(screens, 'star', axis=3, tiled=True)  41 us
    gather x36, local copies, waits for them, and re-layouts  40.1 us
    gather x6, local copies, waits for them, and re-layouts, candidates_one_layer(): return jnp.take(block, wanted, axis=0)  8.87 us
  transfers between devices with their start and end apart: 16, of which 12 were waited for; matrix products, arithmetic and copies ran while one was open for 11% of the time, Pallas kernels for 0%

commit v1 on v0

v1 whole, which is shorter than its diff:
```python
import functools
import math

import jax
import jax.numpy as jnp
import numpy as np
from jax import lax
from jax.experimental import pallas as pl
from jax.experimental.pallas import tpu as pltpu
from jax.sharding import PartitionSpec as P

BIN = 4
SIDE = 16
LANES = 128
SPAN = 12
QUART = 4
THIRD = SPAN // QUART

F32 = jnp.float32
BF16 = jnp.bfloat16


def split_np(table):
    high = table.astype(jnp.bfloat16)
    low = (table - high.astype(np.float64)).astype(jnp.bfloat16)
    return high, low


def split(value):
    high = value.astype(BF16)
    return high, (value - high.astype(F32)).astype(BF16)


def across_tables():
    length = BIN * SIDE
    freq = (np.arange(length) + length // 2) % length
    angle = 2.0 * math.pi * (np.outer(np.arange(SIDE), freq) % length) / length
    real, imag = np.cos(angle), -np.sin(angle)
    out = np.zeros((2, 8, SIDE, 2, BIN, SIDE, 8))
    for i in range(8):
        for b in range(BIN):
            re, im = real[:, b::BIN], imag[:, b::BIN]
            out[0, i, :, 0, b, :, i] = re
            out[1, i, :, 0, b, :, i] = -im
            out[0, i, :, 1, b, :, i] = im
            out[1, i, :, 1, b, :, i] = re
    return split_np(out.reshape(2 * 8 * SIDE, 2 * BIN * SIDE * 8))


def down_table():
    length = BIN * SIDE
    freq = (np.arange(length) + length // 2) % length
    angle = 2.0 * math.pi * (np.outer(freq, np.arange(SIDE)) % length) / length
    real, imag = np.cos(angle), -np.sin(angle)
    order = np.concatenate([np.arange(a, length, BIN) for a in range(BIN)])
    real, imag = real[order], imag[order]
    table = np.block([[real, -imag], [imag, real]])
    high, low = split_np(table)
    return np.concatenate([high, high, low], axis=1)


def place_of(rows_ref, cols_ref, layer, star, devices, total_tiles):
    offset = rows_ref[layer, star]
    strip = lax.div(offset, SIDE)
    part = lax.rem(offset, SIDE)
    tile = jnp.minimum(lax.div(cols_ref[layer, star], LANES), total_tiles - SPAN)
    return strip, part, tile


def first_tile(tile, panel, tiles, held):
    return jnp.clip(tile - panel * tiles, 0, tiles - held)


def crop_kernel(stars, devices, rows_ref, cols_ref, screens_ref, *rest):
    outs, sem = rest[:stars], rest[stars]
    layers, bands, side, width = screens_ref.shape
    tiles = width // LANES
    held = min(SPAN, tiles)
    me = lax.axis_index("star")
    place = lax.axis_index("dev")
    copies = []
    for turn in range(stars):
        star = lax.rem(me + turn, stars)
        for layer in range(layers):
            strip, _, tile = place_of(rows_ref, cols_ref, layer, star, devices, stars * tiles)
            behind = lax.rem(place + bands * devices - strip, devices)
            band = lax.div(strip + behind, devices)
            start = first_tile(tile, me, tiles, held)
            columns = pl.ds(pl.multiple_of(start * LANES, LANES), held * LANES)
            for slot in range(2):
                copy = pltpu.make_async_copy(
                    screens_ref.at[layer, lax.rem(band + slot, bands), :, columns],
                    outs[turn].at[2 * layer + slot],
                    sem.at[turn, 2 * layer + slot],
                )
                copy.start()
                copies.append(copy)
    for copy in copies:
        copy.wait()


def spread_kernel(stars, devices, tiles, rows_ref, cols_ref, *rest):
    parts, out_ref, turned = rest[:stars], rest[stars], rest[stars + 1]
    layers = parts[0].shape[0] // 2
    held = parts[0].shape[2] // LANES
    groups = devices // SIDE
    sub = QUART // groups
    me = lax.axis_index("star")
    place = lax.axis_index("dev")
    row = lax.broadcasted_iota(jnp.int32, (SIDE, LANES), 0)
    for layer in range(layers):
        strip, part, tile = place_of(rows_ref, cols_ref, layer, me, devices, stars * tiles)
        behind = lax.rem(place + (1 << 20) * devices - strip, devices)
        bound = jnp.where(behind == 0, part, 0)
        wraps = row < bound
        for a in range(QUART):
            for b in range(THIRD):
                spot = tile + (THIRD * a + b)
                panel = lax.div(spot, tiles)
                pair = []
                for slot in range(2):
                    value = None
                    for turn in range(stars):
                        sender = lax.rem(me + stars - turn, stars)
                        start = first_tile(tile, sender, tiles, held)
                        local = jnp.clip(spot - sender * tiles - start, 0, held - 1)
                        lanes = pl.ds(pl.multiple_of(local * LANES, LANES), LANES)
                        seen = parts[turn][2 * layer + slot, :, lanes].astype(F32)
                        if value is None:
                            value = seen
                        else:
                            value = jnp.where(panel == sender, seen, value)
                    pair.append(value)
                first = jnp.where(wraps, pair[1], pair[0])
                at = (a // sub) * 2 * sub + a % sub
                turned[layer * THIRD + b, pl.ds(at * SIDE, SIDE), :] = first
                turned[layer * THIRD + b, pl.ds((at + sub) * SIDE, SIDE), :] = pair[1]
    for group in range(groups):
        for r in range(SIDE):
            pieces = [
                turned[unit, pl.ds(group * 2 * sub * SIDE + r, 2 * sub, stride=SIDE), :]
                for unit in range(layers * THIRD)
            ]
            out_ref[group * SIDE + r] = jnp.concatenate(pieces, axis=1).astype(BF16)


def choose_kernel(devices, rows_ref, in_ref, out_ref):
    layers = rows_ref.shape[0]
    width = in_ref.shape[2] // layers
    half = in_ref.shape[1] // 2
    me = lax.axis_index("star")
    mine = lax.rem(lax.axis_index("dev"), SIDE)
    upper = lax.broadcasted_iota(jnp.int32, (2 * half, width), 0) < half
    for layer in range(layers):
        offset = rows_ref[layer, me]
        base = lax.div(offset, SIDE) + (mine < lax.rem(offset, SIDE)).astype(jnp.int32)
        lanes = slice(layer * width, (layer + 1) * width)
        now = in_ref[lax.rem(base, devices), :, lanes].astype(F32)
        last = now
        for j in range(devices):
            if j < devices - 1:
                after = in_ref[lax.rem(base + j + 1, devices), :, lanes].astype(F32)
                low = pltpu.roll(after, half, axis=0)
            else:
                after, low = None, last
            out_ref[j, :, lanes] = jnp.where(upper, now, low).astype(BF16)
            now = after


def sin_cos(value):
    turns = jnp.floor(value * (2.0 / math.pi) + 0.5)
    rest = value - turns * 1.5703125
    rest = rest - turns * 4.837512969970703125e-4
    rest = rest - turns * 7.549789948768648e-8
    square = rest * rest
    sine = rest + rest * square * (
        -1.6666654611e-1 + square * (8.3321608736e-3 - square * 1.9515295891e-4)
    )
    cosine = (
        1.0
        - 0.5 * square
        + square
        * square
        * (4.166664568298827e-2 + square * (-1.388731625493765e-3 + square * 2.443315711809948e-5))
    )
    quarter = turns.astype(jnp.int32)
    odd = (quarter & 1) == 1
    flip_sine = (quarter & 2) == 2
    flip_cosine = ((quarter + 1) & 2) == 2
    s = jnp.where(odd, cosine, sine)
    c = jnp.where(odd, sine, cosine)
    return jnp.where(flip_sine, -s, s), jnp.where(flip_cosine, -c, c)


def matmul(left, right):
    return lax.dot_general(
        left, right, (((1,), (0,)), ((), ())), preferred_element_type=F32
    )


def spots_kernel(
    stars,
    devices,
    total_tiles,
    rows_ref,
    cols_ref,
    wind_ref,
    owner_ref,
    in_ref,
    amp_ref,
    refs_ref,
    high_ref,
    low_ref,
    down_ref,
    out_ref,
    turned,
    window,
    field,
    first,
    binned,
    table,
):
    steps, layers = wind_ref.shape[0], wind_ref.shape[1]
    across = amp_ref.shape[1] // LANES
    groups = devices // SIDE
    sub = QUART // groups
    me = lax.axis_index("star")
    row = lax.broadcasted_iota(jnp.int32, (SIDE, LANES), 0)
    lane = lax.broadcasted_iota(jnp.int32, (SIDE, LANES), 1)

    refer = refs_ref[owner_ref[0, 0]]
    wide = SIDE * SIDE
    pick_row = lax.broadcasted_iota(jnp.int32, (SIDE, wide), 0)
    pick_lane = lax.broadcasted_iota(jnp.int32, (SIDE, wide), 1)
    pick = (pick_row == ((SIDE - (pick_lane & 15)) & 15)).astype(F32)
    base = lax.dot_general(
        refer,
        pick,
        (((1,), (0,)), ((), ())),
        precision=lax.Precision.HIGHEST,
        preferred_element_type=F32,
    )
    for bit in range(4):
        moved = pltpu.roll(base, 1 << bit, axis=0)
        base = jnp.where(((pick_lane >> (4 + bit)) & 1) == 1, moved, base)
    for q in range(SIDE):
        if q == 0:
            block = base
        else:
            block = jnp.where(
                (pick_lane & 15) >= q,
                pltpu.roll(base, q, axis=1),
                pltpu.roll(base, wide + q - SIDE, axis=1),
            )
        high, low = split(block)
        table[pl.ds(q * SIDE, SIDE), :] = high
        table[pl.ds(wide + q * SIDE, SIDE), :] = high
        table[pl.ds(2 * wide + q * SIDE, SIDE), :] = low

    for x in range(devices):
        seen = in_ref[x].astype(F32)
        for unit in range(layers * THIRD):
            turned[unit, pl.ds(x * 2 * sub, 2 * sub), :] = seen[:, unit * LANES : (unit + 1) * LANES]
    for layer in range(layers):
        part = lax.rem(rows_ref[layer, me], SIDE)
        early = row < part
        for a in range(QUART):
            for b in range(THIRD):
                at = (a // sub) * SIDE * 2 * sub + a % sub
                unit = layer * THIRD + b
                one = turned[unit, pl.ds(at, SIDE, stride=2 * sub), :]
                two = turned[unit, pl.ds(at + sub, SIDE, stride=2 * sub), :]
                slot = layer * SPAN + THIRD * a + b
                window[slot, pl.ds(0, SIDE), :] = one
                window[slot, pl.ds(SIDE, SIDE), :] = jnp.where(early, one, two)
                window[slot, pl.ds(2 * SIDE, SIDE), :] = two

    binned[pl.ds(steps * across * SIDE, binned.shape[0] - steps * across * SIDE), :] = jnp.ones(
        (binned.shape[0] - steps * across * SIDE, LANES), F32
    )

    def one_step(step, carry):
        phase = [None] * across
        for layer in range(layers):
            left = cols_ref[layer, me]
            tile = jnp.minimum(lax.div(left, LANES), total_tiles - SPAN)
            shift = left - tile * LANES + wind_ref[step, layer, 1]
            skip = lax.div(shift, LANES)
            fine = lax.rem(shift, LANES)
            start = lax.rem(rows_ref[layer, me], SIDE) + wind_ref[step, layer, 0]
            inside = lane < LANES - fine
            rolled = [
                pltpu.roll(
                    window[layer * SPAN + skip + t, pl.ds(start, SIDE), :],
                    lax.rem(LANES - fine, LANES),
                    axis=1,
                )
                for t in range(across + 1)
            ]
            for t in range(across):
                value = jnp.where(inside, rolled[t], rolled[t + 1])
                phase[t] = value if phase[t] is None else phase[t] + value
        for t in range(across):
            sine, cosine = sin_cos(phase[t])
            amp = amp_ref[:, t * LANES : (t + 1) * LANES]
            for part, value in enumerate((amp * cosine, amp * sine)):
                high, low = split(value)
                lanes = slice(part * LANES, (part + 1) * LANES)
                field[0, pl.ds(t * SIDE, SIDE), lanes] = high
                field[1, pl.ds(t * SIDE, SIDE), lanes] = low
        first[...] = (
            matmul(field[0], high_ref[...])
            + matmul(field[1], high_ref[...])
            + matmul(field[0], low_ref[...])
        )
        wide_out = first.shape[1] // 2
        for t in range(across):
            rows = pl.ds(t * SIDE, SIDE)
            real_high, real_low = split(first[rows, 0:wide_out])
            imag_high, imag_low = split(first[rows, wide_out : 2 * wide_out])
            stacked = jnp.concatenate(
                [real_high, imag_high, real_low, imag_low, real_high, imag_high], axis=0
            )
            spectrum = matmul(down_ref[...], stacked)
            power = spectrum * spectrum
            total = power[0:SIDE]
            for k in range(1, 2 * BIN):
                total = total + power[k * SIDE : (k + 1) * SIDE]
            small = total[:, 0:LANES]
            for k in range(1, BIN):
                small = small + total[:, k * LANES : (k + 1) * LANES]
            binned[pl.ds((step * across + t) * SIDE, SIDE), :] = small
        return carry

    lax.fori_loop(0, steps, one_step, 0)

    lane8 = lax.broadcasted_iota(jnp.int32, (8, LANES), 1)
    for big in range(binned.shape[0] // LANES):
        flipped = binned[pl.ds(big * LANES, LANES), :].T
        halves = []
        for half in range(2):
            regs = [flipped[(half * 8 + q) * 8 : (half * 8 + q + 1) * 8] for q in range(8)]
            for jump in (4, 2, 1):
                keep = ((lane8 >> 4) & jump) == 0
                for i in range(8):
                    if i & jump == 0:
                        one, two = regs[i], regs[i + jump]
                        regs[i] = jnp.where(keep, one, pltpu.roll(two, jump * SIDE, axis=1))
                        regs[i + jump] = jnp.where(
                            keep, pltpu.roll(one, LANES - jump * SIDE, axis=1), two
                        )
            halves.append(regs)
        image = jnp.concatenate(
            [jnp.concatenate([halves[0][g], halves[1][g]], axis=1) for g in range(8)], axis=0
        )
        image = image / jnp.sum(image, axis=1, keepdims=True)
        high, low = split(image)
        found = matmul(jnp.concatenate([high, low, high], axis=1), table[...])
        count = min(64, steps * across * 8 - big * 64)
        out_ref[pl.ds(big * 64, count), :] = found[0:count]


def shards(screens, foot_rows, foot_cols, wind, amplitude, owner, refs):
    stars, devices = lax.axis_size("star"), lax.axis_size("dev")
    layers, _, side, width = screens.shape
    steps = wind.shape[0]
    tiles = width // LANES
    held = min(SPAN, tiles)
    subs = amplitude.shape[1] // side
    smem = pl.BlockSpec(memory_space=pltpu.SMEM)
    vmem = pl.BlockSpec(memory_space=pltpu.VMEM)
    hbm = pl.BlockSpec(memory_space=pl.ANY)
    crops = pl.pallas_call(
        functools.partial(crop_kernel, stars, devices),
        out_shape=[jax.ShapeDtypeStruct((2 * layers, side, held * LANES), BF16)] * stars,
        in_specs=[smem, smem, hbm],
        out_specs=[vmem] * stars,
        scratch_shapes=[pltpu.SemaphoreType.DMA((stars, 2 * layers))],
        name="crop",
    )(foot_rows, foot_cols, screens)
    parts = [crops[0]]
    for turn in range(1, stars):
        parts.append(
            lax.ppermute(crops[turn], "star", [(i, (i + turn) % stars) for i in range(stars)])
        )
    groups = devices // SIDE
    depth = 2 * QUART // groups
    block = jax.ShapeDtypeStruct((devices, depth, layers * THIRD * LANES), BF16)
    sent = pl.pallas_call(
        functools.partial(spread_kernel, stars, devices, tiles),
        out_shape=block,
        in_specs=[smem, smem] + [vmem] * stars,
        out_specs=vmem,
        scratch_shapes=[pltpu.VMEM((layers * THIRD, 2 * QUART * SIDE, LANES), F32)],
        name="spread",
    )(foot_rows, foot_cols, *parts)
    held_rows = lax.all_to_all(sent, "dev", 0, 0, tiled=True)
    chosen = pl.pallas_call(
        functools.partial(choose_kernel, devices),
        out_shape=block,
        in_specs=[smem, vmem],
        out_specs=vmem,
        name="choose",
    )(foot_rows, held_rows)
    strips = lax.all_to_all(chosen, "dev", 0, 0, tiled=True)
    high, low = across_tables()
    count = steps * subs
    padded = -(-count // 64) * 64
    found = pl.pallas_call(
        functools.partial(spots_kernel, stars, devices, stars * tiles),
        out_shape=jax.ShapeDtypeStruct((count, SIDE * SIDE), F32),
        in_specs=[smem] * 4 + [vmem] * 6,
        out_specs=vmem,
        scratch_shapes=[
            pltpu.VMEM((layers * THIRD, devices * depth, LANES), F32),
            pltpu.VMEM((layers * SPAN, 3 * SIDE, LANES), F32),
            pltpu.VMEM((2, subs // 8 * SIDE, 2 * LANES), BF16),
            pltpu.VMEM((subs // 8 * SIDE, high.shape[1]), F32),
            pltpu.VMEM((padded // 8 * SIDE, LANES), F32),
            pltpu.VMEM((3 * SIDE * SIDE, SIDE * SIDE), BF16),
        ],
        compiler_params=pltpu.CompilerParams(vmem_limit_bytes=48 << 20),
        name="spots",
    )(foot_rows, foot_cols, wind, owner, strips, amplitude, refs, high, low, down_table())
    return found.reshape(steps, 1, 1, subs, SIDE * SIDE)


def solution(mesh):
    in_specs = (P(None, None, "dev", "star"), P(), P(), P(), P("dev", None), P("star", "dev"), P())
    out_specs = P(None, "star", "dev", None, None)
    return jax.shard_map(shards, mesh=mesh, in_specs=in_specs, out_specs=out_specs, check_vma=False)
```

time: 275 us -> 52 us (0.19); the launches traced: 270 us -> 51.5 us
  waiting for transfers between devices: 102 us -> 10.8 us
  local copies, waits for them, and re-layouts: 57 us -> 3.61 us
  matrix products: 47.9 us -> 0 us
  starting transfers between devices: 41.3 us -> 4.07 us
  blocking collectives: 0 us -> 19.3 us
  between operations: 15.5 us -> 0.73 us
  Pallas kernels: 0 us -> 13 us
  other arithmetic: 6.5 us -> 0 us
    ppermute x15 -> x1, waiting for transfers between devices: 59.9 us -> 1.42 us  [shards(): lax.ppermute(crops[turn], 'star', [(i, (i + turn) % stars) for i in range...]
    gather x48 -> x0, local copies, waits for them, and re-layouts: 53.4 us -> none
    dot_general x66 -> x0, matrix products: 47.9 us -> none  [contract(): jnp.einsum(form, left, right, precision=lax.Precision.HIGHEST, preferred_...]
    all_gather x1 -> x0, waiting for transfers between devices: 41 us -> none  [shards(): panels = lax.all_gather(screens, 'star', axis=3, tiled=True)]
    ppermute x15 -> x1, starting transfers between devices: 41.2 us -> 0.53 us  [shards(): lax.ppermute(crops[turn], 'star', [(i, (i + turn) % stars) for i in range...]
    all_to_all x0 -> x1, blocking collectives: none -> 19.3 us  [shards(): held_rows = lax.all_to_all(sent, 'dev', 0, 0, tiled=True)]
    pallas_call x0 -> x4, Pallas kernels: none -> 13 us  [the longest x1 6.11 us: shards(): pl.pallas_call(functools.partial(spots_kernel, stars, devices, stars * ti...]
    all_to_all x0 -> x1, waiting for transfers between devices: none -> 9.37 us  [shards(): strips = lax.all_to_all(chosen, 'dev', 0, 0, tiled=True)]
  transfers between devices with their start and end apart: 16 -> 2, of which waited for: 12 -> 2; matrix products, arithmetic and copies ran while one was open for 11% -> 0% of each run, Pallas kernels for 0% -> 0%
where the time goes in v1:
time: 52 us; the launch traced here: 51.5 us
  blocking collectives  19.3 us (37%)
  Pallas kernels  13 us (25%)
  waiting for transfers between devices  10.8 us (21%)
  starting transfers between devices  4.07 us (8%)
  local copies, waits for them, and re-layouts  3.61 us (7%)
  between operations  0.73 us (1%)
    all_to_all x1, blocking collectives, shards(): held_rows = lax.all_to_all(sent, 'dev', 0, 0, tiled=True)  19.3 us
    all_to_all x1, waiting for transfers between devices, shards(): strips = lax.all_to_all(chosen, 'dev', 0, 0, tiled=True)  9.37 us
    pallas_call x1, Pallas kernels, shards(): pl.pallas_call(functools.partial(spots_kernel, stars, devices, stars * ti...  6.11 us
    unnamed x21, local copies, waits for them, and re-layouts  3.61 us
    all_to_all x1, starting transfers between devices, shards(): strips = lax.all_to_all(chosen, 'dev', 0, 0, tiled=True)  3.54 us
    pallas_call x1, Pallas kernels, shards(): pl.pallas_call(functools.partial(crop_kernel, stars, devices), out_shape=...  2.8 us
    pallas_call x1, Pallas kernels, shards(): pl.pallas_call(functools.partial(spread_kernel, stars, devices, tiles), o...  2.26 us
    pallas_call x1, Pallas kernels, shards(): pl.pallas_call(functools.partial(choose_kernel, devices), out_shape=block...  1.82 us
  transfers between devices with their start and end apart: 2, of which 2 were waited for; matrix products, arithmetic and copies ran while one was open for 0% of the time, Pallas kernels for 0%

profile of v1, /device:TPU:0, one launch (start us, length us, event | category | flops | bytes accessed | tf_op | source)
XLA Modules:
  0.0 51.5 jit_solution(330234316527507031)
XLA Ops:
  0.0 0.0 copy-start
  0.0 0.0 copy-start.1
  0.0 0.0 copy-start.6
  0.0 0.0 copy-start.8
  0.0 0.0 copy-start.2
  0.0 0.0 copy-start.4
  0.0 1.4 %copy.16.rows_ref = s32[3,2]{1,0:T(4,128)} copy(s32[3,2]{0,1:T(2,128)} %param.11) | data formatting | bytes 48 | tf_op args[1]
  1.5 0.0 copy-start.3
  1.5 1.3 %copy.17.cols_ref = s32[3,2]{1,0:T(4,128)} copy(s32[3,2]{0,1:T(2,128)} %param.12) | data formatting | bytes 48 | tf_op args[2]
  2.8 0.0 copy-start.5
  2.8 2.8 %crop.1 = (bf16[6,16,1536]{2,1,0:T(8,128)(2,1)}, bf16[6,16,1536]{2,1,0:T(8,128)(2,1)}) custom-call(s32[3,2]{1,0:T(4,128)} %copy.16.rows_ref, s32[3,2]{1,0:T(4,128)} %copy.17.cols_ref, bf16[3,32,16,4096]{3,2,1,0:T(8,128)(2,1)} %screens_ref.1), custom_call_target="tpu_custom_call" | custom-call | tf_op jit(solution)/shard_map/crop/pallas_call | solution.py:373
  5.6 0.5 %collective-permute-start = (bf16[6,16,1536]{2,1,0:T(8,128)(2,1)}, bf16[6,16,1536]{2,1,0:T(8,128)(2,1)S(1)}, u32[]{:S(2)}, u32[]{:S(2)}) collective-permute-start(bf16[6,16,1536]{2,1,0:T(8,128)(2,1)} %get-tuple-element.8), channel_id=1, source_target_pairs={{0,16},{16,0},{1,17},{17,1},{2,18},{18,2},{3,19},{19,3},{4,20},{20... | collective-permute-start | bytes 884744 | tf_op jit(solution)/shard_map/ppermute | solution.py:384
  6.1 1.4 %collective-permute-done.rest_1_ = bf16[6,16,1536]{2,1,0:T(8,128)(2,1)S(1)} collective-permute-done((bf16[6,16,1536]{2,1,0:T(8,128)(2,1)}, bf16[6,16,1536]{2,1,0:T(8,128)(2,1)S(1)}, u32[]{:S(2)}, u32[]{:S(2)}) %collective-permute-start) | collective-permute-done | bytes 294944 | tf_op jit(solution)/shard_map/ppermute | solution.py:384
  7.6 0.0 copy-start.7
  7.6 0.7 %copy-done.7 = bf16[6,16,1536]{2,1,0:T(8,128)(2,1)} copy-done((bf16[6,16,1536]{2,1,0:T(8,128)(2,1)}, bf16[6,16,1536]{2,1,0:T(8,128)(2,1)S(1)}, u32[]{:S(2)}) %copy-start.7) | copy-done | bytes 294936
  8.3 2.3 %spread.1 = bf16[16,8,1152]{2,1,0:T(8,128)(2,1)} custom-call(s32[3,2]{1,0:T(4,128)} %copy.16.rows_ref, s32[3,2]{1,0:T(4,128)} %copy.17.cols_ref, bf16[6,16,1536]{2,1,0:T(8,128)(2,1)} %get-tuple-element.7.rest_0_, bf16[6,16,1536]{2,1,0:T(8,128)(2,1)} %copy-done.7), custom_call_target="tpu_custom_call" | custom-call | tf_op jit(solution)/shard_map/spread/pallas_call | solution.py:389
  10.5 19.3 %all_to_all.10.in_ref = bf16[16,8,1152]{2,1,0:T(8,128)(2,1)} all-to-all(bf16[16,8,1152]{2,1,0:T(8,128)(2,1)} %spread.1), channel_id=1, replica_groups=mesh['star'=2,'dev'=16] {'dev'}, dimensions={0} | all-to-all | bytes 589824 | tf_op jit(solution)/shard_map/all_to_all | solution.py:397
  29.9 1.8 %choose.1 = bf16[16,8,1152]{2,1,0:T(8,128)(2,1)} custom-call(s32[3,2]{1,0:T(4,128)} %copy.16.rows_ref, bf16[16,8,1152]{2,1,0:T(8,128)(2,1)} %all_to_all.10.in_ref), custom_call_target="tpu_custom_call" | custom-call | tf_op jit(solution)/shard_map/choose/pallas_call | solution.py:398
  31.7 3.5 %all-to-all-start.1 = ((bf16[16,8,1152]{2,1,0:T(8,128)(2,1)}), bf16[16,8,1152]{2,1,0:T(8,128)(2,1)S(1)}, u32[]{:S(2)}, u32[]{:S(2)}) async-start(bf16[16,8,1152]{2,1,0:T(8,128)(2,1)} %choose.1), calls=%async_computation.1 | async-start | bytes 589824 | tf_op jit(solution)/shard_map/all_to_all | solution.py:405
  35.2 0.0 copy-done.8
  35.2 0.1 copy.18.wind_ref
  36.0 9.4 %all-to-all-done.1.in_ref = bf16[16,8,1152]{2,1,0:T(8,128)(2,1)S(1)} async-done(((bf16[16,8,1152]{2,1,0:T(8,128)(2,1)}), bf16[16,8,1152]{2,1,0:T(8,128)(2,1)S(1)}, u32[]{:S(2)}, u32[]{:S(2)}) %all-to-all-start.1) | async-done | bytes 294944 | tf_op jit(solution)/shard_map/all_to_all | solution.py:405
  45.4 0.0 copy-done
  45.4 0.0 copy-done.1
  45.4 0.0 copy-done.6
  45.4 0.0 copy-done.2
  45.4 0.0 copy-done.4
  45.4 0.0 copy-done.3
  45.4 0.0 copy-done.5
  45.4 6.1 %spots.1 = f32[240,256]{1,0:T(8,128)} custom-call(s32[3,2]{1,0:T(4,128)S(1)} %copy-done.3, s32[3,2]{1,0:T(4,128)S(1)} %copy-done.5, s32[3,3,2]{2,1,0:T(4,128)S(1)} %copy.18.wind_ref, s32[1,1]{1,0:T(1,128)S(6)} %copy.20.owner_ref, bf16[16,8,1152]{2,1,0:T(8,128)(2,1)S(1)} %all-to-all-done.1.in_ref, f32[16,1280]{1,0:T(8,128)S(1)} %copy-done.2, ...), custom_call_target="tpu_custom_call" | custom-call | tf_op jit(solution)/shard_map/spots/pallas_call | solution.py:409
Async XLA Ops:
  0.0 45.4 %copy-start = (bf16[256,1024]{1,0:T(8,128)(2,1)S(1)}, bf16[256,1024]{1,0:T(8,128)(2,1)}, u32[]{:S(2)}) copy-start(bf16[256,1024]{1,0:T(8,128)(2,1)} %constant.6.clone.high_ref) | copy-start | bytes 1572868
  0.0 45.4 %copy-start.1 = (bf16[256,1024]{1,0:T(8,128)(2,1)S(1)}, bf16[256,1024]{1,0:T(8,128)(2,1)}, u32[]{:S(2)}) copy-start(bf16[256,1024]{1,0:T(8,128)(2,1)} %constant.7.clone.low_ref) | copy-start | bytes 1572868
  0.0 45.4 %copy-start.6 = (bf16[128,96]{1,0:T(8,128)(2,1)S(1)}, bf16[128,96]{1,0:T(8,128)(2,1)}, u32[]{:S(2)}) copy-start(bf16[128,96]{1,0:T(8,128)(2,1)} %constant.8.clone.down_ref) | copy-start | bytes 73732
  0.0 35.2 %copy-start.8 = (s32[3,3,2]{1,2,0:T(2,128)S(1)}, s32[3,3,2]{1,2,0:T(2,128)}, u32[]{:S(2)}) copy-start(s32[3,3,2]{1,2,0:T(2,128)} %param.13) | copy-start | bytes 220
  0.0 45.4 %copy-start.2 = (f32[16,1280]{1,0:T(8,128)S(1)}, f32[16,1280]{1,0:T(8,128)}, u32[]{:S(2)}) copy-start(f32[16,1280]{1,0:T(8,128)} %amp_ref.1) | copy-start | bytes 245764
  0.0 45.4 %copy-start.4 = (f32[6,16,16]{2,1,0:T(8,128)S(1)}, f32[6,16,16]{2,1,0:T(8,128)}, u32[]{:S(2)}) copy-start(f32[6,16,16]{2,1,0:T(8,128)} %refs_ref.1) | copy-start | bytes 18436
  1.5 43.9 %copy-start.3 = (s32[3,2]{1,0:T(4,128)S(1)}, s32[3,2]{1,0:T(4,128)}, u32[]{:S(2)}) copy-start(s32[3,2]{1,0:T(4,128)} %copy.16.rows_ref) | copy-start | bytes 76
  2.8 42.6 %copy-start.5 = (s32[3,2]{1,0:T(4,128)S(1)}, s32[3,2]{1,0:T(4,128)}, u32[]{:S(2)}) copy-start(s32[3,2]{1,0:T(4,128)} %copy.17.cols_ref) | copy-start | bytes 76
  5.6 2.0 %collective-permute-start = (bf16[6,16,1536]{2,1,0:T(8,128)(2,1)}, bf16[6,16,1536]{2,1,0:T(8,128)(2,1)S(1)}, u32[]{:S(2)}, u32[]{:S(2)}) collective-permute-start(bf16[6,16,1536]{2,1,0:T(8,128)(2,1)} %get-tuple-element.8), channel_id=1, source_target_pairs={{0,16},{16,0},{1,17},{17,1},{2,18},{18,2},{3,19},{19,3},{4,20},{20... | collective-permute-start | bytes 884744 | tf_op jit(solution)/shard_map/ppermute | solution.py:384
  7.6 0.7 %copy-start.7 = (bf16[6,16,1536]{2,1,0:T(8,128)(2,1)}, bf16[6,16,1536]{2,1,0:T(8,128)(2,1)S(1)}, u32[]{:S(2)}) copy-start(bf16[6,16,1536]{2,1,0:T(8,128)(2,1)S(1)} %collective-permute-done.rest_1_) | copy-start | bytes 884740
  31.7 13.7 %all-to-all-start.1 = ((bf16[16,8,1152]{2,1,0:T(8,128)(2,1)}), bf16[16,8,1152]{2,1,0:T(8,128)(2,1)S(1)}, u32[]{:S(2)}, u32[]{:S(2)}) async-start(bf16[16,8,1152]{2,1,0:T(8,128)(2,1)} %choose.1), calls=%async_computation.1 | async-start | bytes 589824 | tf_op jit(solution)/shard_map/all_to_all | solution.py:405

commit v2 on v1

--- a/solution.py
+++ b/solution.py
@@ -60,10 +60,10 @@
 
 
 def place_of(rows_ref, cols_ref, layer, star, devices, total_tiles):
-    offset = rows_ref[layer, star]
+    offset = rows_ref[star, layer]
     strip = lax.div(offset, SIDE)
     part = lax.rem(offset, SIDE)
-    tile = jnp.minimum(lax.div(cols_ref[layer, star], LANES), total_tiles - SPAN)
+    tile = jnp.minimum(lax.div(cols_ref[star, layer], LANES), total_tiles - SPAN)
     return strip, part, tile
 
 
@@ -145,14 +145,14 @@
 
 
 def choose_kernel(devices, rows_ref, in_ref, out_ref):
-    layers = rows_ref.shape[0]
+    layers = rows_ref.shape[1]
     width = in_ref.shape[2] // layers
     half = in_ref.shape[1] // 2
     me = lax.axis_index("star")
     mine = lax.rem(lax.axis_index("dev"), SIDE)
     upper = lax.broadcasted_iota(jnp.int32, (2 * half, width), 0) < half
     for layer in range(layers):
-        offset = rows_ref[layer, me]
+        offset = rows_ref[me, layer]
         base = lax.div(offset, SIDE) + (mine < lax.rem(offset, SIDE)).astype(jnp.int32)
         lanes = slice(layer * width, (layer + 1) * width)
         now = in_ref[lax.rem(base, devices), :, lanes].astype(F32)
@@ -198,36 +198,7 @@
     )
 
 
-def spots_kernel(
-    stars,
-    devices,
-    total_tiles,
-    rows_ref,
-    cols_ref,
-    wind_ref,
-    owner_ref,
-    in_ref,
-    amp_ref,
-    refs_ref,
-    high_ref,
-    low_ref,
-    down_ref,
-    out_ref,
-    turned,
-    window,
-    field,
-    first,
-    binned,
-    table,
-):
-    steps, layers = wind_ref.shape[0], wind_ref.shape[1]
-    across = amp_ref.shape[1] // LANES
-    groups = devices // SIDE
-    sub = QUART // groups
-    me = lax.axis_index("star")
-    row = lax.broadcasted_iota(jnp.int32, (SIDE, LANES), 0)
-    lane = lax.broadcasted_iota(jnp.int32, (SIDE, LANES), 1)
-
+def table_kernel(owner_ref, refs_ref, table):
     refer = refs_ref[owner_ref[0, 0]]
     wide = SIDE * SIDE
     pick_row = lax.broadcasted_iota(jnp.int32, (SIDE, wide), 0)
@@ -257,12 +228,41 @@
         table[pl.ds(wide + q * SIDE, SIDE), :] = high
         table[pl.ds(2 * wide + q * SIDE, SIDE), :] = low
 
+
+def spots_kernel(
+    stars,
+    devices,
+    total_tiles,
+    rows_ref,
+    cols_ref,
+    wind_ref,
+    in_ref,
+    amp_ref,
+    table,
+    high_ref,
+    low_ref,
+    down_ref,
+    out_ref,
+    turned,
+    window,
+    field,
+    first,
+    binned,
+):
+    steps, layers = wind_ref.shape[0], wind_ref.shape[2]
+    across = amp_ref.shape[1] // LANES
+    groups = devices // SIDE
+    sub = QUART // groups
+    me = lax.axis_index("star")
+    row = lax.broadcasted_iota(jnp.int32, (SIDE, LANES), 0)
+    lane = lax.broadcasted_iota(jnp.int32, (SIDE, LANES), 1)
+
     for x in range(devices):
         seen = in_ref[x].astype(F32)
         for unit in range(layers * THIRD):
             turned[unit, pl.ds(x * 2 * sub, 2 * sub), :] = seen[:, unit * LANES : (unit + 1) * LANES]
     for layer in range(layers):
-        part = lax.rem(rows_ref[layer, me], SIDE)
+        part = lax.rem(rows_ref[me, layer], SIDE)
         early = row < part
         for a in range(QUART):
             for b in range(THIRD):
@@ -282,12 +282,12 @@
     def one_step(step, carry):
         phase = [None] * across
         for layer in range(layers):
-            left = cols_ref[layer, me]
+            left = cols_ref[me, layer]
             tile = jnp.minimum(lax.div(left, LANES), total_tiles - SPAN)
-            shift = left - tile * LANES + wind_ref[step, layer, 1]
+            shift = left - tile * LANES + wind_ref[step, 1, layer]
             skip = lax.div(shift, LANES)
             fine = lax.rem(shift, LANES)
-            start = lax.rem(rows_ref[layer, me], SIDE) + wind_ref[step, layer, 0]
+            start = lax.rem(rows_ref[me, layer], SIDE) + wind_ref[step, 0, layer]
             inside = lane < LANES - fine
             rolled = [
                 pltpu.roll(
@@ -364,18 +364,22 @@
     stars, devices = lax.axis_size("star"), lax.axis_size("dev")
     layers, _, side, width = screens.shape
     steps = wind.shape[0]
+    foot_rows, foot_cols = foot_rows.T, foot_cols.T
+    wind = wind.transpose(0, 2, 1)
     tiles = width // LANES
     held = min(SPAN, tiles)
     subs = amplitude.shape[1] // side
     smem = pl.BlockSpec(memory_space=pltpu.SMEM)
     vmem = pl.BlockSpec(memory_space=pltpu.VMEM)
-    hbm = pl.BlockSpec(memory_space=pl.ANY)
+    hbm = pl.BlockSpec(memory_space=pltpu.HBM)
+    screens = pltpu.with_memory_space_constraint(screens, pltpu.HBM)
     crops = pl.pallas_call(
         functools.partial(crop_kernel, stars, devices),
         out_shape=[jax.ShapeDtypeStruct((2 * layers, side, held * LANES), BF16)] * stars,
         in_specs=[smem, smem, hbm],
         out_specs=[vmem] * stars,
         scratch_shapes=[pltpu.SemaphoreType.DMA((stars, 2 * layers))],
+        compiler_params=pltpu.CompilerParams(vmem_limit_bytes=2 << 20),
         name="crop",
     )(foot_rows, foot_cols, screens)
     parts = [crops[0]]
@@ -392,6 +396,7 @@
         in_specs=[smem, smem] + [vmem] * stars,
         out_specs=vmem,
         scratch_shapes=[pltpu.VMEM((layers * THIRD, 2 * QUART * SIDE, LANES), F32)],
+        compiler_params=pltpu.CompilerParams(vmem_limit_bytes=4 << 20),
         name="spread",
     )(foot_rows, foot_cols, *parts)
     held_rows = lax.all_to_all(sent, "dev", 0, 0, tiled=True)
@@ -400,16 +405,26 @@
         out_shape=block,
         in_specs=[smem, vmem],
         out_specs=vmem,
+        compiler_params=pltpu.CompilerParams(vmem_limit_bytes=2 << 20),
         name="choose",
     )(foot_rows, held_rows)
     strips = lax.all_to_all(chosen, "dev", 0, 0, tiled=True)
+    wide = SIDE * SIDE
+    table = pl.pallas_call(
+        table_kernel,
+        out_shape=jax.ShapeDtypeStruct((3 * wide, wide), BF16),
+        in_specs=[smem, vmem],
+        out_specs=vmem,
+        compiler_params=pltpu.CompilerParams(vmem_limit_bytes=2 << 20),
+        name="table",
+    )(owner, refs)
     high, low = across_tables()
     count = steps * subs
     padded = -(-count // 64) * 64
     found = pl.pallas_call(
         functools.partial(spots_kernel, stars, devices, stars * tiles),
         out_shape=jax.ShapeDtypeStruct((count, SIDE * SIDE), F32),
-        in_specs=[smem] * 4 + [vmem] * 6,
+        in_specs=[smem] * 3 + [vmem] * 6,
         out_specs=vmem,
         scratch_shapes=[
             pltpu.VMEM((layers * THIRD, devices * depth, LANES), F32),
@@ -417,11 +432,10 @@
             pltpu.VMEM((2, subs // 8 * SIDE, 2 * LANES), BF16),
             pltpu.VMEM((subs // 8 * SIDE, high.shape[1]), F32),
             pltpu.VMEM((padded // 8 * SIDE, LANES), F32),
-            pltpu.VMEM((3 * SIDE * SIDE, SIDE * SIDE), BF16),
         ],
-        compiler_params=pltpu.CompilerParams(vmem_limit_bytes=48 << 20),
+        compiler_params=pltpu.CompilerParams(vmem_limit_bytes=16 << 20),
         name="spots",
-    )(foot_rows, foot_cols, wind, owner, strips, amplitude, refs, high, low, down_table())
+    )(foot_rows, foot_cols, wind, strips, amplitude, table, high, low, down_table())
     return found.reshape(steps, 1, 1, subs, SIDE * SIDE)
 
 

time: 52 us -> 46.2 us (0.89)
  Pallas kernels: 13 us -> 10.3 us
  local copies, waits for them, and re-layouts: 3.61 us -> 1.48 us
    unnamed x21 -> x20, local copies, waits for them, and re-layouts: 3.61 us -> 1.48 us
    pallas_call x1, Pallas kernels: 2.26 us -> 1.05 us  [shards(): pl.pallas_call(functools.partial(spread_kernel, stars, devices, tiles), o...]
    pallas_call x1, Pallas kernels: 2.8 us -> 1.78 us  [shards(): pl.pallas_call(functools.partial(crop_kernel, stars, devices), out_shape=...]
  transfers between devices with their start and end apart: 2 -> 2, of which waited for: 2 -> 2; matrix products, arithmetic and copies ran while one was open for 0% -> 0% of each run, Pallas kernels for 0% -> 1%
where the time goes in v2:
time: 46.2 us; the launch traced here: 45.9 us
  blocking collectives  19 us (41%)
  Pallas kernels  10.3 us (22%)
  waiting for transfers between devices  10.3 us (22%)
  starting transfers between devices  4.06 us (9%)
  local copies, waits for them, and re-layouts  1.48 us (3%)
  between operations  0.72 us (2%)
    all_to_all x1, blocking collectives, shards(): held_rows = lax.all_to_all(sent, 'dev', 0, 0, tiled=True)  19 us
    all_to_all x1, waiting for transfers between devices, shards(): strips = lax.all_to_all(chosen, 'dev', 0, 0, tiled=True)  9.12 us
    pallas_call x1, Pallas kernels, shards(): pl.pallas_call(functools.partial(spots_kernel, stars, devices, stars * ti...  5.68 us
    all_to_all x1, starting transfers between devices, shards(): strips = lax.all_to_all(chosen, 'dev', 0, 0, tiled=True)  3.54 us
    pallas_call x1, Pallas kernels, shards(): pl.pallas_call(functools.partial(crop_kernel, stars, devices), out_shape=...  1.78 us
    unnamed x20, local copies, waits for them, and re-layouts  1.48 us
    pallas_call x1, Pallas kernels, shards(): pl.pallas_call(functools.partial(choose_kernel, devices), out_shape=block...  1.41 us
    ppermute x1, waiting for transfers between devices, shards(): lax.ppermute(crops[turn], 'star', [(i, (i + turn) % stars) for i in range...  1.21 us
  transfers between devices with their start and end apart: 2, of which 2 were waited for; matrix products, arithmetic and copies ran while one was open for 0% of the time, Pallas kernels for 1%

profile of v2, /device:TPU:0, one launch (start us, length us, event | category | flops | bytes accessed | tf_op | source)
XLA Modules:
  0.0 45.9 jit_solution(3743411446524906322)
XLA Ops:
  0.0 0.0 copy-start
  0.0 0.0 copy-start.1
  0.0 0.0 copy-start.4
  0.0 0.0 copy-start.3
  0.0 0.0 copy-start.2
  0.0 0.0 copy-start.5
  0.0 0.8 %copy-done.5 = s32[3,2]{0,1:T(2,128)S(1)} copy-done((s32[3,2]{0,1:T(2,128)S(1)}, s32[3,2]{0,1:T(2,128)}, u32[]{:S(2)}) %copy-start.5) | copy-done | bytes 48
  0.8 0.0 copy-start.7
  0.8 0.7 %copy-done.7 = s32[3,2]{0,1:T(2,128)S(1)} copy-done((s32[3,2]{0,1:T(2,128)S(1)}, s32[3,2]{0,1:T(2,128)}, u32[]{:S(2)}) %copy-start.7) | copy-done | bytes 48
  1.5 0.0 copy-start.6
  1.5 0.0 copy-start.8
  1.5 0.0 copy-start.9
  1.5 1.8 %crop.1 = (bf16[6,16,1536]{2,1,0:T(8,128)(2,1)S(1)}, bf16[6,16,1536]{2,1,0:T(8,128)(2,1)S(1)}) custom-call(s32[2,3]{1,0:T(2,128)S(1)} %bitcast.6, s32[2,3]{1,0:T(2,128)S(1)} %bitcast.10, bf16[3,32,16,4096]{3,2,1,0:T(8,128)(2,1)} %screens_ref.1), custom_call_target="tpu_custom_call" | custom-call | tf_op jit(solution)/shard_map/crop/pallas_call | solution.py:376
  3.3 0.5 %collective-permute-start = (bf16[6,16,1536]{2,1,0:T(8,128)(2,1)S(1)}, bf16[6,16,1536]{2,1,0:T(8,128)(2,1)S(1)}, u32[]{:S(2)}, u32[]{:S(2)}) collective-permute-start(bf16[6,16,1536]{2,1,0:T(8,128)(2,1)S(1)} %get-tuple-element.8), channel_id=1, source_target_pairs={{0,16},{16,0},{1,17},{17,1},{2,18},{18,2},{3,19},{19,3},{4,20},{20... | collective-permute-start | bytes 884744 | tf_op jit(solution)/shard_map/ppermute | solution.py:388
  3.8 1.2 %collective-permute-done.rest_1_ = bf16[6,16,1536]{2,1,0:T(8,128)(2,1)S(1)} collective-permute-done((bf16[6,16,1536]{2,1,0:T(8,128)(2,1)S(1)}, bf16[6,16,1536]{2,1,0:T(8,128)(2,1)S(1)}, u32[]{:S(2)}, u32[]{:S(2)}) %collective-permute-start) | collective-permute-done | bytes 294944 | tf_op jit(solution)/shard_map/ppermute | solution.py:388
  5.0 0.0 copy-done.6
  5.0 0.0 copy-done.8
  5.0 1.1 %spread.1 = bf16[16,8,1152]{2,1,0:T(8,128)(2,1)S(1)} custom-call(s32[2,3]{1,0:T(2,128)S(1)} %bitcast.7, s32[2,3]{1,0:T(2,128)S(1)} %bitcast.11, bf16[6,16,1536]{2,1,0:T(8,128)(2,1)S(1)} %get-tuple-element.7.rest_0_, bf16[6,16,1536]{2,1,0:T(8,128)(2,1)S(1)} %collective-permute-done.rest_1_), custom_call_target="tpu_custom_call" | custom-call | tf_op jit(solution)/shard_map/spread/pallas_call | solution.py:393
  6.1 19.0 %all_to_all.10.in_ref = bf16[16,8,1152]{2,1,0:T(8,128)(2,1)S(1)} all-to-all(bf16[16,8,1152]{2,1,0:T(8,128)(2,1)S(1)} %spread.1), channel_id=1, replica_groups=mesh['star'=2,'dev'=16] {'dev'}, dimensions={0} | all-to-all | bytes 589824 | tf_op jit(solution)/shard_map/all_to_all | solution.py:402
  25.1 1.4 %choose.1 = bf16[16,8,1152]{2,1,0:T(8,128)(2,1)} custom-call(s32[2,3]{1,0:T(2,128)S(1)} %bitcast.8, bf16[16,8,1152]{2,1,0:T(8,128)(2,1)S(1)} %all_to_all.10.in_ref), custom_call_target="tpu_custom_call" | custom-call | tf_op jit(solution)/shard_map/choose/pallas_call | solution.py:403
  26.5 3.5 %all-to-all-start.1 = ((bf16[16,8,1152]{2,1,0:T(8,128)(2,1)}), bf16[16,8,1152]{2,1,0:T(8,128)(2,1)S(1)}, u32[]{:S(2)}, u32[]{:S(2)}) async-start(bf16[16,8,1152]{2,1,0:T(8,128)(2,1)} %choose.1), calls=%async_computation.1 | async-start | bytes 589824 | tf_op jit(solution)/shard_map/all_to_all | solution.py:411
  30.7 0.0 copy-done.3
  30.7 0.3 table.1
  31.0 9.1 %all-to-all-done.1.in_ref = bf16[16,8,1152]{2,1,0:T(8,128)(2,1)S(1)} async-done(((bf16[16,8,1152]{2,1,0:T(8,128)(2,1)}), bf16[16,8,1152]{2,1,0:T(8,128)(2,1)S(1)}, u32[]{:S(2)}, u32[]{:S(2)}) %all-to-all-start.1) | async-done | bytes 294944 | tf_op jit(solution)/shard_map/all_to_all | solution.py:411
  40.2 0.0 copy-done
  40.2 0.0 copy-done.1
  40.2 0.0 copy-done.4
  40.2 0.0 copy-done.2
  40.2 0.0 copy-done.9
  40.2 5.7 %spots.1 = f32[240,256]{1,0:T(8,128)} custom-call(s32[2,3]{1,0:T(2,128)S(1)} %bitcast.9, s32[2,3]{1,0:T(2,128)S(1)} %bitcast.12, s32[3,2,3]{2,1,0:T(2,128)S(1)} %bitcast.13, bf16[16,8,1152]{2,1,0:T(8,128)(2,1)S(1)} %all-to-all-done.1.in_ref, f32[16,1280]{1,0:T(8,128)S(1)} %copy-done.2, bf16[768,256]{1,0:T(8,128)(2,1)S(1)} %table.1, ...), custom_call_target="tpu_custom_call" | custom-call | tf_op jit(solution)/shard_map/spots/pallas_call | solution.py:424
Async XLA Ops:
  0.0 40.2 %copy-start = (bf16[256,1024]{1,0:T(8,128)(2,1)S(1)}, bf16[256,1024]{1,0:T(8,128)(2,1)}, u32[]{:S(2)}) copy-start(bf16[256,1024]{1,0:T(8,128)(2,1)} %constant.6.clone.high_ref) | copy-start | bytes 1572868
  0.0 40.2 %copy-start.1 = (bf16[256,1024]{1,0:T(8,128)(2,1)S(1)}, bf16[256,1024]{1,0:T(8,128)(2,1)}, u32[]{:S(2)}) copy-start(bf16[256,1024]{1,0:T(8,128)(2,1)} %constant.7.clone.low_ref) | copy-start | bytes 1572868
  0.0 40.2 %copy-start.4 = (bf16[128,96]{1,0:T(8,128)(2,1)S(1)}, bf16[128,96]{1,0:T(8,128)(2,1)}, u32[]{:S(2)}) copy-start(bf16[128,96]{1,0:T(8,128)(2,1)} %constant.8.clone.down_ref) | copy-start | bytes 73732
  0.0 30.7 %copy-start.3 = (f32[6,16,16]{2,1,0:T(8,128)S(1)}, f32[6,16,16]{2,1,0:T(8,128)}, u32[]{:S(2)}) copy-start(f32[6,16,16]{2,1,0:T(8,128)} %refs_ref.1) | copy-start | bytes 18436
  0.0 40.2 %copy-start.2 = (f32[16,1280]{1,0:T(8,128)S(1)}, f32[16,1280]{1,0:T(8,128)}, u32[]{:S(2)}) copy-start(f32[16,1280]{1,0:T(8,128)} %amp_ref.1) | copy-start | bytes 245764
  0.0 0.8 %copy-start.5 = (s32[3,2]{0,1:T(2,128)S(1)}, s32[3,2]{0,1:T(2,128)}, u32[]{:S(2)}) copy-start(s32[3,2]{0,1:T(2,128)} %param.11) | copy-start | bytes 76
  0.8 0.7 %copy-start.7 = (s32[3,2]{0,1:T(2,128)S(1)}, s32[3,2]{0,1:T(2,128)}, u32[]{:S(2)}) copy-start(s32[3,2]{0,1:T(2,128)} %param.12) | copy-start | bytes 76
  1.5 3.5 %copy-start.6 = (s32[3,2]{0,1:T(2,128)S(1)}, s32[3,2]{0,1:T(2,128)}, u32[]{:S(2)}) copy-start(s32[3,2]{0,1:T(2,128)} %param.11) | copy-start | bytes 76
  1.5 3.5 %copy-start.8 = (s32[3,2]{0,1:T(2,128)S(1)}, s32[3,2]{0,1:T(2,128)}, u32[]{:S(2)}) copy-start(s32[3,2]{0,1:T(2,128)} %param.12) | copy-start | bytes 76
  1.5 38.7 %copy-start.9 = (s32[3,3,2]{1,2,0:T(2,128)S(1)}, s32[3,3,2]{1,2,0:T(2,128)}, u32[]{:S(2)}) copy-start(s32[3,3,2]{1,2,0:T(2,128)} %param.13) | copy-start | bytes 220
  3.3 1.7 %collective-permute-start = (bf16[6,16,1536]{2,1,0:T(8,128)(2,1)S(1)}, bf16[6,16,1536]{2,1,0:T(8,128)(2,1)S(1)}, u32[]{:S(2)}, u32[]{:S(2)}) collective-permute-start(bf16[6,16,1536]{2,1,0:T(8,128)(2,1)S(1)} %get-tuple-element.8), channel_id=1, source_target_pairs={{0,16},{16,0},{1,17},{17,1},{2,18},{18,2},{3,19},{19,3},{4,20},{20... | collective-permute-start | bytes 884744 | tf_op jit(solution)/shard_map/ppermute | solution.py:388
  26.5 13.7 %all-to-all-start.1 = ((bf16[16,8,1152]{2,1,0:T(8,128)(2,1)}), bf16[16,8,1152]{2,1,0:T(8,128)(2,1)S(1)}, u32[]{:S(2)}, u32[]{:S(2)}) async-start(bf16[16,8,1152]{2,1,0:T(8,128)(2,1)} %choose.1), calls=%async_computation.1 | async-start | bytes 589824 | tf_op jit(solution)/shard_map/all_to_all | solution.py:411

commit v3 on v2

--- a/solution.py
+++ b/solution.py
@@ -71,8 +71,16 @@
     return jnp.clip(tile - panel * tiles, 0, tiles - held)
 
 
-def crop_kernel(stars, devices, rows_ref, cols_ref, screens_ref, *rest):
-    outs, sem = rest[:stars], rest[stars]
+def crop_kernel(stars, devices, rows_hbm, cols_hbm, screens_ref, *rest):
+    outs, (sem, rows_ref, cols_ref, scalar_sem) = rest[:stars], rest[stars:]
+    scalars = [
+        pltpu.make_async_copy(rows_hbm, rows_ref, scalar_sem.at[0]),
+        pltpu.make_async_copy(cols_hbm, cols_ref, scalar_sem.at[1]),
+    ]
+    for copy in scalars:
+        copy.start()
+    for copy in scalars:
+        copy.wait()
     layers, bands, side, width = screens_ref.shape
     tiles = width // LANES
     held = min(SPAN, tiles)
@@ -239,8 +247,7 @@
     in_ref,
     amp_ref,
     table,
-    high_ref,
-    low_ref,
+    across_ref,
     down_ref,
     out_ref,
     turned,
@@ -248,6 +255,7 @@
     field,
     first,
     binned,
+    images,
 ):
     steps, layers = wind_ref.shape[0], wind_ref.shape[2]
     across = amp_ref.shape[1] // LANES
@@ -279,7 +287,7 @@
         (binned.shape[0] - steps * across * SIDE, LANES), F32
     )
 
-    def one_step(step, carry):
+    for step in range(steps):
         phase = [None] * across
         for layer in range(layers):
             left = cols_ref[me, layer]
@@ -303,36 +311,34 @@
         for t in range(across):
             sine, cosine = sin_cos(phase[t])
             amp = amp_ref[:, t * LANES : (t + 1) * LANES]
+            rows = pl.ds((step * across + t) * SIDE, SIDE)
             for part, value in enumerate((amp * cosine, amp * sine)):
                 high, low = split(value)
-                lanes = slice(part * LANES, (part + 1) * LANES)
-                field[0, pl.ds(t * SIDE, SIDE), lanes] = high
-                field[1, pl.ds(t * SIDE, SIDE), lanes] = low
-        first[...] = (
-            matmul(field[0], high_ref[...])
-            + matmul(field[1], high_ref[...])
-            + matmul(field[0], low_ref[...])
+                at = part * LANES
+                field[rows, at : at + LANES] = high
+                field[rows, at + 2 * LANES : at + 3 * LANES] = low
+                field[rows, at + 4 * LANES : at + 5 * LANES] = high
+
+    first[...] = matmul(field[...], across_ref[...])
+
+    wide_out = first.shape[1] // 2
+
+    for turn in range(steps * across):
+        rows = pl.ds(turn * SIDE, SIDE)
+        real_high, real_low = split(first[rows, 0:wide_out])
+        imag_high, imag_low = split(first[rows, wide_out : 2 * wide_out])
+        stacked = jnp.concatenate(
+            [real_high, imag_high, real_low, imag_low, real_high, imag_high], axis=0
         )
-        wide_out = first.shape[1] // 2
-        for t in range(across):
-            rows = pl.ds(t * SIDE, SIDE)
-            real_high, real_low = split(first[rows, 0:wide_out])
-            imag_high, imag_low = split(first[rows, wide_out : 2 * wide_out])
-            stacked = jnp.concatenate(
-                [real_high, imag_high, real_low, imag_low, real_high, imag_high], axis=0
-            )
-            spectrum = matmul(down_ref[...], stacked)
-            power = spectrum * spectrum
-            total = power[0:SIDE]
-            for k in range(1, 2 * BIN):
-                total = total + power[k * SIDE : (k + 1) * SIDE]
-            small = total[:, 0:LANES]
-            for k in range(1, BIN):
-                small = small + total[:, k * LANES : (k + 1) * LANES]
-            binned[pl.ds((step * across + t) * SIDE, SIDE), :] = small
-        return carry
-
-    lax.fori_loop(0, steps, one_step, 0)
+        spectrum = matmul(down_ref[...], stacked)
+        power = spectrum * spectrum
+        total = power[0:SIDE]
+        for k in range(1, 2 * BIN):
+            total = total + power[k * SIDE : (k + 1) * SIDE]
+        small = total[:, 0:LANES]
+        for k in range(1, BIN):
+            small = small + total[:, k * LANES : (k + 1) * LANES]
+        binned[rows, :] = small
 
     lane8 = lax.broadcasted_iota(jnp.int32, (8, LANES), 1)
     for big in range(binned.shape[0] // LANES):
@@ -355,9 +361,40 @@
         )
         image = image / jnp.sum(image, axis=1, keepdims=True)
         high, low = split(image)
-        found = matmul(jnp.concatenate([high, low, high], axis=1), table[...])
-        count = min(64, steps * across * 8 - big * 64)
-        out_ref[pl.ds(big * 64, count), :] = found[0:count]
+        rows = pl.ds(big * 64, 64)
+        wide = SIDE * SIDE
+        images[rows, 0:wide] = high
+        images[rows, wide : 2 * wide] = low
+        images[rows, 2 * wide : 3 * wide] = high
+    out_ref[...] = matmul(images[...], table[...])[0 : out_ref.shape[0]]
+
+
+def spots_call(stars, devices, total_tiles, foot_rows, foot_cols, wind, strips, amplitude, table):
+    smem = pl.BlockSpec(memory_space=pltpu.SMEM)
+    vmem = pl.BlockSpec(memory_space=pltpu.VMEM)
+    steps, layers = wind.shape[0], wind.shape[2]
+    depth = strips.shape[1]
+    subs = amplitude.shape[1] // SIDE
+    high, low = across_tables()
+    table_across = np.concatenate([high, high, low], axis=0)
+    count = steps * subs
+    padded = -(-count // 64) * 64
+    return pl.pallas_call(
+        functools.partial(spots_kernel, stars, devices, total_tiles),
+        out_shape=jax.ShapeDtypeStruct((count, SIDE * SIDE), F32),
+        in_specs=[smem] * 3 + [vmem] * 5,
+        out_specs=vmem,
+        scratch_shapes=[
+            pltpu.VMEM((layers * THIRD, devices * depth, LANES), F32),
+            pltpu.VMEM((layers * SPAN, 3 * SIDE, LANES), F32),
+            pltpu.VMEM((count // 8 * SIDE, 6 * LANES), BF16),
+            pltpu.VMEM((count // 8 * SIDE, high.shape[1]), F32),
+            pltpu.VMEM((padded // 8 * SIDE, LANES), F32),
+            pltpu.VMEM((padded, 3 * SIDE * SIDE), BF16),
+        ],
+        compiler_params=pltpu.CompilerParams(vmem_limit_bytes=16 << 20),
+        name="spots",
+    )(foot_rows, foot_cols, wind, strips, amplitude, table, table_across, down_table())
 
 
 def shards(screens, foot_rows, foot_cols, wind, amplitude, owner, refs):
@@ -376,12 +413,21 @@
     crops = pl.pallas_call(
         functools.partial(crop_kernel, stars, devices),
         out_shape=[jax.ShapeDtypeStruct((2 * layers, side, held * LANES), BF16)] * stars,
-        in_specs=[smem, smem, hbm],
+        in_specs=[hbm] * 3,
         out_specs=[vmem] * stars,
-        scratch_shapes=[pltpu.SemaphoreType.DMA((stars, 2 * layers))],
+        scratch_shapes=[
+            pltpu.SemaphoreType.DMA((stars, 2 * layers)),
+            pltpu.SMEM(foot_rows.shape, jnp.int32),
+            pltpu.SMEM(foot_cols.shape, jnp.int32),
+            pltpu.SemaphoreType.DMA((2,)),
+        ],
         compiler_params=pltpu.CompilerParams(vmem_limit_bytes=2 << 20),
         name="crop",
-    )(foot_rows, foot_cols, screens)
+    )(
+        pltpu.with_memory_space_constraint(foot_rows, pltpu.HBM),
+        pltpu.with_memory_space_constraint(foot_cols, pltpu.HBM),
+        screens,
+    )
     parts = [crops[0]]
     for turn in range(1, stars):
         parts.append(
@@ -418,24 +464,9 @@
         compiler_params=pltpu.CompilerParams(vmem_limit_bytes=2 << 20),
         name="table",
     )(owner, refs)
-    high, low = across_tables()
-    count = steps * subs
-    padded = -(-count // 64) * 64
-    found = pl.pallas_call(
-        functools.partial(spots_kernel, stars, devices, stars * tiles),
-        out_shape=jax.ShapeDtypeStruct((count, SIDE * SIDE), F32),
-        in_specs=[smem] * 3 + [vmem] * 6,
-        out_specs=vmem,
-        scratch_shapes=[
-            pltpu.VMEM((layers * THIRD, devices * depth, LANES), F32),
-            pltpu.VMEM((layers * SPAN, 3 * SIDE, LANES), F32),
-            pltpu.VMEM((2, subs // 8 * SIDE, 2 * LANES), BF16),
-            pltpu.VMEM((subs // 8 * SIDE, high.shape[1]), F32),
-            pltpu.VMEM((padded // 8 * SIDE, LANES), F32),
-        ],
-        compiler_params=pltpu.CompilerParams(vmem_limit_bytes=16 << 20),
-        name="spots",
-    )(foot_rows, foot_cols, wind, strips, amplitude, table, high, low, down_table())
+    found = spots_call(
+        stars, devices, stars * tiles, foot_rows, foot_cols, wind, strips, amplitude, table
+    )
     return found.reshape(steps, 1, 1, subs, SIDE * SIDE)
 
 

time: 46.2 us -> 44.1 us (0.955)
  local copies, waits for them, and re-layouts: 1.48 us -> 0.03 us
  Pallas kernels: 10.3 us -> 9.61 us
    unnamed x20 -> x14, local copies, waits for them, and re-layouts: 1.48 us -> 0.03 us
    pallas_call x1, Pallas kernels: 5.68 us -> 4.73 us  [spots_call(): pl.pallas_call(functools.partial(spots_kernel, stars, devices, total_tile...]
where the time goes in v3:
time: 44.1 us; the launch traced here: 43.8 us
  blocking collectives  19 us (43%)
  waiting for transfers between devices  10.3 us (23%)
  Pallas kernels  9.61 us (22%)
  starting transfers between devices  4.07 us (9%)
  between operations  0.72 us (2%)
    all_to_all x1, blocking collectives, shards(): held_rows = lax.all_to_all(sent, 'dev', 0, 0, tiled=True)  19 us
    all_to_all x1, waiting for transfers between devices, shards(): strips = lax.all_to_all(chosen, 'dev', 0, 0, tiled=True)  9.12 us
    pallas_call x1, Pallas kernels, spots_call(): pl.pallas_call(functools.partial(spots_kernel, stars, devices, total_tile...  4.73 us
    all_to_all x1, starting transfers between devices, shards(): strips = lax.all_to_all(chosen, 'dev', 0, 0, tiled=True)  3.54 us
    pallas_call x1, Pallas kernels, shards(): pl.pallas_call(functools.partial(crop_kernel, stars, devices), out_shape=...  2.07 us
    pallas_call x1, Pallas kernels, shards(): pl.pallas_call(functools.partial(choose_kernel, devices), out_shape=block...  1.41 us
    ppermute x1, waiting for transfers between devices, shards(): lax.ppermute(crops[turn], 'star', [(i, (i + turn) % stars) for i in range...  1.21 us
    pallas_call x1, Pallas kernels, shards(): pl.pallas_call(functools.partial(spread_kernel, stars, devices, tiles), o...  1.05 us
  transfers between devices with their start and end apart: 2, of which 2 were waited for; matrix products, arithmetic and copies ran while one was open for 0% of the time, Pallas kernels for 1%

profile of v3, /device:TPU:0, one launch (start us, length us, event | category | flops | bytes accessed | tf_op | source)
XLA Modules:
  0.0 43.8 jit_solution(3043234328933555917)
XLA Ops:
  0.0 0.0 copy-start
  0.0 0.0 copy-start.3
  0.0 0.0 copy-start.4
  0.0 0.0 copy-start.5
  0.0 0.0 copy-start.2
  0.0 0.0 copy-start.6
  0.0 0.0 copy-start.1
  0.0 2.1 %crop.1 = (bf16[6,16,1536]{2,1,0:T(8,128)(2,1)S(1)}, bf16[6,16,1536]{2,1,0:T(8,128)(2,1)S(1)}) custom-call(s32[2,3]{1,0:T(2,128)} %bitcast.6, s32[2,3]{1,0:T(2,128)} %bitcast.10, bf16[3,32,16,4096]{3,2,1,0:T(8,128)(2,1)} %screens_ref.1), custom_call_target="tpu_custom_call" | custom-call | tf_op jit(solution)/shard_map/crop/pallas_call | solution.py:413
  2.1 0.5 %collective-permute-start = (bf16[6,16,1536]{2,1,0:T(8,128)(2,1)S(1)}, bf16[6,16,1536]{2,1,0:T(8,128)(2,1)S(1)}, u32[]{:S(2)}, u32[]{:S(2)}) collective-permute-start(bf16[6,16,1536]{2,1,0:T(8,128)(2,1)S(1)} %get-tuple-element.8), channel_id=1, source_target_pairs={{0,16},{16,0},{1,17},{17,1},{2,18},{18,2},{3,19},{19,3},{4,20},{20... | collective-permute-start | bytes 884744 | tf_op jit(solution)/shard_map/ppermute | solution.py:434
  2.6 1.2 %collective-permute-done.rest_1_ = bf16[6,16,1536]{2,1,0:T(8,128)(2,1)S(1)} collective-permute-done((bf16[6,16,1536]{2,1,0:T(8,128)(2,1)S(1)}, bf16[6,16,1536]{2,1,0:T(8,128)(2,1)S(1)}, u32[]{:S(2)}, u32[]{:S(2)}) %collective-permute-start) | collective-permute-done | bytes 294944 | tf_op jit(solution)/shard_map/ppermute | solution.py:434
  3.9 0.0 copy-done.4
  3.9 0.0 copy-done.5
  3.9 1.1 %spread.1 = bf16[16,8,1152]{2,1,0:T(8,128)(2,1)S(1)} custom-call(s32[2,3]{1,0:T(2,128)S(1)} %bitcast.7, s32[2,3]{1,0:T(2,128)S(1)} %bitcast.11, bf16[6,16,1536]{2,1,0:T(8,128)(2,1)S(1)} %get-tuple-element.7.rest_0_, bf16[6,16,1536]{2,1,0:T(8,128)(2,1)S(1)} %collective-permute-done.rest_1_), custom_call_target="tpu_custom_call" | custom-call | tf_op jit(solution)/shard_map/spread/pallas_call | solution.py:439
  4.9 19.0 %all_to_all.10.in_ref = bf16[16,8,1152]{2,1,0:T(8,128)(2,1)S(1)} all-to-all(bf16[16,8,1152]{2,1,0:T(8,128)(2,1)S(1)} %spread.1), channel_id=1, replica_groups=mesh['star'=2,'dev'=16] {'dev'}, dimensions={0} | all-to-all | bytes 589824 | tf_op jit(solution)/shard_map/all_to_all | solution.py:448
  23.9 1.4 %choose.1 = bf16[16,8,1152]{2,1,0:T(8,128)(2,1)} custom-call(s32[2,3]{1,0:T(2,128)S(1)} %bitcast.8, bf16[16,8,1152]{2,1,0:T(8,128)(2,1)S(1)} %all_to_all.10.in_ref), custom_call_target="tpu_custom_call" | custom-call | tf_op jit(solution)/shard_map/choose/pallas_call | solution.py:449
  25.3 3.5 %all-to-all-start.1 = ((bf16[16,8,1152]{2,1,0:T(8,128)(2,1)}), bf16[16,8,1152]{2,1,0:T(8,128)(2,1)S(1)}, u32[]{:S(2)}, u32[]{:S(2)}) async-start(bf16[16,8,1152]{2,1,0:T(8,128)(2,1)} %choose.1), calls=%async_computation.1 | async-start | bytes 589824 | tf_op jit(solution)/shard_map/all_to_all | solution.py:457
  29.5 0.0 copy-done.2
  29.5 0.3 table.1
  29.9 9.1 %all-to-all-done.1.in_ref = bf16[16,8,1152]{2,1,0:T(8,128)(2,1)S(1)} async-done(((bf16[16,8,1152]{2,1,0:T(8,128)(2,1)}), bf16[16,8,1152]{2,1,0:T(8,128)(2,1)S(1)}, u32[]{:S(2)}, u32[]{:S(2)}) %all-to-all-start.1) | async-done | bytes 294944 | tf_op jit(solution)/shard_map/all_to_all | solution.py:457
  39.0 0.0 copy-done
  39.0 0.0 copy-done.3
  39.0 0.0 copy-done.6
  39.0 0.0 copy-done.1
  39.0 4.7 %spots.1 = f32[240,256]{1,0:T(8,128)} custom-call(s32[2,3]{1,0:T(2,128)S(1)} %bitcast.9, s32[2,3]{1,0:T(2,128)S(1)} %bitcast.12, s32[3,2,3]{2,1,0:T(2,128)S(1)} %bitcast.13, bf16[16,8,1152]{2,1,0:T(8,128)(2,1)S(1)} %all-to-all-done.1.in_ref, f32[16,1280]{1,0:T(8,128)S(1)} %copy-done.1, bf16[768,256]{1,0:T(8,128)(2,1)S(1)} %table.1, ...), custom_call_target="tpu_custom_call" | custom-call | tf_op jit(solution)/shard_map/spots/pallas_call | solution.py:382
Async XLA Ops:
  0.0 39.0 %copy-start = (bf16[768,1024]{1,0:T(8,128)(2,1)S(1)}, bf16[768,1024]{1,0:T(8,128)(2,1)}, u32[]{:S(2)}) copy-start(bf16[768,1024]{1,0:T(8,128)(2,1)} %constant.4.clone.across_ref) | copy-start | bytes 4718596
  0.0 39.0 %copy-start.3 = (bf16[128,96]{1,0:T(8,128)(2,1)S(1)}, bf16[128,96]{1,0:T(8,128)(2,1)}, u32[]{:S(2)}) copy-start(bf16[128,96]{1,0:T(8,128)(2,1)} %constant.5.clone.down_ref) | copy-start | bytes 73732
  0.0 3.9 %copy-start.4 = (s32[3,2]{0,1:T(2,128)S(1)}, s32[3,2]{0,1:T(2,128)}, u32[]{:S(2)}) copy-start(s32[3,2]{0,1:T(2,128)} %param.10) | copy-start | bytes 76
  0.0 3.9 %copy-start.5 = (s32[3,2]{0,1:T(2,128)S(1)}, s32[3,2]{0,1:T(2,128)}, u32[]{:S(2)}) copy-start(s32[3,2]{0,1:T(2,128)} %param.11) | copy-start | bytes 76
  0.0 29.5 %copy-start.2 = (f32[6,16,16]{2,1,0:T(8,128)S(1)}, f32[6,16,16]{2,1,0:T(8,128)}, u32[]{:S(2)}) copy-start(f32[6,16,16]{2,1,0:T(8,128)} %refs_ref.1) | copy-start | bytes 18436
  0.0 39.0 %copy-start.6 = (s32[3,3,2]{1,2,0:T(2,128)S(1)}, s32[3,3,2]{1,2,0:T(2,128)}, u32[]{:S(2)}) copy-start(s32[3,3,2]{1,2,0:T(2,128)} %param.12) | copy-start | bytes 220
  0.0 39.0 %copy-start.1 = (f32[16,1280]{1,0:T(8,128)S(1)}, f32[16,1280]{1,0:T(8,128)}, u32[]{:S(2)}) copy-start(f32[16,1280]{1,0:T(8,128)} %amp_ref.1) | copy-start | bytes 245764
  2.1 1.7 %collective-permute-start = (bf16[6,16,1536]{2,1,0:T(8,128)(2,1)S(1)}, bf16[6,16,1536]{2,1,0:T(8,128)(2,1)S(1)}, u32[]{:S(2)}, u32[]{:S(2)}) collective-permute-start(bf16[6,16,1536]{2,1,0:T(8,128)(2,1)S(1)} %get-tuple-element.8), channel_id=1, source_target_pairs={{0,16},{16,0},{1,17},{17,1},{2,18},{18,2},{3,19},{19,3},{4,20},{20... | collective-permute-start | bytes 884744 | tf_op jit(solution)/shard_map/ppermute | solution.py:434
  25.3 13.7 %all-to-all-start.1 = ((bf16[16,8,1152]{2,1,0:T(8,128)(2,1)}), bf16[16,8,1152]{2,1,0:T(8,128)(2,1)S(1)}, u32[]{:S(2)}, u32[]{:S(2)}) async-start(bf16[16,8,1152]{2,1,0:T(8,128)(2,1)} %choose.1), calls=%async_computation.1 | async-start | bytes 589824 | tf_op jit(solution)/shard_map/all_to_all | solution.py:457

commit v4 on v3

--- a/solution.py
+++ b/solution.py
@@ -107,7 +107,7 @@
         copy.wait()
 
 
-def spread_kernel(stars, devices, tiles, rows_ref, cols_ref, *rest):
+def spread_kernel(stars, devices, tiles, rows_ref, cols_ref, _, *rest):
     parts, out_ref, turned = rest[:stars], rest[stars], rest[stars + 1]
     layers = parts[0].shape[0] // 2
     held = parts[0].shape[2] // LANES
@@ -436,15 +436,24 @@
     groups = devices // SIDE
     depth = 2 * QUART // groups
     block = jax.ShapeDtypeStruct((devices, depth, layers * THIRD * LANES), BF16)
+    wide = SIDE * SIDE
+    table = pl.pallas_call(
+        table_kernel,
+        out_shape=jax.ShapeDtypeStruct((3 * wide, wide), BF16),
+        in_specs=[smem, vmem],
+        out_specs=vmem,
+        compiler_params=pltpu.CompilerParams(vmem_limit_bytes=2 << 20),
+        name="table",
+    )(owner, refs)
     sent = pl.pallas_call(
         functools.partial(spread_kernel, stars, devices, tiles),
         out_shape=block,
-        in_specs=[smem, smem] + [vmem] * stars,
+        in_specs=[smem, smem, pl.BlockSpec(memory_space=pl.ANY)] + [vmem] * stars,
         out_specs=vmem,
         scratch_shapes=[pltpu.VMEM((layers * THIRD, 2 * QUART * SIDE, LANES), F32)],
         compiler_params=pltpu.CompilerParams(vmem_limit_bytes=4 << 20),
         name="spread",
-    )(foot_rows, foot_cols, *parts)
+    )(foot_rows, foot_cols, table, *parts)
     held_rows = lax.all_to_all(sent, "dev", 0, 0, tiled=True)
     chosen = pl.pallas_call(
         functools.partial(choose_kernel, devices),
@@ -455,15 +464,6 @@
         name="choose",
     )(foot_rows, held_rows)
     strips = lax.all_to_all(chosen, "dev", 0, 0, tiled=True)
-    wide = SIDE * SIDE
-    table = pl.pallas_call(
-        table_kernel,
-        out_shape=jax.ShapeDtypeStruct((3 * wide, wide), BF16),
-        in_specs=[smem, vmem],
-        out_specs=vmem,
-        compiler_params=pltpu.CompilerParams(vmem_limit_bytes=2 << 20),
-        name="table",
-    )(owner, refs)
     found = spots_call(
         stars, devices, stars * tiles, foot_rows, foot_cols, wind, strips, amplitude, table
     )

time: 44.1 us -> 43.1 us (0.977)
  blocking collectives: 19 us -> 32.5 us
  waiting for transfers between devices: 10.3 us -> 0.19 us
  starting transfers between devices: 4.07 us -> 0.53 us
  Pallas kernels: 9.61 us -> 8.92 us
    all_to_all x0 -> x1, blocking collectives: none -> 13.5 us  [shards(): strips = lax.all_to_all(chosen, 'dev', 0, 0, tiled=True)]
    all_to_all x1 -> x0, waiting for transfers between devices: 9.12 us -> none  [shards(): strips = lax.all_to_all(chosen, 'dev', 0, 0, tiled=True)]
    all_to_all x1 -> x0, starting transfers between devices: 3.54 us -> none  [shards(): strips = lax.all_to_all(chosen, 'dev', 0, 0, tiled=True)]
    ppermute x1, waiting for transfers between devices: 1.21 us -> 0.19 us  [shards(): lax.ppermute(crops[turn], 'star', [(i, (i + turn) % stars) for i in range...]
    pallas_call x1, Pallas kernels: 1.41 us -> 0.69 us  [shards(): pl.pallas_call(functools.partial(choose_kernel, devices), out_shape=block...]
  transfers between devices with their start and end apart: 2 -> 1, of which waited for: 2 -> 1; matrix products, arithmetic and copies ran while one was open for 0% -> 0% of each run, Pallas kernels for 1% -> 1%
where the time goes in v4:
time: 43.1 us; the launch traced here: 42.9 us
  blocking collectives  32.5 us (75%)
  Pallas kernels  8.92 us (21%)
  between operations  0.72 us (2%)
  starting transfers between devices  0.53 us (1%)
    all_to_all x1, blocking collectives, shards(): held_rows = lax.all_to_all(sent, 'dev', 0, 0, tiled=True)  19 us
    all_to_all x1, blocking collectives, shards(): strips = lax.all_to_all(chosen, 'dev', 0, 0, tiled=True)  13.5 us
    pallas_call x1, Pallas kernels, spots_call(): pl.pallas_call(functools.partial(spots_kernel, stars, devices, total_tile...  4.75 us
    pallas_call x1, Pallas kernels, shards(): pl.pallas_call(functools.partial(crop_kernel, stars, devices), out_shape=...  2.07 us
    pallas_call x1, Pallas kernels, shards(): pl.pallas_call(functools.partial(spread_kernel, stars, devices, tiles), o...  1.05 us
  transfers between devices with their start and end apart: 1, of which 1 were waited for; matrix products, arithmetic and copies ran while one was open for 0% of the time, Pallas kernels for 1%

profile of v4, /device:TPU:0, one launch (start us, length us, event | category | flops | bytes accessed | tf_op | source)
XLA Modules:
  0.0 42.9 jit_solution(1089228488596910082)
XLA Ops:
  0.0 0.0 copy-start
  0.0 0.0 copy-start.3
  0.0 0.0 copy-start.4
  0.0 0.0 copy-start.5
  0.0 0.0 copy-start.2
  0.0 0.0 copy-start.6
  0.0 0.0 copy-start.1
  0.0 2.1 %crop.1 = (bf16[6,16,1536]{2,1,0:T(8,128)(2,1)S(1)}, bf16[6,16,1536]{2,1,0:T(8,128)(2,1)S(1)}) custom-call(s32[2,3]{1,0:T(2,128)} %bitcast.6, s32[2,3]{1,0:T(2,128)} %bitcast.10, bf16[3,32,16,4096]{3,2,1,0:T(8,128)(2,1)} %screens_ref.1), custom_call_target="tpu_custom_call" | custom-call | tf_op jit(solution)/shard_map/crop/pallas_call | solution.py:413
  2.1 0.5 %collective-permute-start = (bf16[6,16,1536]{2,1,0:T(8,128)(2,1)S(1)}, bf16[6,16,1536]{2,1,0:T(8,128)(2,1)S(1)}, u32[]{:S(2)}, u32[]{:S(2)}) collective-permute-start(bf16[6,16,1536]{2,1,0:T(8,128)(2,1)S(1)} %get-tuple-element.8), channel_id=1, source_target_pairs={{0,16},{16,0},{1,17},{17,1},{2,18},{18,2},{3,19},{19,3},{4,20},{20... | collective-permute-start | bytes 884744 | tf_op jit(solution)/shard_map/ppermute | solution.py:434
  3.3 0.0 copy-done.2
  3.3 0.3 table.1._
  3.7 0.2 collective-permute-done.rest_1_
  3.9 0.0 copy-done.4
  3.9 0.0 copy-done.5
  3.9 1.1 %spread.1 = bf16[16,8,1152]{2,1,0:T(8,128)(2,1)S(1)} custom-call(s32[2,3]{1,0:T(2,128)S(1)} %bitcast.7, s32[2,3]{1,0:T(2,128)S(1)} %bitcast.11, bf16[768,256]{1,0:T(8,128)(2,1)S(1)} %table.1._, bf16[6,16,1536]{2,1,0:T(8,128)(2,1)S(1)} %get-tuple-element.7.rest_0_, bf16[6,16,1536]{2,1,0:T(8,128)(2,1)S(1)} %collective-permute-done.rest_1_), custom_call_target="tpu_custom_call" | custom-call | tf_op jit(solution)/shard_map/spread/pallas_call | solution.py:448
  4.9 19.0 %all_to_all.10.in_ref = bf16[16,8,1152]{2,1,0:T(8,128)(2,1)S(1)} all-to-all(bf16[16,8,1152]{2,1,0:T(8,128)(2,1)S(1)} %spread.1), channel_id=1, replica_groups=mesh['star'=2,'dev'=16] {'dev'}, dimensions={0} | all-to-all | bytes 589824 | tf_op jit(solution)/shard_map/all_to_all | solution.py:457
  23.9 0.7 %choose.1 = bf16[16,8,1152]{2,1,0:T(8,128)(2,1)S(1)} custom-call(s32[2,3]{1,0:T(2,128)S(1)} %bitcast.8, bf16[16,8,1152]{2,1,0:T(8,128)(2,1)S(1)} %all_to_all.10.in_ref), custom_call_target="tpu_custom_call" | custom-call | tf_op jit(solution)/shard_map/choose/pallas_call | solution.py:458
  24.6 13.5 %all_to_all.11.in_ref = bf16[16,8,1152]{2,1,0:T(8,128)(2,1)S(1)} all-to-all(bf16[16,8,1152]{2,1,0:T(8,128)(2,1)S(1)} %choose.1), channel_id=1, replica_groups=mesh['star'=2,'dev'=16] {'dev'}, dimensions={0} | all-to-all | bytes 589824 | tf_op jit(solution)/shard_map/all_to_all | solution.py:466
  38.1 0.0 copy-done
  38.1 0.0 copy-done.3
  38.1 0.0 copy-done.6
  38.1 0.0 copy-done.1
  38.1 4.7 %spots.1 = f32[240,256]{1,0:T(8,128)} custom-call(s32[2,3]{1,0:T(2,128)S(1)} %bitcast.9, s32[2,3]{1,0:T(2,128)S(1)} %bitcast.12, s32[3,2,3]{2,1,0:T(2,128)S(1)} %bitcast.13, bf16[16,8,1152]{2,1,0:T(8,128)(2,1)S(1)} %all_to_all.11.in_ref, f32[16,1280]{1,0:T(8,128)S(1)} %copy-done.1, bf16[768,256]{1,0:T(8,128)(2,1)S(1)} %table.1._, ...), custom_call_target="tpu_custom_call" | custom-call | tf_op jit(solution)/shard_map/spots/pallas_call | solution.py:382
Async XLA Ops:
  0.0 38.1 %copy-start = (bf16[768,1024]{1,0:T(8,128)(2,1)S(1)}, bf16[768,1024]{1,0:T(8,128)(2,1)}, u32[]{:S(2)}) copy-start(bf16[768,1024]{1,0:T(8,128)(2,1)} %constant.4.clone.across_ref) | copy-start | bytes 4718596
  0.0 38.1 %copy-start.3 = (bf16[128,96]{1,0:T(8,128)(2,1)S(1)}, bf16[128,96]{1,0:T(8,128)(2,1)}, u32[]{:S(2)}) copy-start(bf16[128,96]{1,0:T(8,128)(2,1)} %constant.5.clone.down_ref) | copy-start | bytes 73732
  0.0 3.9 %copy-start.4 = (s32[3,2]{0,1:T(2,128)S(1)}, s32[3,2]{0,1:T(2,128)}, u32[]{:S(2)}) copy-start(s32[3,2]{0,1:T(2,128)} %param.10) | copy-start | bytes 76
  0.0 3.9 %copy-start.5 = (s32[3,2]{0,1:T(2,128)S(1)}, s32[3,2]{0,1:T(2,128)}, u32[]{:S(2)}) copy-start(s32[3,2]{0,1:T(2,128)} %param.11) | copy-start | bytes 76
  0.0 3.3 %copy-start.2 = (f32[6,16,16]{2,1,0:T(8,128)S(1)}, f32[6,16,16]{2,1,0:T(8,128)}, u32[]{:S(2)}) copy-start(f32[6,16,16]{2,1,0:T(8,128)} %refs_ref.1) | copy-start | bytes 18436
  0.0 38.1 %copy-start.6 = (s32[3,3,2]{1,2,0:T(2,128)S(1)}, s32[3,3,2]{1,2,0:T(2,128)}, u32[]{:S(2)}) copy-start(s32[3,3,2]{1,2,0:T(2,128)} %param.12) | copy-start | bytes 220
  0.0 38.1 %copy-start.1 = (f32[16,1280]{1,0:T(8,128)S(1)}, f32[16,1280]{1,0:T(8,128)}, u32[]{:S(2)}) copy-start(f32[16,1280]{1,0:T(8,128)} %amp_ref.1) | copy-start | bytes 245764
  2.1 1.7 %collective-permute-start = (bf16[6,16,1536]{2,1,0:T(8,128)(2,1)S(1)}, bf16[6,16,1536]{2,1,0:T(8,128)(2,1)S(1)}, u32[]{:S(2)}, u32[]{:S(2)}) collective-permute-start(bf16[6,16,1536]{2,1,0:T(8,128)(2,1)S(1)} %get-tuple-element.8), channel_id=1, source_target_pairs={{0,16},{16,0},{1,17},{17,1},{2,18},{18,2},{3,19},{19,3},{4,20},{20... | collective-permute-start | bytes 884744 | tf_op jit(solution)/shard_map/ppermute | solution.py:434

commit v5 on v4

--- a/solution.py
+++ b/solution.py
@@ -64,6 +64,18 @@
     strip = lax.div(offset, SIDE)
     part = lax.rem(offset, SIDE)
     tile = jnp.minimum(lax.div(cols_ref[star, layer], LANES), total_tiles - SPAN)
+    return strip, part, tile
+
+
+def own_row(ref, star):
+    row = ref[pl.ds(star, 1), :]
+    return [row[0, layer] for layer in range(ref.shape[1])]
+
+
+def place_of_own(offset, left, total_tiles):
+    strip = lax.div(offset, SIDE)
+    part = lax.rem(offset, SIDE)
+    tile = jnp.minimum(lax.div(left, LANES), total_tiles - SPAN)
     return strip, part, tile
 
 
@@ -116,8 +128,9 @@
     me = lax.axis_index("star")
     place = lax.axis_index("dev")
     row = lax.broadcasted_iota(jnp.int32, (SIDE, LANES), 0)
+    offsets, lefts = own_row(rows_ref, me), own_row(cols_ref, me)
     for layer in range(layers):
-        strip, part, tile = place_of(rows_ref, cols_ref, layer, me, devices, stars * tiles)
+        strip, part, tile = place_of_own(offsets[layer], lefts[layer], stars * tiles)
         behind = lax.rem(place + (1 << 20) * devices - strip, devices)
         bound = jnp.where(behind == 0, part, 0)
         wraps = row < bound
@@ -159,8 +172,9 @@
     me = lax.axis_index("star")
     mine = lax.rem(lax.axis_index("dev"), SIDE)
     upper = lax.broadcasted_iota(jnp.int32, (2 * half, width), 0) < half
+    offsets = own_row(rows_ref, me)
     for layer in range(layers):
-        offset = rows_ref[me, layer]
+        offset = offsets[layer]
         base = lax.div(offset, SIDE) + (mine < lax.rem(offset, SIDE)).astype(jnp.int32)
         lanes = slice(layer * width, (layer + 1) * width)
         now = in_ref[lax.rem(base, devices), :, lanes].astype(F32)
@@ -253,9 +267,6 @@
     turned,
     window,
     field,
-    first,
-    binned,
-    images,
 ):
     steps, layers = wind_ref.shape[0], wind_ref.shape[2]
     across = amp_ref.shape[1] // LANES
@@ -264,13 +275,15 @@
     me = lax.axis_index("star")
     row = lax.broadcasted_iota(jnp.int32, (SIDE, LANES), 0)
     lane = lax.broadcasted_iota(jnp.int32, (SIDE, LANES), 1)
+    offsets, lefts = own_row(rows_ref, me), own_row(cols_ref, me)
+    shifts = [wind_ref[step] for step in range(steps)]
 
     for x in range(devices):
         seen = in_ref[x].astype(F32)
         for unit in range(layers * THIRD):
             turned[unit, pl.ds(x * 2 * sub, 2 * sub), :] = seen[:, unit * LANES : (unit + 1) * LANES]
     for layer in range(layers):
-        part = lax.rem(rows_ref[me, layer], SIDE)
+        part = lax.rem(offsets[layer], SIDE)
         early = row < part
         for a in range(QUART):
             for b in range(THIRD):
@@ -283,19 +296,15 @@
                 window[slot, pl.ds(SIDE, SIDE), :] = jnp.where(early, one, two)
                 window[slot, pl.ds(2 * SIDE, SIDE), :] = two
 
-    binned[pl.ds(steps * across * SIDE, binned.shape[0] - steps * across * SIDE), :] = jnp.ones(
-        (binned.shape[0] - steps * across * SIDE, LANES), F32
-    )
-
     for step in range(steps):
         phase = [None] * across
         for layer in range(layers):
-            left = cols_ref[me, layer]
+            left = lefts[layer]
             tile = jnp.minimum(lax.div(left, LANES), total_tiles - SPAN)
-            shift = left - tile * LANES + wind_ref[step, 1, layer]
+            shift = left - tile * LANES + shifts[step][1, layer]
             skip = lax.div(shift, LANES)
             fine = lax.rem(shift, LANES)
-            start = lax.rem(rows_ref[me, layer], SIDE) + wind_ref[step, 0, layer]
+            start = lax.rem(offsets[layer], SIDE) + shifts[step][0, layer]
             inside = lane < LANES - fine
             rolled = [
                 pltpu.roll(
@@ -319,30 +328,34 @@
                 field[rows, at + 2 * LANES : at + 3 * LANES] = low
                 field[rows, at + 4 * LANES : at + 5 * LANES] = high
 
-    first[...] = matmul(field[...], across_ref[...])
+    first = matmul(field[...], across_ref[...])
 
     wide_out = first.shape[1] // 2
-
-    for turn in range(steps * across):
-        rows = pl.ds(turn * SIDE, SIDE)
-        real_high, real_low = split(first[rows, 0:wide_out])
-        imag_high, imag_low = split(first[rows, wide_out : 2 * wide_out])
-        stacked = jnp.concatenate(
-            [real_high, imag_high, real_low, imag_low, real_high, imag_high], axis=0
-        )
-        spectrum = matmul(down_ref[...], stacked)
-        power = spectrum * spectrum
-        total = power[0:SIDE]
-        for k in range(1, 2 * BIN):
-            total = total + power[k * SIDE : (k + 1) * SIDE]
-        small = total[:, 0:LANES]
-        for k in range(1, BIN):
-            small = small + total[:, k * LANES : (k + 1) * LANES]
-        binned[rows, :] = small
-
+    wide = SIDE * SIDE
     lane8 = lax.broadcasted_iota(jnp.int32, (8, LANES), 1)
-    for big in range(binned.shape[0] // LANES):
-        flipped = binned[pl.ds(big * LANES, LANES), :].T
+    turns = steps * across
+    found = []
+    for big in range(0, turns, 8):
+        smalls = []
+        for turn in range(big, min(big + 8, turns)):
+            rows = pl.ds(turn * SIDE, SIDE)
+            real_high, real_low = split(first[turn * SIDE : (turn + 1) * SIDE, 0:wide_out])
+            imag_high, imag_low = split(first[turn * SIDE : (turn + 1) * SIDE, wide_out : 2 * wide_out])
+            stacked = jnp.concatenate(
+                [real_high, imag_high, real_low, imag_low, real_high, imag_high], axis=0
+            )
+            spectrum = matmul(down_ref[...], stacked)
+            power = spectrum * spectrum
+            total = power[0:SIDE]
+            for k in range(1, 2 * BIN):
+                total = total + power[k * SIDE : (k + 1) * SIDE]
+            small = total[:, 0:LANES]
+            for k in range(1, BIN):
+                small = small + total[:, k * LANES : (k + 1) * LANES]
+            smalls.append(small)
+        while len(smalls) < 8:
+            smalls.append(jnp.ones((SIDE, LANES), F32))
+        flipped = jnp.concatenate(smalls, axis=0).T
         halves = []
         for half in range(2):
             regs = [flipped[(half * 8 + q) * 8 : (half * 8 + q + 1) * 8] for q in range(8)]
@@ -359,18 +372,13 @@
         image = jnp.concatenate(
             [jnp.concatenate([halves[0][g], halves[1][g]], axis=1) for g in range(8)], axis=0
         )
-        image = image / jnp.sum(image, axis=1, keepdims=True)
+        image = image * (1.0 / jnp.sum(image, axis=1, keepdims=True))
         high, low = split(image)
-        rows = pl.ds(big * 64, 64)
-        wide = SIDE * SIDE
-        images[rows, 0:wide] = high
-        images[rows, wide : 2 * wide] = low
-        images[rows, 2 * wide : 3 * wide] = high
-    out_ref[...] = matmul(images[...], table[...])[0 : out_ref.shape[0]]
+        found.append(jnp.concatenate([high, low, high], axis=1))
+    out_ref[...] = matmul(jnp.concatenate(found, axis=0), table[...])[0 : out_ref.shape[0]]
 
 
 def spots_call(stars, devices, total_tiles, foot_rows, foot_cols, wind, strips, amplitude, table):
-    smem = pl.BlockSpec(memory_space=pltpu.SMEM)
     vmem = pl.BlockSpec(memory_space=pltpu.VMEM)
     steps, layers = wind.shape[0], wind.shape[2]
     depth = strips.shape[1]
@@ -382,15 +390,12 @@
     return pl.pallas_call(
         functools.partial(spots_kernel, stars, devices, total_tiles),
         out_shape=jax.ShapeDtypeStruct((count, SIDE * SIDE), F32),
-        in_specs=[smem] * 3 + [vmem] * 5,
+        in_specs=[vmem] * 8,
         out_specs=vmem,
         scratch_shapes=[
             pltpu.VMEM((layers * THIRD, devices * depth, LANES), F32),
             pltpu.VMEM((layers * SPAN, 3 * SIDE, LANES), F32),
             pltpu.VMEM((count // 8 * SIDE, 6 * LANES), BF16),
-            pltpu.VMEM((count // 8 * SIDE, high.shape[1]), F32),
-            pltpu.VMEM((padded // 8 * SIDE, LANES), F32),
-            pltpu.VMEM((padded, 3 * SIDE * SIDE), BF16),
         ],
         compiler_params=pltpu.CompilerParams(vmem_limit_bytes=16 << 20),
         name="spots",
@@ -448,7 +453,7 @@
     sent = pl.pallas_call(
         functools.partial(spread_kernel, stars, devices, tiles),
         out_shape=block,
-        in_specs=[smem, smem, pl.BlockSpec(memory_space=pl.ANY)] + [vmem] * stars,
+        in_specs=[vmem, vmem, pl.BlockSpec(memory_space=pl.ANY)] + [vmem] * stars,
         out_specs=vmem,
         scratch_shapes=[pltpu.VMEM((layers * THIRD, 2 * QUART * SIDE, LANES), F32)],
         compiler_params=pltpu.CompilerParams(vmem_limit_bytes=4 << 20),
@@ -458,7 +463,7 @@
     chosen = pl.pallas_call(
         functools.partial(choose_kernel, devices),
         out_shape=block,
-        in_specs=[smem, vmem],
+        in_specs=[vmem, vmem],
         out_specs=vmem,
         compiler_params=pltpu.CompilerParams(vmem_limit_bytes=2 << 20),
         name="choose",

time: 43.1 us -> 41.6 us (0.965)
  Pallas kernels: 8.92 us -> 7.41 us
    pallas_call x1, Pallas kernels: 4.75 us -> 4.2 us  [spots_call(): pl.pallas_call(functools.partial(spots_kernel, stars, devices, total_tile...]
    pallas_call x1, Pallas kernels: 0.69 us -> 0.2 us  [shards(): pl.pallas_call(functools.partial(choose_kernel, devices), out_shape=block...]
    pallas_call x1, Pallas kernels: 1.05 us -> 0.58 us  [shards(): pl.pallas_call(functools.partial(spread_kernel, stars, devices, tiles), o...]
where the time goes in v5:
time: 41.6 us; the launch traced here: 41.4 us
  blocking collectives  32.5 us (78%)
  Pallas kernels  7.41 us (18%)
  between operations  0.72 us (2%)
  starting transfers between devices  0.53 us (1%)
    all_to_all x1, blocking collectives, shards(): held_rows = lax.all_to_all(sent, 'dev', 0, 0, tiled=True)  19 us
    all_to_all x1, blocking collectives, shards(): strips = lax.all_to_all(chosen, 'dev', 0, 0, tiled=True)  13.5 us
    pallas_call x1, Pallas kernels, spots_call(): pl.pallas_call(functools.partial(spots_kernel, stars, devices, total_tile...  4.2 us
    pallas_call x1, Pallas kernels, shards(): pl.pallas_call(functools.partial(crop_kernel, stars, devices), out_shape=...  2.07 us
  transfers between devices with their start and end apart: 1, of which 1 were waited for; matrix products, arithmetic and copies ran while one was open for 0% of the time, Pallas kernels for 1%

profile of v5, /device:TPU:0, one launch (start us, length us, event | category | flops | bytes accessed | tf_op | source)
XLA Modules:
  0.0 41.4 jit_solution(5082614248439422788)
XLA Ops:
  0.0 0.0 copy-start
  0.0 0.0 copy-start.3
  0.0 0.0 copy-start.4
  0.0 0.0 copy-start.5
  0.0 0.0 copy-start.2
  0.0 0.0 copy-start.6
  0.0 0.0 copy-start.1
  0.0 2.1 %crop.1 = (bf16[6,16,1536]{2,1,0:T(8,128)(2,1)S(1)}, bf16[6,16,1536]{2,1,0:T(8,128)(2,1)S(1)}) custom-call(s32[2,3]{1,0:T(2,128)} %bitcast.6, s32[2,3]{1,0:T(2,128)} %bitcast.10, bf16[3,32,16,4096]{3,2,1,0:T(8,128)(2,1)} %screens_ref.1), custom_call_target="tpu_custom_call" | custom-call | tf_op jit(solution)/shard_map/crop/pallas_call | solution.py:418
  2.1 0.5 %collective-permute-start = (bf16[6,16,1536]{2,1,0:T(8,128)(2,1)S(1)}, bf16[6,16,1536]{2,1,0:T(8,128)(2,1)S(1)}, u32[]{:S(2)}, u32[]{:S(2)}) collective-permute-start(bf16[6,16,1536]{2,1,0:T(8,128)(2,1)S(1)} %get-tuple-element.8), channel_id=1, source_target_pairs={{0,16},{16,0},{1,17},{17,1},{2,18},{18,2},{3,19},{19,3},{4,20},{20... | collective-permute-start | bytes 884744 | tf_op jit(solution)/shard_map/ppermute | solution.py:439
  3.3 0.0 copy-done.2
  3.3 0.3 table.1._
  3.7 0.2 collective-permute-done.rest_1_
  3.9 0.0 copy-done.4
  3.9 0.0 copy-done.5
  3.9 0.6 %spread.1 = bf16[16,8,1152]{2,1,0:T(8,128)(2,1)S(1)} custom-call(s32[2,3]{1,0:T(2,128)S(1)} %bitcast.7, s32[2,3]{1,0:T(2,128)S(1)} %bitcast.11, bf16[768,256]{1,0:T(8,128)(2,1)S(1)} %table.1._, bf16[6,16,1536]{2,1,0:T(8,128)(2,1)S(1)} %get-tuple-element.7.rest_0_, bf16[6,16,1536]{2,1,0:T(8,128)(2,1)S(1)} %collective-permute-done.rest_1_), custom_call_target="tpu_custom_call" | custom-call | tf_op jit(solution)/shard_map/spread/pallas_call | solution.py:453
  4.5 19.0 %all_to_all.10.in_ref = bf16[16,8,1152]{2,1,0:T(8,128)(2,1)S(1)} all-to-all(bf16[16,8,1152]{2,1,0:T(8,128)(2,1)S(1)} %spread.1), channel_id=1, replica_groups=mesh['star'=2,'dev'=16] {'dev'}, dimensions={0} | all-to-all | bytes 589824 | tf_op jit(solution)/shard_map/all_to_all | solution.py:462
  23.5 0.2 choose.1
  23.7 13.5 %all_to_all.11.in_ref = bf16[16,8,1152]{2,1,0:T(8,128)(2,1)S(1)} all-to-all(bf16[16,8,1152]{2,1,0:T(8,128)(2,1)S(1)} %choose.1), channel_id=1, replica_groups=mesh['star'=2,'dev'=16] {'dev'}, dimensions={0} | all-to-all | bytes 589824 | tf_op jit(solution)/shard_map/all_to_all | solution.py:471
  37.1 0.0 copy-done
  37.2 0.0 copy-done.3
  37.2 0.0 copy-done.6
  37.2 0.0 copy-done.1
  37.2 4.2 %spots.1 = f32[240,256]{1,0:T(8,128)} custom-call(s32[2,3]{1,0:T(2,128)S(1)} %bitcast.9, s32[2,3]{1,0:T(2,128)S(1)} %bitcast.12, s32[3,2,3]{2,1,0:T(2,128)S(1)} %bitcast.13, bf16[16,8,1152]{2,1,0:T(8,128)(2,1)S(1)} %all_to_all.11.in_ref, f32[16,1280]{1,0:T(8,128)S(1)} %copy-done.1, bf16[768,256]{1,0:T(8,128)(2,1)S(1)} %table.1._, ...), custom_call_target="tpu_custom_call" | custom-call | tf_op jit(solution)/shard_map/spots/pallas_call | solution.py:390
Async XLA Ops:
  0.0 37.2 %copy-start = (bf16[768,1024]{1,0:T(8,128)(2,1)S(1)}, bf16[768,1024]{1,0:T(8,128)(2,1)}, u32[]{:S(2)}) copy-start(bf16[768,1024]{1,0:T(8,128)(2,1)} %constant.4.clone.across_ref) | copy-start | bytes 4718596
  0.0 37.2 %copy-start.3 = (bf16[128,96]{1,0:T(8,128)(2,1)S(1)}, bf16[128,96]{1,0:T(8,128)(2,1)}, u32[]{:S(2)}) copy-start(bf16[128,96]{1,0:T(8,128)(2,1)} %constant.5.clone.down_ref) | copy-start | bytes 73732
  0.0 3.9 %copy-start.4 = (s32[3,2]{0,1:T(2,128)S(1)}, s32[3,2]{0,1:T(2,128)}, u32[]{:S(2)}) copy-start(s32[3,2]{0,1:T(2,128)} %param.10) | copy-start | bytes 76
  0.0 3.9 %copy-start.5 = (s32[3,2]{0,1:T(2,128)S(1)}, s32[3,2]{0,1:T(2,128)}, u32[]{:S(2)}) copy-start(s32[3,2]{0,1:T(2,128)} %param.11) | copy-start | bytes 76
  0.0 3.3 %copy-start.2 = (f32[6,16,16]{2,1,0:T(8,128)S(1)}, f32[6,16,16]{2,1,0:T(8,128)}, u32[]{:S(2)}) copy-start(f32[6,16,16]{2,1,0:T(8,128)} %refs_ref.1) | copy-start | bytes 18436
  0.0 37.1 %copy-start.6 = (s32[3,3,2]{1,2,0:T(2,128)S(1)}, s32[3,3,2]{1,2,0:T(2,128)}, u32[]{:S(2)}) copy-start(s32[3,3,2]{1,2,0:T(2,128)} %param.12) | copy-start | bytes 220
  0.0 37.1 %copy-start.1 = (f32[16,1280]{1,0:T(8,128)S(1)}, f32[16,1280]{1,0:T(8,128)}, u32[]{:S(2)}) copy-start(f32[16,1280]{1,0:T(8,128)} %amp_ref.1) | copy-start | bytes 245764
  2.1 1.7 %collective-permute-start = (bf16[6,16,1536]{2,1,0:T(8,128)(2,1)S(1)}, bf16[6,16,1536]{2,1,0:T(8,128)(2,1)S(1)}, u32[]{:S(2)}, u32[]{:S(2)}) collective-permute-start(bf16[6,16,1536]{2,1,0:T(8,128)(2,1)S(1)} %get-tuple-element.8), channel_id=1, source_target_pairs={{0,16},{16,0},{1,17},{17,1},{2,18},{18,2},{3,19},{19,3},{4,20},{20... | collective-permute-start | bytes 884744 | tf_op jit(solution)/shard_map/ppermute | solution.py:439

commit v6 on v5

--- a/solution.py
+++ b/solution.py
@@ -15,6 +15,7 @@
 SPAN = 12
 QUART = 4
 THIRD = SPAN // QUART
+GROUP = 8
 
 F32 = jnp.float32
 BF16 = jnp.bfloat16
@@ -123,8 +124,6 @@
     parts, out_ref, turned = rest[:stars], rest[stars], rest[stars + 1]
     layers = parts[0].shape[0] // 2
     held = parts[0].shape[2] // LANES
-    groups = devices // SIDE
-    sub = QUART // groups
     me = lax.axis_index("star")
     place = lax.axis_index("dev")
     row = lax.broadcasted_iota(jnp.int32, (SIDE, LANES), 0)
@@ -132,8 +131,7 @@
     for layer in range(layers):
         strip, part, tile = place_of_own(offsets[layer], lefts[layer], stars * tiles)
         behind = lax.rem(place + (1 << 20) * devices - strip, devices)
-        bound = jnp.where(behind == 0, part, 0)
-        wraps = row < bound
+        wraps = row < jnp.where(behind == 0, SIDE, jnp.where(behind == 1, part, 0))
         for a in range(QUART):
             for b in range(THIRD):
                 spot = tile + (THIRD * a + b)
@@ -152,41 +150,49 @@
                         else:
                             value = jnp.where(panel == sender, seen, value)
                     pair.append(value)
-                first = jnp.where(wraps, pair[1], pair[0])
-                at = (a // sub) * 2 * sub + a % sub
-                turned[layer * THIRD + b, pl.ds(at * SIDE, SIDE), :] = first
-                turned[layer * THIRD + b, pl.ds((at + sub) * SIDE, SIDE), :] = pair[1]
-    for group in range(groups):
-        for r in range(SIDE):
+                turned[0, layer * THIRD + b, pl.ds(a * SIDE, SIDE), :] = pair[0]
+                turned[1, layer * THIRD + b, pl.ds(a * SIDE, SIDE), :] = jnp.where(
+                    wraps, pair[1], pair[0]
+                )
+    last = devices // GROUP - 1
+    for x in range(GROUP):
+        for kind in range(2):
             pieces = [
-                turned[unit, pl.ds(group * 2 * sub * SIDE + r, 2 * sub, stride=SIDE), :]
+                turned[kind, unit, pl.ds(x, 2 * QUART, stride=GROUP), :]
                 for unit in range(layers * THIRD)
             ]
-            out_ref[group * SIDE + r] = jnp.concatenate(pieces, axis=1).astype(BF16)
+            block = jnp.concatenate(pieces, axis=1).astype(BF16)
+            if kind == 1:
+                out_ref[last * GROUP + x] = block
+            else:
+                for group in range(last):
+                    out_ref[group * GROUP + x] = block
 
 
 def choose_kernel(devices, rows_ref, in_ref, out_ref):
     layers = rows_ref.shape[1]
     width = in_ref.shape[2] // layers
-    half = in_ref.shape[1] // 2
     me = lax.axis_index("star")
-    mine = lax.rem(lax.axis_index("dev"), SIDE)
-    upper = lax.broadcasted_iota(jnp.int32, (2 * half, width), 0) < half
+    place = lax.axis_index("dev")
+    mine = lax.rem(place, GROUP)
+    first = place - mine
+    even = lax.broadcasted_iota(jnp.int32, (2 * QUART, width), 0) % 2 == 0
     offsets = own_row(rows_ref, me)
     for layer in range(layers):
         offset = offsets[layer]
-        base = lax.div(offset, SIDE) + (mine < lax.rem(offset, SIDE)).astype(jnp.int32)
+        part = lax.rem(offset, SIDE)
+        strip = lax.div(offset, SIDE) + first
+        base = [strip + (mine + GROUP * u < part).astype(jnp.int32) for u in range(2)]
         lanes = slice(layer * width, (layer + 1) * width)
-        now = in_ref[lax.rem(base, devices), :, lanes].astype(F32)
-        last = now
-        for j in range(devices):
-            if j < devices - 1:
-                after = in_ref[lax.rem(base + j + 1, devices), :, lanes].astype(F32)
-                low = pltpu.roll(after, half, axis=0)
-            else:
-                after, low = None, last
-            out_ref[j, :, lanes] = jnp.where(upper, now, low).astype(BF16)
-            now = after
+        for j in range(GROUP + 1):
+            one, two = (
+                in_ref[lax.rem(base[u] + j, devices), :, lanes].astype(F32) for u in range(2)
+            )
+            item = jnp.where(even, one, two).astype(BF16)
+            if j < GROUP:
+                out_ref[j, pl.ds(0, 2 * QUART), lanes] = item
+            if j > 0:
+                out_ref[j - 1, pl.ds(2 * QUART, 2 * QUART), lanes] = item
 
 
 def sin_cos(value):
@@ -270,31 +276,31 @@
 ):
     steps, layers = wind_ref.shape[0], wind_ref.shape[2]
     across = amp_ref.shape[1] // LANES
-    groups = devices // SIDE
-    sub = QUART // groups
     me = lax.axis_index("star")
     row = lax.broadcasted_iota(jnp.int32, (SIDE, LANES), 0)
     lane = lax.broadcasted_iota(jnp.int32, (SIDE, LANES), 1)
     offsets, lefts = own_row(rows_ref, me), own_row(cols_ref, me)
     shifts = [wind_ref[step] for step in range(steps)]
 
-    for x in range(devices):
+    depth = in_ref.shape[1]
+    for x in range(GROUP):
         seen = in_ref[x].astype(F32)
         for unit in range(layers * THIRD):
-            turned[unit, pl.ds(x * 2 * sub, 2 * sub), :] = seen[:, unit * LANES : (unit + 1) * LANES]
+            turned[unit, pl.ds(x * depth, depth), :] = seen[:, unit * LANES : (unit + 1) * LANES]
     for layer in range(layers):
         part = lax.rem(offsets[layer], SIDE)
-        early = row < part
         for a in range(QUART):
             for b in range(THIRD):
-                at = (a // sub) * SIDE * 2 * sub + a % sub
                 unit = layer * THIRD + b
-                one = turned[unit, pl.ds(at, SIDE, stride=2 * sub), :]
-                two = turned[unit, pl.ds(at + sub, SIDE, stride=2 * sub), :]
                 slot = layer * SPAN + THIRD * a + b
-                window[slot, pl.ds(0, SIDE), :] = one
-                window[slot, pl.ds(SIDE, SIDE), :] = jnp.where(early, one, two)
-                window[slot, pl.ds(2 * SIDE, SIDE), :] = two
+                for u in range(2):
+                    early = row[0:GROUP] + GROUP * u < part
+                    one, two = (
+                        turned[unit, pl.ds(e * 2 * QUART + 2 * a + u, GROUP, stride=depth), :]
+                        for e in range(2)
+                    )
+                    for turn, value in enumerate((one, jnp.where(early, one, two), two)):
+                        window[slot, pl.ds(turn * SIDE + u * GROUP, GROUP), :] = value
 
     for step in range(steps):
         phase = [None] * across
@@ -393,7 +399,7 @@
         in_specs=[vmem] * 8,
         out_specs=vmem,
         scratch_shapes=[
-            pltpu.VMEM((layers * THIRD, devices * depth, LANES), F32),
+            pltpu.VMEM((layers * THIRD, GROUP * depth, LANES), F32),
             pltpu.VMEM((layers * SPAN, 3 * SIDE, LANES), F32),
             pltpu.VMEM((count // 8 * SIDE, 6 * LANES), BF16),
         ],
@@ -438,9 +444,8 @@
         parts.append(
             lax.ppermute(crops[turn], "star", [(i, (i + turn) % stars) for i in range(stars)])
         )
-    groups = devices // SIDE
-    depth = 2 * QUART // groups
-    block = jax.ShapeDtypeStruct((devices, depth, layers * THIRD * LANES), BF16)
+    block = jax.ShapeDtypeStruct((devices, 2 * QUART, layers * THIRD * LANES), BF16)
+    groups = [[g + x for x in range(GROUP)] for g in range(0, devices, GROUP)]
     wide = SIDE * SIDE
     table = pl.pallas_call(
         table_kernel,
@@ -455,20 +460,20 @@
         out_shape=block,
         in_specs=[vmem, vmem, pl.BlockSpec(memory_space=pl.ANY)] + [vmem] * stars,
         out_specs=vmem,
-        scratch_shapes=[pltpu.VMEM((layers * THIRD, 2 * QUART * SIDE, LANES), F32)],
+        scratch_shapes=[pltpu.VMEM((2, layers * THIRD, QUART * SIDE, LANES), F32)],
         compiler_params=pltpu.CompilerParams(vmem_limit_bytes=4 << 20),
         name="spread",
     )(foot_rows, foot_cols, table, *parts)
     held_rows = lax.all_to_all(sent, "dev", 0, 0, tiled=True)
     chosen = pl.pallas_call(
         functools.partial(choose_kernel, devices),
-        out_shape=block,
+        out_shape=jax.ShapeDtypeStruct((GROUP, 4 * QUART, block.shape[2]), BF16),
         in_specs=[vmem, vmem],
         out_specs=vmem,
         compiler_params=pltpu.CompilerParams(vmem_limit_bytes=2 << 20),
         name="choose",
     )(foot_rows, held_rows)
-    strips = lax.all_to_all(chosen, "dev", 0, 0, tiled=True)
+    strips = lax.all_to_all(chosen, "dev", 0, 0, axis_index_groups=groups, tiled=True)
     found = spots_call(
         stars, devices, stars * tiles, foot_rows, foot_cols, wind, strips, amplitude, table
     )

time: 41.6 us -> 37.6 us (0.904)
  blocking collectives: 32.5 us -> 28.5 us
    all_to_all x1, blocking collectives: 13.5 us -> 9.48 us  [shards(): lax.all_to_all(chosen, 'dev', 0, 0, axis_index_groups=groups, tiled=True)]
where the time goes in v6:
time: 37.6 us; the launch traced here: 37.4 us
  blocking collectives  28.5 us (76%)
  Pallas kernels  7.42 us (20%)
  between operations  0.72 us (2%)
  starting transfers between devices  0.53 us (1%)
    all_to_all x1, blocking collectives, shards(): held_rows = lax.all_to_all(sent, 'dev', 0, 0, tiled=True)  19 us
    all_to_all x1, blocking collectives, shards(): lax.all_to_all(chosen, 'dev', 0, 0, axis_index_groups=groups, tiled=True)  9.48 us
    pallas_call x1, Pallas kernels, spots_call(): pl.pallas_call(functools.partial(spots_kernel, stars, devices, total_tile...  4.28 us
    pallas_call x1, Pallas kernels, shards(): pl.pallas_call(functools.partial(crop_kernel, stars, devices), out_shape=...  2.07 us
  transfers between devices with their start and end apart: 1, of which 1 were waited for; matrix products, arithmetic and copies ran while one was open for 0% of the time, Pallas kernels for 1%

profile of v6, /device:TPU:0, one launch (start us, length us, event | category | flops | bytes accessed | tf_op | source)
XLA Modules:
  0.0 37.4 jit_solution(710315762719477889)
XLA Ops:
  0.0 0.0 copy-start
  0.0 0.0 copy-start.3
  0.0 0.0 copy-start.4
  0.0 0.0 copy-start.5
  0.0 0.0 copy-start.2
  0.0 0.0 copy-start.6
  0.0 0.0 copy-start.1
  0.0 2.1 %crop.1 = (bf16[6,16,1536]{2,1,0:T(8,128)(2,1)S(1)}, bf16[6,16,1536]{2,1,0:T(8,128)(2,1)S(1)}) custom-call(s32[2,3]{1,0:T(2,128)} %bitcast.6, s32[2,3]{1,0:T(2,128)} %bitcast.10, bf16[3,32,16,4096]{3,2,1,0:T(8,128)(2,1)} %screens_ref.1), custom_call_target="tpu_custom_call" | custom-call | tf_op jit(solution)/shard_map/crop/pallas_call | solution.py:424
  2.1 0.5 %collective-permute-start = (bf16[6,16,1536]{2,1,0:T(8,128)(2,1)S(1)}, bf16[6,16,1536]{2,1,0:T(8,128)(2,1)S(1)}, u32[]{:S(2)}, u32[]{:S(2)}) collective-permute-start(bf16[6,16,1536]{2,1,0:T(8,128)(2,1)S(1)} %get-tuple-element.8), channel_id=1, source_target_pairs={{0,16},{16,0},{1,17},{17,1},{2,18},{18,2},{3,19},{19,3},{4,20},{20... | collective-permute-start | bytes 884744 | tf_op jit(solution)/shard_map/ppermute | solution.py:445
  3.3 0.0 copy-done.2
  3.3 0.3 table.1._
  3.7 0.2 collective-permute-done.rest_1_
  3.9 0.0 copy-done.4
  3.9 0.0 copy-done.5
  3.9 0.5 %spread.1 = bf16[16,8,1152]{2,1,0:T(8,128)(2,1)S(1)} custom-call(s32[2,3]{1,0:T(2,128)S(1)} %bitcast.7, s32[2,3]{1,0:T(2,128)S(1)} %bitcast.11, bf16[768,256]{1,0:T(8,128)(2,1)S(1)} %table.1._, bf16[6,16,1536]{2,1,0:T(8,128)(2,1)S(1)} %get-tuple-element.7.rest_0_, bf16[6,16,1536]{2,1,0:T(8,128)(2,1)S(1)} %collective-permute-done.rest_1_), custom_call_target="tpu_custom_call" | custom-call | tf_op jit(solution)/shard_map/spread/pallas_call | solution.py:458
  4.4 19.0 %all_to_all.10.in_ref = bf16[16,8,1152]{2,1,0:T(8,128)(2,1)S(1)} all-to-all(bf16[16,8,1152]{2,1,0:T(8,128)(2,1)S(1)} %spread.1), channel_id=1, replica_groups=mesh['star'=2,'dev'=16] {'dev'}, dimensions={0} | all-to-all | bytes 589824 | tf_op jit(solution)/shard_map/all_to_all | solution.py:467
  23.4 0.2 choose.1
  23.6 9.5 %all_to_all.11.in_ref = bf16[8,16,1152]{2,1,0:T(8,128)(2,1)S(1)} all-to-all(bf16[8,16,1152]{2,1,0:T(8,128)(2,1)S(1)} %choose.1), channel_id=1, replica_groups={{0,1,2,3,4,5,6,7},{8,9,10,11,12,13,14,15},{16,17,18,19,20,21,22,23},{24..., dimensions={0} | all-to-all | bytes 589824 | tf_op jit(solution)/shard_map/all_to_all | solution.py:476
  33.1 0.0 copy-done
  33.1 0.0 copy-done.3
  33.1 0.0 copy-done.6
  33.1 0.0 copy-done.1
  33.1 4.3 %spots.1 = f32[240,256]{1,0:T(8,128)} custom-call(s32[2,3]{1,0:T(2,128)S(1)} %bitcast.9, s32[2,3]{1,0:T(2,128)S(1)} %bitcast.12, s32[3,2,3]{2,1,0:T(2,128)S(1)} %bitcast.13, bf16[8,16,1152]{2,1,0:T(8,128)(2,1)S(1)} %all_to_all.11.in_ref, f32[16,1280]{1,0:T(8,128)S(1)} %copy-done.1, bf16[768,256]{1,0:T(8,128)(2,1)S(1)} %table.1._, ...), custom_call_target="tpu_custom_call" | custom-call | tf_op jit(solution)/shard_map/spots/pallas_call | solution.py:396
Async XLA Ops:
  0.0 33.1 %copy-start = (bf16[768,1024]{1,0:T(8,128)(2,1)S(1)}, bf16[768,1024]{1,0:T(8,128)(2,1)}, u32[]{:S(2)}) copy-start(bf16[768,1024]{1,0:T(8,128)(2,1)} %constant.4.clone.across_ref) | copy-start | bytes 4718596
  0.0 33.1 %copy-start.3 = (bf16[128,96]{1,0:T(8,128)(2,1)S(1)}, bf16[128,96]{1,0:T(8,128)(2,1)}, u32[]{:S(2)}) copy-start(bf16[128,96]{1,0:T(8,128)(2,1)} %constant.5.clone.down_ref) | copy-start | bytes 73732
  0.0 3.9 %copy-start.4 = (s32[3,2]{0,1:T(2,128)S(1)}, s32[3,2]{0,1:T(2,128)}, u32[]{:S(2)}) copy-start(s32[3,2]{0,1:T(2,128)} %param.10) | copy-start | bytes 76
  0.0 3.9 %copy-start.5 = (s32[3,2]{0,1:T(2,128)S(1)}, s32[3,2]{0,1:T(2,128)}, u32[]{:S(2)}) copy-start(s32[3,2]{0,1:T(2,128)} %param.11) | copy-start | bytes 76
  0.0 3.3 %copy-start.2 = (f32[6,16,16]{2,1,0:T(8,128)S(1)}, f32[6,16,16]{2,1,0:T(8,128)}, u32[]{:S(2)}) copy-start(f32[6,16,16]{2,1,0:T(8,128)} %refs_ref.1) | copy-start | bytes 18436
  0.0 33.1 %copy-start.6 = (s32[3,3,2]{1,2,0:T(2,128)S(1)}, s32[3,3,2]{1,2,0:T(2,128)}, u32[]{:S(2)}) copy-start(s32[3,3,2]{1,2,0:T(2,128)} %param.12) | copy-start | bytes 220
  0.0 33.1 %copy-start.1 = (f32[16,1280]{1,0:T(8,128)S(1)}, f32[16,1280]{1,0:T(8,128)}, u32[]{:S(2)}) copy-start(f32[16,1280]{1,0:T(8,128)} %amp_ref.1) | copy-start | bytes 245764
  2.1 1.7 %collective-permute-start = (bf16[6,16,1536]{2,1,0:T(8,128)(2,1)S(1)}, bf16[6,16,1536]{2,1,0:T(8,128)(2,1)S(1)}, u32[]{:S(2)}, u32[]{:S(2)}) collective-permute-start(bf16[6,16,1536]{2,1,0:T(8,128)(2,1)S(1)} %get-tuple-element.8), channel_id=1, source_target_pairs={{0,16},{16,0},{1,17},{17,1},{2,18},{18,2},{3,19},{19,3},{4,20},{20... | collective-permute-start | bytes 884744 | tf_op jit(solution)/shard_map/ppermute | solution.py:445

commit v7 on v6

--- a/solution.py
+++ b/solution.py
@@ -150,23 +150,21 @@
                         else:
                             value = jnp.where(panel == sender, seen, value)
                     pair.append(value)
-                turned[0, layer * THIRD + b, pl.ds(a * SIDE, SIDE), :] = pair[0]
-                turned[1, layer * THIRD + b, pl.ds(a * SIDE, SIDE), :] = jnp.where(
-                    wraps, pair[1], pair[0]
-                )
+                rows = pl.ds(a, SIDE, stride=QUART)
+                turned[0, layer * THIRD + b, rows, :] = pair[0]
+                turned[1, layer * THIRD + b, rows, :] = jnp.where(wraps, pair[1], pair[0])
+    half = GROUP // 2
     last = devices // GROUP - 1
-    for x in range(GROUP):
+    for m in range(half):
         for kind in range(2):
-            pieces = [
-                turned[kind, unit, pl.ds(x, 2 * QUART, stride=GROUP), :]
-                for unit in range(layers * THIRD)
-            ]
+            rows = slice(m * SIDE, (m + 1) * SIDE)
+            pieces = [turned[kind, unit, rows, :] for unit in range(layers * THIRD)]
             block = jnp.concatenate(pieces, axis=1).astype(BF16)
             if kind == 1:
-                out_ref[last * GROUP + x] = block
+                out_ref[last * half + m] = block
             else:
                 for group in range(last):
-                    out_ref[group * GROUP + x] = block
+                    out_ref[group * half + m] = block
 
 
 def choose_kernel(devices, rows_ref, in_ref, out_ref):
@@ -174,25 +172,26 @@
     width = in_ref.shape[2] // layers
     me = lax.axis_index("star")
     place = lax.axis_index("dev")
-    mine = lax.rem(place, GROUP)
-    first = place - mine
-    even = lax.broadcasted_iota(jnp.int32, (2 * QUART, width), 0) % 2 == 0
+    first = place - lax.rem(place, GROUP)
+    odd = lax.rem(place, 2)
+    m = lax.div(place - first, 2)
+    row = lax.broadcasted_iota(jnp.int32, (SIDE, width), 0)
+    residue = m * QUART + lax.div(row, QUART)
     offsets = own_row(rows_ref, me)
     for layer in range(layers):
         offset = offsets[layer]
-        part = lax.rem(offset, SIDE)
-        strip = lax.div(offset, SIDE) + first
-        base = [strip + (mine + GROUP * u < part).astype(jnp.int32) for u in range(2)]
+        early = residue < lax.rem(offset, SIDE)
         lanes = slice(layer * width, (layer + 1) * width)
-        for j in range(GROUP + 1):
-            one, two = (
-                in_ref[lax.rem(base[u] + j, devices), :, lanes].astype(F32) for u in range(2)
-            )
-            item = jnp.where(even, one, two).astype(BF16)
-            if j < GROUP:
-                out_ref[j, pl.ds(0, 2 * QUART), lanes] = item
-            if j > 0:
-                out_ref[j - 1, pl.ds(2 * QUART, 2 * QUART), lanes] = item
+        for j in range(GROUP):
+            start = lax.div(offset, SIDE) + first + j
+            step = lax.rem(start + odd, 2)
+            late_from = lax.div(lax.rem(start + step, devices), 2)
+            early_from = lax.div(lax.rem(start + 2 - step, devices), 2)
+            out_ref[j, :, lanes] = jnp.where(
+                early,
+                in_ref[early_from, :, lanes].astype(F32),
+                in_ref[late_from, :, lanes].astype(F32),
+            ).astype(BF16)
 
 
 def sin_cos(value):
@@ -277,30 +276,29 @@
     steps, layers = wind_ref.shape[0], wind_ref.shape[2]
     across = amp_ref.shape[1] // LANES
     me = lax.axis_index("star")
-    row = lax.broadcasted_iota(jnp.int32, (SIDE, LANES), 0)
+    place = lax.axis_index("dev")
     lane = lax.broadcasted_iota(jnp.int32, (SIDE, LANES), 1)
     offsets, lefts = own_row(rows_ref, me), own_row(cols_ref, me)
     shifts = [wind_ref[step] for step in range(steps)]
 
-    depth = in_ref.shape[1]
+    half = GROUP // 2
     for x in range(GROUP):
         seen = in_ref[x].astype(F32)
+        at = (x % 2) * half * SIDE + x // 2 * SIDE
         for unit in range(layers * THIRD):
-            turned[unit, pl.ds(x * depth, depth), :] = seen[:, unit * LANES : (unit + 1) * LANES]
+            turned[unit, pl.ds(at, SIDE), :] = seen[:, unit * LANES : (unit + 1) * LANES]
     for layer in range(layers):
-        part = lax.rem(offsets[layer], SIDE)
+        odd = lax.rem(lax.div(offsets[layer], SIDE) + place, 2)
         for a in range(QUART):
             for b in range(THIRD):
                 unit = layer * THIRD + b
                 slot = layer * SPAN + THIRD * a + b
-                for u in range(2):
-                    early = row[0:GROUP] + GROUP * u < part
-                    one, two = (
-                        turned[unit, pl.ds(e * 2 * QUART + 2 * a + u, GROUP, stride=depth), :]
-                        for e in range(2)
-                    )
-                    for turn, value in enumerate((one, jnp.where(early, one, two), two)):
-                        window[slot, pl.ds(turn * SIDE + u * GROUP, GROUP), :] = value
+                one, two = (
+                    turned[unit, pl.ds(parity * half * SIDE + a, SIDE, stride=QUART), :]
+                    for parity in (odd, 1 - odd)
+                )
+                for turn, value in enumerate((one, two, one)):
+                    window[slot, pl.ds(turn * SIDE, SIDE), :] = value
 
     for step in range(steps):
         phase = [None] * across
@@ -444,7 +442,8 @@
         parts.append(
             lax.ppermute(crops[turn], "star", [(i, (i + turn) % stars) for i in range(stars)])
         )
-    block = jax.ShapeDtypeStruct((devices, 2 * QUART, layers * THIRD * LANES), BF16)
+    block = jax.ShapeDtypeStruct((devices // 2, SIDE, layers * THIRD * LANES), BF16)
+    parities = [list(range(c, devices, 2)) for c in range(2)]
     groups = [[g + x for x in range(GROUP)] for g in range(0, devices, GROUP)]
     wide = SIDE * SIDE
     table = pl.pallas_call(
@@ -464,10 +463,10 @@
         compiler_params=pltpu.CompilerParams(vmem_limit_bytes=4 << 20),
         name="spread",
     )(foot_rows, foot_cols, table, *parts)
-    held_rows = lax.all_to_all(sent, "dev", 0, 0, tiled=True)
+    held_rows = lax.all_to_all(sent, "dev", 0, 0, axis_index_groups=parities, tiled=True)
     chosen = pl.pallas_call(
         functools.partial(choose_kernel, devices),
-        out_shape=jax.ShapeDtypeStruct((GROUP, 4 * QUART, block.shape[2]), BF16),
+        out_shape=jax.ShapeDtypeStruct((GROUP,) + block.shape[1:], BF16),
         in_specs=[vmem, vmem],
         out_specs=vmem,
         compiler_params=pltpu.CompilerParams(vmem_limit_bytes=2 << 20),

time: 37.6 us -> 36.5 us (0.971)
  blocking collectives: 28.5 us -> 27.4 us
    all_to_all x1, blocking collectives: 19 us -> 17.6 us  [shards(): lax.all_to_all(sent, 'dev', 0, 0, axis_index_groups=parities, tiled=True)]
where the time goes in v7:
time: 36.5 us; the launch traced here: 36.3 us
  blocking collectives  27.4 us (75%)
  Pallas kernels  7.36 us (20%)
  between operations  0.72 us (2%)
  starting transfers between devices  0.53 us (1%)
    all_to_all x1, blocking collectives, shards(): lax.all_to_all(sent, 'dev', 0, 0, axis_index_groups=parities, tiled=True)  17.6 us
    all_to_all x1, blocking collectives, shards(): lax.all_to_all(chosen, 'dev', 0, 0, axis_index_groups=groups, tiled=True)  9.8 us
    pallas_call x1, Pallas kernels, spots_call(): pl.pallas_call(functools.partial(spots_kernel, stars, devices, total_tile...  4.18 us
    pallas_call x1, Pallas kernels, shards(): pl.pallas_call(functools.partial(crop_kernel, stars, devices), out_shape=...  2.07 us
  transfers between devices with their start and end apart: 1, of which 1 were waited for; matrix products, arithmetic and copies ran while one was open for 0% of the time, Pallas kernels for 1%

profile of v7, /device:TPU:0, one launch (start us, length us, event | category | flops | bytes accessed | tf_op | source)
XLA Modules:
  0.0 36.3 jit_solution(9326774640837261240)
XLA Ops:
  0.0 0.0 copy-start
  0.0 0.0 copy-start.3
  0.0 0.0 copy-start.4
  0.0 0.0 copy-start.5
  0.0 0.0 copy-start.2
  0.0 0.0 copy-start.6
  0.0 0.0 copy-start.1
  0.0 2.1 %crop.1 = (bf16[6,16,1536]{2,1,0:T(8,128)(2,1)S(1)}, bf16[6,16,1536]{2,1,0:T(8,128)(2,1)S(1)}) custom-call(s32[2,3]{1,0:T(2,128)} %bitcast.6, s32[2,3]{1,0:T(2,128)} %bitcast.10, bf16[3,32,16,4096]{3,2,1,0:T(8,128)(2,1)} %screens_ref.1), custom_call_target="tpu_custom_call" | custom-call | tf_op jit(solution)/shard_map/crop/pallas_call | solution.py:422
  2.1 0.5 %collective-permute-start = (bf16[6,16,1536]{2,1,0:T(8,128)(2,1)S(1)}, bf16[6,16,1536]{2,1,0:T(8,128)(2,1)S(1)}, u32[]{:S(2)}, u32[]{:S(2)}) collective-permute-start(bf16[6,16,1536]{2,1,0:T(8,128)(2,1)S(1)} %get-tuple-element.8), channel_id=1, source_target_pairs={{0,16},{16,0},{1,17},{17,1},{2,18},{18,2},{3,19},{19,3},{4,20},{20... | collective-permute-start | bytes 884744 | tf_op jit(solution)/shard_map/ppermute | solution.py:443
  3.3 0.0 copy-done.2
  3.3 0.3 table.1._
  3.7 0.2 collective-permute-done.rest_1_
  3.9 0.0 copy-done.4
  3.9 0.0 copy-done.5
  3.9 0.5 %spread.1 = bf16[8,16,1152]{2,1,0:T(8,128)(2,1)S(1)} custom-call(s32[2,3]{1,0:T(2,128)S(1)} %bitcast.7, s32[2,3]{1,0:T(2,128)S(1)} %bitcast.11, bf16[768,256]{1,0:T(8,128)(2,1)S(1)} %table.1._, bf16[6,16,1536]{2,1,0:T(8,128)(2,1)S(1)} %get-tuple-element.7.rest_0_, bf16[6,16,1536]{2,1,0:T(8,128)(2,1)S(1)} %collective-permute-done.rest_1_), custom_call_target="tpu_custom_call" | custom-call | tf_op jit(solution)/shard_map/spread/pallas_call | solution.py:457
  4.3 17.6 %all_to_all.10.in_ref = bf16[8,16,1152]{2,1,0:T(8,128)(2,1)S(1)} all-to-all(bf16[8,16,1152]{2,1,0:T(8,128)(2,1)S(1)} %spread.1), channel_id=1, replica_groups={{0,2,4,6,8,10,12,14},{1,3,5,7,9,11,13,15},{16,18,20,22,24,26,28,30},{17..., dimensions={0} | all-to-all | bytes 589824 | tf_op jit(solution)/shard_map/all_to_all | solution.py:466
  22.0 0.3 choose.1
  22.3 9.8 %all_to_all.11.in_ref = bf16[8,16,1152]{2,1,0:T(8,128)(2,1)S(1)} all-to-all(bf16[8,16,1152]{2,1,0:T(8,128)(2,1)S(1)} %choose.1), channel_id=1, replica_groups={{0,1,2,3,4,5,6,7},{8,9,10,11,12,13,14,15},{16,17,18,19,20,21,22,23},{24..., dimensions={0} | all-to-all | bytes 589824 | tf_op jit(solution)/shard_map/all_to_all | solution.py:475
  32.1 0.0 copy-done
  32.1 0.0 copy-done.3
  32.1 0.0 copy-done.6
  32.1 0.0 copy-done.1
  32.1 4.2 %spots.1 = f32[240,256]{1,0:T(8,128)} custom-call(s32[2,3]{1,0:T(2,128)S(1)} %bitcast.9, s32[2,3]{1,0:T(2,128)S(1)} %bitcast.12, s32[3,2,3]{2,1,0:T(2,128)S(1)} %bitcast.13, bf16[8,16,1152]{2,1,0:T(8,128)(2,1)S(1)} %all_to_all.11.in_ref, f32[16,1280]{1,0:T(8,128)S(1)} %copy-done.1, bf16[768,256]{1,0:T(8,128)(2,1)S(1)} %table.1._, ...), custom_call_target="tpu_custom_call" | custom-call | tf_op jit(solution)/shard_map/spots/pallas_call | solution.py:394
Async XLA Ops:
  0.0 32.1 %copy-start = (bf16[768,1024]{1,0:T(8,128)(2,1)S(1)}, bf16[768,1024]{1,0:T(8,128)(2,1)}, u32[]{:S(2)}) copy-start(bf16[768,1024]{1,0:T(8,128)(2,1)} %constant.4.clone.across_ref) | copy-start | bytes 4718596
  0.0 32.1 %copy-start.3 = (bf16[128,96]{1,0:T(8,128)(2,1)S(1)}, bf16[128,96]{1,0:T(8,128)(2,1)}, u32[]{:S(2)}) copy-start(bf16[128,96]{1,0:T(8,128)(2,1)} %constant.5.clone.down_ref) | copy-start | bytes 73732
  0.0 3.9 %copy-start.4 = (s32[3,2]{0,1:T(2,128)S(1)}, s32[3,2]{0,1:T(2,128)}, u32[]{:S(2)}) copy-start(s32[3,2]{0,1:T(2,128)} %param.10) | copy-start | bytes 76
  0.0 3.9 %copy-start.5 = (s32[3,2]{0,1:T(2,128)S(1)}, s32[3,2]{0,1:T(2,128)}, u32[]{:S(2)}) copy-start(s32[3,2]{0,1:T(2,128)} %param.11) | copy-start | bytes 76
  0.0 3.3 %copy-start.2 = (f32[6,16,16]{2,1,0:T(8,128)S(1)}, f32[6,16,16]{2,1,0:T(8,128)}, u32[]{:S(2)}) copy-start(f32[6,16,16]{2,1,0:T(8,128)} %refs_ref.1) | copy-start | bytes 18436
  0.0 32.1 %copy-start.6 = (s32[3,3,2]{1,2,0:T(2,128)S(1)}, s32[3,3,2]{1,2,0:T(2,128)}, u32[]{:S(2)}) copy-start(s32[3,3,2]{1,2,0:T(2,128)} %param.12) | copy-start | bytes 220
  0.0 32.0 %copy-start.1 = (f32[16,1280]{1,0:T(8,128)S(1)}, f32[16,1280]{1,0:T(8,128)}, u32[]{:S(2)}) copy-start(f32[16,1280]{1,0:T(8,128)} %amp_ref.1) | copy-start | bytes 245764
  2.1 1.7 %collective-permute-start = (bf16[6,16,1536]{2,1,0:T(8,128)(2,1)S(1)}, bf16[6,16,1536]{2,1,0:T(8,128)(2,1)S(1)}, u32[]{:S(2)}, u32[]{:S(2)}) collective-permute-start(bf16[6,16,1536]{2,1,0:T(8,128)(2,1)S(1)} %get-tuple-element.8), channel_id=1, source_target_pairs={{0,16},{16,0},{1,17},{17,1},{2,18},{18,2},{3,19},{19,3},{4,20},{20... | collective-permute-start | bytes 884744 | tf_op jit(solution)/shard_map/ppermute | solution.py:443

commit v8 on v7

--- a/solution.py
+++ b/solution.py
@@ -13,8 +13,9 @@
 SIDE = 16
 LANES = 128
 SPAN = 12
-QUART = 4
-THIRD = SPAN // QUART
+FULL = 10
+HALF = FULL // 2
+TAIL = 32
 GROUP = 8
 
 F32 = jnp.float32
@@ -127,38 +128,58 @@
     me = lax.axis_index("star")
     place = lax.axis_index("dev")
     row = lax.broadcasted_iota(jnp.int32, (SIDE, LANES), 0)
+    lane = lax.broadcasted_iota(jnp.int32, (SIDE, LANES), 1)
+    tails = [None, None]
     offsets, lefts = own_row(rows_ref, me), own_row(cols_ref, me)
     for layer in range(layers):
         strip, part, tile = place_of_own(offsets[layer], lefts[layer], stars * tiles)
         behind = lax.rem(place + (1 << 20) * devices - strip, devices)
         wraps = row < jnp.where(behind == 0, SIDE, jnp.where(behind == 1, part, 0))
-        for a in range(QUART):
-            for b in range(THIRD):
-                spot = tile + (THIRD * a + b)
-                panel = lax.div(spot, tiles)
-                pair = []
-                for slot in range(2):
-                    value = None
-                    for turn in range(stars):
-                        sender = lax.rem(me + stars - turn, stars)
-                        start = first_tile(tile, sender, tiles, held)
-                        local = jnp.clip(spot - sender * tiles - start, 0, held - 1)
-                        lanes = pl.ds(pl.multiple_of(local * LANES, LANES), LANES)
-                        seen = parts[turn][2 * layer + slot, :, lanes].astype(F32)
-                        if value is None:
-                            value = seen
-                        else:
-                            value = jnp.where(panel == sender, seen, value)
-                    pair.append(value)
-                rows = pl.ds(a, SIDE, stride=QUART)
-                turned[0, layer * THIRD + b, rows, :] = pair[0]
-                turned[1, layer * THIRD + b, rows, :] = jnp.where(wraps, pair[1], pair[0])
+        shift = lefts[layer] - tile * LANES
+        skip, fine = lax.div(shift, LANES), lax.rem(shift, LANES)
+        inside = lane < LANES - fine
+        rolled = []
+        for t in range(FULL + 2):
+            spot = tile + skip + t
+            panel = lax.div(spot, tiles)
+            pair = []
+            for slot in range(2):
+                value = None
+                for turn in range(stars):
+                    sender = lax.rem(me + stars - turn, stars)
+                    start = first_tile(tile, sender, tiles, held)
+                    local = jnp.clip(spot - sender * tiles - start, 0, held - 1)
+                    lanes = pl.ds(pl.multiple_of(local * LANES, LANES), LANES)
+                    seen = parts[turn][2 * layer + slot, :, lanes].astype(F32)
+                    if value is None:
+                        value = seen
+                    else:
+                        value = jnp.where(panel == sender, seen, value)
+                pair.append(value)
+            mixed = jnp.where(wraps, pair[1], pair[0])
+            rolled.append(
+                [pltpu.roll(v, lax.rem(LANES - fine, LANES), axis=1) for v in (pair[0], mixed)]
+            )
+        for kind in range(2):
+            for t in range(FULL + 1):
+                value = jnp.where(inside, rolled[t][kind], rolled[t + 1][kind])
+                if t < FULL:
+                    rows = pl.ds(t // HALF, SIDE, stride=2)
+                    turned[kind, layer * HALF + t % HALF, rows, :] = value
+                elif layer == 0:
+                    tails[kind] = value
+                else:
+                    value = pltpu.roll(value, layer * TAIL, axis=1)
+                    tails[kind] = jnp.where(lane < layer * TAIL, tails[kind], value)
+    for kind in range(2):
+        for side in range(2):
+            turned[kind, layers * HALF, pl.ds(side, SIDE, stride=2), :] = tails[kind]
     half = GROUP // 2
     last = devices // GROUP - 1
     for m in range(half):
         for kind in range(2):
-            rows = slice(m * SIDE, (m + 1) * SIDE)
-            pieces = [turned[kind, unit, rows, :] for unit in range(layers * THIRD)]
+            rows = slice(m * 8, (m + 1) * 8)
+            pieces = [turned[kind, unit, rows, :] for unit in range(layers * HALF + 1)]
             block = jnp.concatenate(pieces, axis=1).astype(BF16)
             if kind == 1:
                 out_ref[last * half + m] = block
@@ -169,15 +190,18 @@
 
 def choose_kernel(devices, rows_ref, in_ref, out_ref):
     layers = rows_ref.shape[1]
-    width = in_ref.shape[2] // layers
+    width = HALF * LANES
     me = lax.axis_index("star")
     place = lax.axis_index("dev")
     first = place - lax.rem(place, GROUP)
     odd = lax.rem(place, 2)
     m = lax.div(place - first, 2)
-    row = lax.broadcasted_iota(jnp.int32, (SIDE, width), 0)
-    residue = m * QUART + lax.div(row, QUART)
+    row = lax.broadcasted_iota(jnp.int32, (8, width), 0)
+    lane = lax.broadcasted_iota(jnp.int32, (8, LANES), 1)
+    residue = m * 4 + lax.div(row, 2)
     offsets = own_row(rows_ref, me)
+    last = slice(layers * width, layers * width + LANES)
+    tails = [None] * GROUP
     for layer in range(layers):
         offset = offsets[layer]
         early = residue < lax.rem(offset, SIDE)
@@ -192,6 +216,14 @@
                 in_ref[early_from, :, lanes].astype(F32),
                 in_ref[late_from, :, lanes].astype(F32),
             ).astype(BF16)
+            tail = jnp.where(
+                early[:, 0:LANES],
+                in_ref[early_from, :, last].astype(F32),
+                in_ref[late_from, :, last].astype(F32),
+            )
+            tails[j] = tail if layer == 0 else jnp.where(lane < layer * TAIL, tails[j], tail)
+    for j in range(GROUP):
+        out_ref[j, :, last] = tails[j].astype(BF16)
 
 
 def sin_cos(value):
@@ -278,41 +310,38 @@
     me = lax.axis_index("star")
     place = lax.axis_index("dev")
     lane = lax.broadcasted_iota(jnp.int32, (SIDE, LANES), 1)
-    offsets, lefts = own_row(rows_ref, me), own_row(cols_ref, me)
+    offsets = own_row(rows_ref, me)
     shifts = [wind_ref[step] for step in range(steps)]
 
     half = GROUP // 2
     for x in range(GROUP):
         seen = in_ref[x].astype(F32)
-        at = (x % 2) * half * SIDE + x // 2 * SIDE
-        for unit in range(layers * THIRD):
-            turned[unit, pl.ds(at, SIDE), :] = seen[:, unit * LANES : (unit + 1) * LANES]
+        at = (x % 2) * half * 8 + x // 2 * 8
+        for unit in range(layers * HALF + 1):
+            turned[unit, pl.ds(at, 8), :] = seen[:, unit * LANES : (unit + 1) * LANES]
     for layer in range(layers):
         odd = lax.rem(lax.div(offsets[layer], SIDE) + place, 2)
-        for a in range(QUART):
-            for b in range(THIRD):
-                unit = layer * THIRD + b
-                slot = layer * SPAN + THIRD * a + b
-                one, two = (
-                    turned[unit, pl.ds(parity * half * SIDE + a, SIDE, stride=QUART), :]
-                    for parity in (odd, 1 - odd)
-                )
-                for turn, value in enumerate((one, two, one)):
-                    window[slot, pl.ds(turn * SIDE, SIDE), :] = value
+        for t in range(FULL + 1):
+            unit = layer * HALF + t % HALF if t < FULL else layers * HALF
+            at = t // HALF if t < FULL else 0
+            one, two = (
+                turned[unit, pl.ds(parity * half * 8 + at, SIDE, stride=2), :]
+                for parity in (odd, 1 - odd)
+            )
+            if t == FULL and layer > 0:
+                one, two = (pltpu.roll(v, LANES - layer * TAIL, axis=1) for v in (one, two))
+            for turn, value in enumerate((one, two, one)):
+                window[layer * (FULL + 1) + t, pl.ds(turn * SIDE, SIDE), :] = value
 
     for step in range(steps):
         phase = [None] * across
         for layer in range(layers):
-            left = lefts[layer]
-            tile = jnp.minimum(lax.div(left, LANES), total_tiles - SPAN)
-            shift = left - tile * LANES + shifts[step][1, layer]
-            skip = lax.div(shift, LANES)
-            fine = lax.rem(shift, LANES)
+            fine = shifts[step][1, layer]
             start = lax.rem(offsets[layer], SIDE) + shifts[step][0, layer]
             inside = lane < LANES - fine
             rolled = [
                 pltpu.roll(
-                    window[layer * SPAN + skip + t, pl.ds(start, SIDE), :],
+                    window[layer * (FULL + 1) + t, pl.ds(start, SIDE), :],
                     lax.rem(LANES - fine, LANES),
                     axis=1,
                 )
@@ -397,8 +426,8 @@
         in_specs=[vmem] * 8,
         out_specs=vmem,
         scratch_shapes=[
-            pltpu.VMEM((layers * THIRD, GROUP * depth, LANES), F32),
-            pltpu.VMEM((layers * SPAN, 3 * SIDE, LANES), F32),
+            pltpu.VMEM((layers * HALF + 1, GROUP * depth, LANES), F32),
+            pltpu.VMEM((layers * (FULL + 1), 3 * SIDE, LANES), F32),
             pltpu.VMEM((count // 8 * SIDE, 6 * LANES), BF16),
         ],
         compiler_params=pltpu.CompilerParams(vmem_limit_bytes=16 << 20),
@@ -442,7 +471,7 @@
         parts.append(
             lax.ppermute(crops[turn], "star", [(i, (i + turn) % stars) for i in range(stars)])
         )
-    block = jax.ShapeDtypeStruct((devices // 2, SIDE, layers * THIRD * LANES), BF16)
+    block = jax.ShapeDtypeStruct((devices // 2, 8, (layers * HALF + 1) * LANES), BF16)
     parities = [list(range(c, devices, 2)) for c in range(2)]
     groups = [[g + x for x in range(GROUP)] for g in range(0, devices, GROUP)]
     wide = SIDE * SIDE
@@ -459,7 +488,7 @@
         out_shape=block,
         in_specs=[vmem, vmem, pl.BlockSpec(memory_space=pl.ANY)] + [vmem] * stars,
         out_specs=vmem,
-        scratch_shapes=[pltpu.VMEM((2, layers * THIRD, QUART * SIDE, LANES), F32)],
+        scratch_shapes=[pltpu.VMEM((2, layers * HALF + 1, 2 * SIDE, LANES), F32)],
         compiler_params=pltpu.CompilerParams(vmem_limit_bytes=4 << 20),
         name="spread",
     )(foot_rows, foot_cols, table, *parts)

time: 36.5 us -> 35.4 us (0.970)
  blocking collectives: 27.4 us -> 26.3 us
    all_to_all x1, blocking collectives: 17.6 us -> 16.2 us  [shards(): lax.all_to_all(sent, 'dev', 0, 0, axis_index_groups=parities, tiled=True)]
where the time goes in v8:
time: 35.4 us; the launch traced here: 35.2 us
  blocking collectives  26.3 us (74%)
  Pallas kernels  7.44 us (21%)
  between operations  0.72 us (2%)
  starting transfers between devices  0.53 us (1%)
    all_to_all x1, blocking collectives, shards(): lax.all_to_all(sent, 'dev', 0, 0, axis_index_groups=parities, tiled=True)  16.2 us
    all_to_all x1, blocking collectives, shards(): lax.all_to_all(chosen, 'dev', 0, 0, axis_index_groups=groups, tiled=True)  10 us
    pallas_call x1, Pallas kernels, spots_call(): pl.pallas_call(functools.partial(spots_kernel, stars, devices, total_tile...  4.17 us
    pallas_call x1, Pallas kernels, shards(): pl.pallas_call(functools.partial(crop_kernel, stars, devices), out_shape=...  2.07 us
  transfers between devices with their start and end apart: 1, of which 1 were waited for; matrix products, arithmetic and copies ran while one was open for 0% of the time, Pallas kernels for 1%

profile of v8, /device:TPU:0, one launch (start us, length us, event | category | flops | bytes accessed | tf_op | source)
XLA Modules:
  0.0 35.2 jit_solution(15635914968028694915)
XLA Ops:
  0.0 0.0 copy-start
  0.0 0.0 copy-start.3
  0.0 0.0 copy-start.4
  0.0 0.0 copy-start.5
  0.0 0.0 copy-start.2
  0.0 0.0 copy-start.6
  0.0 0.0 copy-start.1
  0.0 2.1 %crop.1 = (bf16[6,16,1536]{2,1,0:T(8,128)(2,1)S(1)}, bf16[6,16,1536]{2,1,0:T(8,128)(2,1)S(1)}) custom-call(s32[2,3]{1,0:T(2,128)} %bitcast.6, s32[2,3]{1,0:T(2,128)} %bitcast.10, bf16[3,32,16,4096]{3,2,1,0:T(8,128)(2,1)} %screens_ref.1), custom_call_target="tpu_custom_call" | custom-call | tf_op jit(solution)/shard_map/crop/pallas_call | solution.py:451
  2.1 0.5 %collective-permute-start = (bf16[6,16,1536]{2,1,0:T(8,128)(2,1)S(1)}, bf16[6,16,1536]{2,1,0:T(8,128)(2,1)S(1)}, u32[]{:S(2)}, u32[]{:S(2)}) collective-permute-start(bf16[6,16,1536]{2,1,0:T(8,128)(2,1)S(1)} %get-tuple-element.8), channel_id=1, source_target_pairs={{0,16},{16,0},{1,17},{17,1},{2,18},{18,2},{3,19},{19,3},{4,20},{20... | collective-permute-start | bytes 884744 | tf_op jit(solution)/shard_map/ppermute | solution.py:472
  3.3 0.0 copy-done.2
  3.3 0.3 table.1._
  3.7 0.2 collective-permute-done.rest_1_
  3.9 0.0 copy-done.4
  3.9 0.0 copy-done.5
  3.9 0.6 %spread.1 = bf16[8,8,2048]{2,1,0:T(8,128)(2,1)S(1)} custom-call(s32[2,3]{1,0:T(2,128)S(1)} %bitcast.7, s32[2,3]{1,0:T(2,128)S(1)} %bitcast.11, bf16[768,256]{1,0:T(8,128)(2,1)S(1)} %table.1._, bf16[6,16,1536]{2,1,0:T(8,128)(2,1)S(1)} %get-tuple-element.7.rest_0_, bf16[6,16,1536]{2,1,0:T(8,128)(2,1)S(1)} %collective-permute-done.rest_1_), custom_call_target="tpu_custom_call" | custom-call | tf_op jit(solution)/shard_map/spread/pallas_call | solution.py:486
  4.4 16.2 %all_to_all.10.in_ref = bf16[8,8,2048]{2,1,0:T(8,128)(2,1)S(1)} all-to-all(bf16[8,8,2048]{2,1,0:T(8,128)(2,1)S(1)} %spread.1), channel_id=1, replica_groups={{0,2,4,6,8,10,12,14},{1,3,5,7,9,11,13,15},{16,18,20,22,24,26,28,30},{17..., dimensions={0} | all-to-all | bytes 524288 | tf_op jit(solution)/shard_map/all_to_all | solution.py:495
  20.6 0.3 choose.1
  20.9 10.0 %all_to_all.11.in_ref = bf16[8,8,2048]{2,1,0:T(8,128)(2,1)S(1)} all-to-all(bf16[8,8,2048]{2,1,0:T(8,128)(2,1)S(1)} %choose.1), channel_id=1, replica_groups={{0,1,2,3,4,5,6,7},{8,9,10,11,12,13,14,15},{16,17,18,19,20,21,22,23},{24..., dimensions={0} | all-to-all | bytes 524288 | tf_op jit(solution)/shard_map/all_to_all | solution.py:504
  31.0 0.0 copy-done
  31.0 0.0 copy-done.3
  31.0 0.0 copy-done.6
  31.0 0.0 copy-done.1
  31.0 4.2 %spots.1 = f32[240,256]{1,0:T(8,128)} custom-call(s32[2,3]{1,0:T(2,128)S(1)} %bitcast.9, s32[2,3]{1,0:T(2,128)S(1)} %bitcast.12, s32[3,2,3]{2,1,0:T(2,128)S(1)} %bitcast.13, bf16[8,8,2048]{2,1,0:T(8,128)(2,1)S(1)} %all_to_all.11.in_ref, f32[16,1280]{1,0:T(8,128)S(1)} %copy-done.1, bf16[768,256]{1,0:T(8,128)(2,1)S(1)} %table.1._, ...), custom_call_target="tpu_custom_call" | custom-call | tf_op jit(solution)/shard_map/spots/pallas_call | solution.py:423
Async XLA Ops:
  0.0 31.0 %copy-start = (bf16[768,1024]{1,0:T(8,128)(2,1)S(1)}, bf16[768,1024]{1,0:T(8,128)(2,1)}, u32[]{:S(2)}) copy-start(bf16[768,1024]{1,0:T(8,128)(2,1)} %constant.4.clone.across_ref) | copy-start | bytes 4718596
  0.0 31.0 %copy-start.3 = (bf16[128,96]{1,0:T(8,128)(2,1)S(1)}, bf16[128,96]{1,0:T(8,128)(2,1)}, u32[]{:S(2)}) copy-start(bf16[128,96]{1,0:T(8,128)(2,1)} %constant.5.clone.down_ref) | copy-start | bytes 73732
  0.0 3.9 %copy-start.4 = (s32[3,2]{0,1:T(2,128)S(1)}, s32[3,2]{0,1:T(2,128)}, u32[]{:S(2)}) copy-start(s32[3,2]{0,1:T(2,128)} %param.10) | copy-start | bytes 76
  0.0 3.9 %copy-start.5 = (s32[3,2]{0,1:T(2,128)S(1)}, s32[3,2]{0,1:T(2,128)}, u32[]{:S(2)}) copy-start(s32[3,2]{0,1:T(2,128)} %param.11) | copy-start | bytes 76
  0.0 3.3 %copy-start.2 = (f32[6,16,16]{2,1,0:T(8,128)S(1)}, f32[6,16,16]{2,1,0:T(8,128)}, u32[]{:S(2)}) copy-start(f32[6,16,16]{2,1,0:T(8,128)} %refs_ref.1) | copy-start | bytes 18436
  0.0 31.0 %copy-start.6 = (s32[3,3,2]{1,2,0:T(2,128)S(1)}, s32[3,3,2]{1,2,0:T(2,128)}, u32[]{:S(2)}) copy-start(s32[3,3,2]{1,2,0:T(2,128)} %param.12) | copy-start | bytes 220
  0.0 31.0 %copy-start.1 = (f32[16,1280]{1,0:T(8,128)S(1)}, f32[16,1280]{1,0:T(8,128)}, u32[]{:S(2)}) copy-start(f32[16,1280]{1,0:T(8,128)} %amp_ref.1) | copy-start | bytes 245764
  2.1 1.7 %collective-permute-start = (bf16[6,16,1536]{2,1,0:T(8,128)(2,1)S(1)}, bf16[6,16,1536]{2,1,0:T(8,128)(2,1)S(1)}, u32[]{:S(2)}, u32[]{:S(2)}) collective-permute-start(bf16[6,16,1536]{2,1,0:T(8,128)(2,1)S(1)} %get-tuple-element.8), channel_id=1, source_target_pairs={{0,16},{16,0},{1,17},{17,1},{2,18},{18,2},{3,19},{19,3},{4,20},{20... | collective-permute-start | bytes 884744 | tf_op jit(solution)/shard_map/ppermute | solution.py:472

commit v9 on v8

--- a/solution.py
+++ b/solution.py
@@ -367,7 +367,7 @@
     wide = SIDE * SIDE
     lane8 = lax.broadcasted_iota(jnp.int32, (8, LANES), 1)
     turns = steps * across
-    found = []
+    found, scales = [], []
     for big in range(0, turns, 8):
         smalls = []
         for turn in range(big, min(big + 8, turns)):
@@ -405,10 +405,11 @@
         image = jnp.concatenate(
             [jnp.concatenate([halves[0][g], halves[1][g]], axis=1) for g in range(8)], axis=0
         )
-        image = image * (1.0 / jnp.sum(image, axis=1, keepdims=True))
+        scales.append(1.0 / jnp.sum(image, axis=1, keepdims=True))
         high, low = split(image)
         found.append(jnp.concatenate([high, low, high], axis=1))
-    out_ref[...] = matmul(jnp.concatenate(found, axis=0), table[...])[0 : out_ref.shape[0]]
+    result = matmul(jnp.concatenate(found, axis=0), table[...]) * jnp.concatenate(scales, axis=0)
+    out_ref[...] = result[0 : out_ref.shape[0]]
 
 
 def spots_call(stars, devices, total_tiles, foot_rows, foot_cols, wind, strips, amplitude, table):

time: 35.4 us -> 35.2 us (level)
  no operation moved by 1% of the time
where the time goes in v9:
time: 35.2 us; the launch traced here: 35 us
  blocking collectives  26.3 us (75%)
  Pallas kernels  7.26 us (21%)
  between operations  0.72 us (2%)
  starting transfers between devices  0.53 us (2%)
    all_to_all x1, blocking collectives, shards(): lax.all_to_all(sent, 'dev', 0, 0, axis_index_groups=parities, tiled=True)  16.2 us
    all_to_all x1, blocking collectives, shards(): lax.all_to_all(chosen, 'dev', 0, 0, axis_index_groups=groups, tiled=True)  10 us
    pallas_call x1, Pallas kernels, spots_call(): pl.pallas_call(functools.partial(spots_kernel, stars, devices, total_tile...  3.99 us
    pallas_call x1, Pallas kernels, shards(): pl.pallas_call(functools.partial(crop_kernel, stars, devices), out_shape=...  2.07 us
  transfers between devices with their start and end apart: 1, of which 1 were waited for; matrix products, arithmetic and copies ran while one was open for 0% of the time, Pallas kernels for 1%

profile of v9, /device:TPU:0, one launch (start us, length us, event | category | flops | bytes accessed | tf_op | source)
XLA Modules:
  0.0 35.0 jit_solution(17546122582207447456)
XLA Ops:
  0.0 0.0 copy-start
  0.0 0.0 copy-start.3
  0.0 0.0 copy-start.4
  0.0 0.0 copy-start.5
  0.0 0.0 copy-start.2
  0.0 0.0 copy-start.6
  0.0 0.0 copy-start.1
  0.0 2.1 %crop.1 = (bf16[6,16,1536]{2,1,0:T(8,128)(2,1)S(1)}, bf16[6,16,1536]{2,1,0:T(8,128)(2,1)S(1)}) custom-call(s32[2,3]{1,0:T(2,128)} %bitcast.6, s32[2,3]{1,0:T(2,128)} %bitcast.10, bf16[3,32,16,4096]{3,2,1,0:T(8,128)(2,1)} %screens_ref.1), custom_call_target="tpu_custom_call" | custom-call | tf_op jit(solution)/shard_map/crop/pallas_call | solution.py:452
  2.1 0.5 %collective-permute-start = (bf16[6,16,1536]{2,1,0:T(8,128)(2,1)S(1)}, bf16[6,16,1536]{2,1,0:T(8,128)(2,1)S(1)}, u32[]{:S(2)}, u32[]{:S(2)}) collective-permute-start(bf16[6,16,1536]{2,1,0:T(8,128)(2,1)S(1)} %get-tuple-element.8), channel_id=1, source_target_pairs={{0,16},{16,0},{1,17},{17,1},{2,18},{18,2},{3,19},{19,3},{4,20},{20... | collective-permute-start | bytes 884744 | tf_op jit(solution)/shard_map/ppermute | solution.py:473
  3.3 0.0 copy-done.2
  3.3 0.3 table.1._
  3.7 0.2 collective-permute-done.rest_1_
  3.9 0.0 copy-done.4
  3.9 0.0 copy-done.5
  3.9 0.6 %spread.1 = bf16[8,8,2048]{2,1,0:T(8,128)(2,1)S(1)} custom-call(s32[2,3]{1,0:T(2,128)S(1)} %bitcast.7, s32[2,3]{1,0:T(2,128)S(1)} %bitcast.11, bf16[768,256]{1,0:T(8,128)(2,1)S(1)} %table.1._, bf16[6,16,1536]{2,1,0:T(8,128)(2,1)S(1)} %get-tuple-element.7.rest_0_, bf16[6,16,1536]{2,1,0:T(8,128)(2,1)S(1)} %collective-permute-done.rest_1_), custom_call_target="tpu_custom_call" | custom-call | tf_op jit(solution)/shard_map/spread/pallas_call | solution.py:487
  4.4 16.2 %all_to_all.10.in_ref = bf16[8,8,2048]{2,1,0:T(8,128)(2,1)S(1)} all-to-all(bf16[8,8,2048]{2,1,0:T(8,128)(2,1)S(1)} %spread.1), channel_id=1, replica_groups={{0,2,4,6,8,10,12,14},{1,3,5,7,9,11,13,15},{16,18,20,22,24,26,28,30},{17..., dimensions={0} | all-to-all | bytes 524288 | tf_op jit(solution)/shard_map/all_to_all | solution.py:496
  20.6 0.3 choose.1
  20.9 10.0 %all_to_all.11.in_ref = bf16[8,8,2048]{2,1,0:T(8,128)(2,1)S(1)} all-to-all(bf16[8,8,2048]{2,1,0:T(8,128)(2,1)S(1)} %choose.1), channel_id=1, replica_groups={{0,1,2,3,4,5,6,7},{8,9,10,11,12,13,14,15},{16,17,18,19,20,21,22,23},{24..., dimensions={0} | all-to-all | bytes 524288 | tf_op jit(solution)/shard_map/all_to_all | solution.py:505
  31.0 0.0 copy-done
  31.0 0.0 copy-done.3
  31.0 0.0 copy-done.6
  31.0 0.0 copy-done.1
  31.0 4.0 %spots.1 = f32[240,256]{1,0:T(8,128)} custom-call(s32[2,3]{1,0:T(2,128)S(1)} %bitcast.9, s32[2,3]{1,0:T(2,128)S(1)} %bitcast.12, s32[3,2,3]{2,1,0:T(2,128)S(1)} %bitcast.13, bf16[8,8,2048]{2,1,0:T(8,128)(2,1)S(1)} %all_to_all.11.in_ref, f32[16,1280]{1,0:T(8,128)S(1)} %copy-done.1, bf16[768,256]{1,0:T(8,128)(2,1)S(1)} %table.1._, ...), custom_call_target="tpu_custom_call" | custom-call | tf_op jit(solution)/shard_map/spots/pallas_call | solution.py:424
Async XLA Ops:
  0.0 31.0 %copy-start = (bf16[768,1024]{1,0:T(8,128)(2,1)S(1)}, bf16[768,1024]{1,0:T(8,128)(2,1)}, u32[]{:S(2)}) copy-start(bf16[768,1024]{1,0:T(8,128)(2,1)} %constant.4.clone.across_ref) | copy-start | bytes 4718596
  0.0 31.0 %copy-start.3 = (bf16[128,96]{1,0:T(8,128)(2,1)S(1)}, bf16[128,96]{1,0:T(8,128)(2,1)}, u32[]{:S(2)}) copy-start(bf16[128,96]{1,0:T(8,128)(2,1)} %constant.5.clone.down_ref) | copy-start | bytes 73732
  0.0 3.9 %copy-start.4 = (s32[3,2]{0,1:T(2,128)S(1)}, s32[3,2]{0,1:T(2,128)}, u32[]{:S(2)}) copy-start(s32[3,2]{0,1:T(2,128)} %param.10) | copy-start | bytes 76
  0.0 3.9 %copy-start.5 = (s32[3,2]{0,1:T(2,128)S(1)}, s32[3,2]{0,1:T(2,128)}, u32[]{:S(2)}) copy-start(s32[3,2]{0,1:T(2,128)} %param.11) | copy-start | bytes 76
  0.0 3.3 %copy-start.2 = (f32[6,16,16]{2,1,0:T(8,128)S(1)}, f32[6,16,16]{2,1,0:T(8,128)}, u32[]{:S(2)}) copy-start(f32[6,16,16]{2,1,0:T(8,128)} %refs_ref.1) | copy-start | bytes 18436
  0.0 31.0 %copy-start.6 = (s32[3,3,2]{1,2,0:T(2,128)S(1)}, s32[3,3,2]{1,2,0:T(2,128)}, u32[]{:S(2)}) copy-start(s32[3,3,2]{1,2,0:T(2,128)} %param.12) | copy-start | bytes 220
  0.0 31.0 %copy-start.1 = (f32[16,1280]{1,0:T(8,128)S(1)}, f32[16,1280]{1,0:T(8,128)}, u32[]{:S(2)}) copy-start(f32[16,1280]{1,0:T(8,128)} %amp_ref.1) | copy-start | bytes 245764
  2.1 1.7 %collective-permute-start = (bf16[6,16,1536]{2,1,0:T(8,128)(2,1)S(1)}, bf16[6,16,1536]{2,1,0:T(8,128)(2,1)S(1)}, u32[]{:S(2)}, u32[]{:S(2)}) collective-permute-start(bf16[6,16,1536]{2,1,0:T(8,128)(2,1)S(1)} %get-tuple-element.8), channel_id=1, source_target_pairs={{0,16},{16,0},{1,17},{17,1},{2,18},{18,2},{3,19},{19,3},{4,20},{20... | collective-permute-start | bytes 884744 | tf_op jit(solution)/shard_map/ppermute | solution.py:473

commit v10 on v9

--- a/solution.py
+++ b/solution.py
@@ -291,9 +291,7 @@
 def spots_kernel(
     stars,
     devices,
-    total_tiles,
     rows_ref,
-    cols_ref,
     wind_ref,
     in_ref,
     amp_ref,
@@ -412,7 +410,7 @@
     out_ref[...] = result[0 : out_ref.shape[0]]
 
 
-def spots_call(stars, devices, total_tiles, foot_rows, foot_cols, wind, strips, amplitude, table):
+def spots_call(stars, devices, foot_rows, wind, strips, amplitude, table):
     vmem = pl.BlockSpec(memory_space=pltpu.VMEM)
     steps, layers = wind.shape[0], wind.shape[2]
     depth = strips.shape[1]
@@ -422,9 +420,9 @@
     count = steps * subs
     padded = -(-count // 64) * 64
     return pl.pallas_call(
-        functools.partial(spots_kernel, stars, devices, total_tiles),
+        functools.partial(spots_kernel, stars, devices),
         out_shape=jax.ShapeDtypeStruct((count, SIDE * SIDE), F32),
-        in_specs=[vmem] * 8,
+        in_specs=[vmem] * 7,
         out_specs=vmem,
         scratch_shapes=[
             pltpu.VMEM((layers * HALF + 1, GROUP * depth, LANES), F32),
@@ -433,7 +431,7 @@
         ],
         compiler_params=pltpu.CompilerParams(vmem_limit_bytes=16 << 20),
         name="spots",
-    )(foot_rows, foot_cols, wind, strips, amplitude, table, table_across, down_table())
+    )(foot_rows, wind, strips, amplitude, table, table_across, down_table())
 
 
 def shards(screens, foot_rows, foot_cols, wind, amplitude, owner, refs):
@@ -504,7 +502,7 @@
     )(foot_rows, held_rows)
     strips = lax.all_to_all(chosen, "dev", 0, 0, axis_index_groups=groups, tiled=True)
     found = spots_call(
-        stars, devices, stars * tiles, foot_rows, foot_cols, wind, strips, amplitude, table
+        stars, devices, foot_rows, wind, strips, amplitude, table
     )
     return found.reshape(steps, 1, 1, subs, SIDE * SIDE)
 

time: 35.2 us -> 35.2 us (level)
  no operation moved by 1% of the time
where the time goes in v10:
time: 35.2 us; the launch traced here: 35 us
  blocking collectives  26.3 us (75%)
  Pallas kernels  7.26 us (21%)
  between operations  0.72 us (2%)
  starting transfers between devices  0.53 us (2%)
    all_to_all x1, blocking collectives, shards(): lax.all_to_all(sent, 'dev', 0, 0, axis_index_groups=parities, tiled=True)  16.2 us
    all_to_all x1, blocking collectives, shards(): lax.all_to_all(chosen, 'dev', 0, 0, axis_index_groups=groups, tiled=True)  10 us
    pallas_call x1, Pallas kernels, spots_call(): pl.pallas_call(functools.partial(spots_kernel, stars, devices), out_shape...  3.99 us
    pallas_call x1, Pallas kernels, shards(): pl.pallas_call(functools.partial(crop_kernel, stars, devices), out_shape=...  2.07 us
  transfers between devices with their start and end apart: 1, of which 1 were waited for; matrix products, arithmetic and copies ran while one was open for 0% of the time, Pallas kernels for 1%

profile of v10, /device:TPU:0, one launch (start us, length us, event | category | flops | bytes accessed | tf_op | source)
XLA Modules:
  0.0 35.0 jit_solution(13793555985279722079)
XLA Ops:
  0.0 0.0 copy-start
  0.0 0.0 copy-start.3
  0.0 0.0 copy-start.4
  0.0 0.0 copy-start.5
  0.0 0.0 copy-start.2
  0.0 0.0 copy-start.6
  0.0 0.0 copy-start.1
  0.0 2.1 %crop.1 = (bf16[6,16,1536]{2,1,0:T(8,128)(2,1)S(1)}, bf16[6,16,1536]{2,1,0:T(8,128)(2,1)S(1)}) custom-call(s32[2,3]{1,0:T(2,128)} %bitcast.6, s32[2,3]{1,0:T(2,128)} %bitcast.10, bf16[3,32,16,4096]{3,2,1,0:T(8,128)(2,1)} %screens_ref.1), custom_call_target="tpu_custom_call" | custom-call | tf_op jit(solution)/shard_map/crop/pallas_call | solution.py:450
  2.1 0.5 %collective-permute-start = (bf16[6,16,1536]{2,1,0:T(8,128)(2,1)S(1)}, bf16[6,16,1536]{2,1,0:T(8,128)(2,1)S(1)}, u32[]{:S(2)}, u32[]{:S(2)}) collective-permute-start(bf16[6,16,1536]{2,1,0:T(8,128)(2,1)S(1)} %get-tuple-element.8), channel_id=1, source_target_pairs={{0,16},{16,0},{1,17},{17,1},{2,18},{18,2},{3,19},{19,3},{4,20},{20... | collective-permute-start | bytes 884744 | tf_op jit(solution)/shard_map/ppermute | solution.py:471
  3.3 0.0 copy-done.2
  3.3 0.3 table.1._
  3.7 0.2 collective-permute-done.rest_1_
  3.9 0.0 copy-done.4
  3.9 0.0 copy-done.5
  3.9 0.6 %spread.1 = bf16[8,8,2048]{2,1,0:T(8,128)(2,1)S(1)} custom-call(s32[2,3]{1,0:T(2,128)S(1)} %bitcast.7, s32[2,3]{1,0:T(2,128)S(1)} %bitcast.11, bf16[768,256]{1,0:T(8,128)(2,1)S(1)} %table.1._, bf16[6,16,1536]{2,1,0:T(8,128)(2,1)S(1)} %get-tuple-element.7.rest_0_, bf16[6,16,1536]{2,1,0:T(8,128)(2,1)S(1)} %collective-permute-done.rest_1_), custom_call_target="tpu_custom_call" | custom-call | tf_op jit(solution)/shard_map/spread/pallas_call | solution.py:485
  4.4 16.2 %all_to_all.10.in_ref = bf16[8,8,2048]{2,1,0:T(8,128)(2,1)S(1)} all-to-all(bf16[8,8,2048]{2,1,0:T(8,128)(2,1)S(1)} %spread.1), channel_id=1, replica_groups={{0,2,4,6,8,10,12,14},{1,3,5,7,9,11,13,15},{16,18,20,22,24,26,28,30},{17..., dimensions={0} | all-to-all | bytes 524288 | tf_op jit(solution)/shard_map/all_to_all | solution.py:494
  20.6 0.3 choose.1
  20.9 10.0 %all_to_all.11.in_ref = bf16[8,8,2048]{2,1,0:T(8,128)(2,1)S(1)} all-to-all(bf16[8,8,2048]{2,1,0:T(8,128)(2,1)S(1)} %choose.1), channel_id=1, replica_groups={{0,1,2,3,4,5,6,7},{8,9,10,11,12,13,14,15},{16,17,18,19,20,21,22,23},{24..., dimensions={0} | all-to-all | bytes 524288 | tf_op jit(solution)/shard_map/all_to_all | solution.py:503
  31.0 0.0 copy-done
  31.0 0.0 copy-done.3
  31.0 0.0 copy-done.6
  31.0 0.0 copy-done.1
  31.0 4.0 %spots.1 = f32[240,256]{1,0:T(8,128)} custom-call(s32[2,3]{1,0:T(2,128)S(1)} %bitcast.9, s32[3,2,3]{2,1,0:T(2,128)S(1)} %bitcast.12, bf16[8,8,2048]{2,1,0:T(8,128)(2,1)S(1)} %all_to_all.11.in_ref, f32[16,1280]{1,0:T(8,128)S(1)} %copy-done.1, bf16[768,256]{1,0:T(8,128)(2,1)S(1)} %table.1._, bf16[768,1024]{1,0:T(8,128)(2,1)S(1)} %copy-done, ...), custom_call_target="tpu_custom_call" | custom-call | tf_op jit(solution)/shard_map/spots/pallas_call | solution.py:422
Async XLA Ops:
  0.0 31.0 %copy-start = (bf16[768,1024]{1,0:T(8,128)(2,1)S(1)}, bf16[768,1024]{1,0:T(8,128)(2,1)}, u32[]{:S(2)}) copy-start(bf16[768,1024]{1,0:T(8,128)(2,1)} %constant.4.clone.across_ref) | copy-start | bytes 4718596
  0.0 31.0 %copy-start.3 = (bf16[128,96]{1,0:T(8,128)(2,1)S(1)}, bf16[128,96]{1,0:T(8,128)(2,1)}, u32[]{:S(2)}) copy-start(bf16[128,96]{1,0:T(8,128)(2,1)} %constant.5.clone.down_ref) | copy-start | bytes 73732
  0.0 3.9 %copy-start.4 = (s32[3,2]{0,1:T(2,128)S(1)}, s32[3,2]{0,1:T(2,128)}, u32[]{:S(2)}) copy-start(s32[3,2]{0,1:T(2,128)} %param.10) | copy-start | bytes 76
  0.0 3.9 %copy-start.5 = (s32[3,2]{0,1:T(2,128)S(1)}, s32[3,2]{0,1:T(2,128)}, u32[]{:S(2)}) copy-start(s32[3,2]{0,1:T(2,128)} %param.11) | copy-start | bytes 76
  0.0 3.3 %copy-start.2 = (f32[6,16,16]{2,1,0:T(8,128)S(1)}, f32[6,16,16]{2,1,0:T(8,128)}, u32[]{:S(2)}) copy-start(f32[6,16,16]{2,1,0:T(8,128)} %refs_ref.1) | copy-start | bytes 18436
  0.0 31.0 %copy-start.6 = (s32[3,3,2]{1,2,0:T(2,128)S(1)}, s32[3,3,2]{1,2,0:T(2,128)}, u32[]{:S(2)}) copy-start(s32[3,3,2]{1,2,0:T(2,128)} %param.12) | copy-start | bytes 220
  0.0 31.0 %copy-start.1 = (f32[16,1280]{1,0:T(8,128)S(1)}, f32[16,1280]{1,0:T(8,128)}, u32[]{:S(2)}) copy-start(f32[16,1280]{1,0:T(8,128)} %amp_ref.1) | copy-start | bytes 245764
  2.1 1.7 %collective-permute-start = (bf16[6,16,1536]{2,1,0:T(8,128)(2,1)S(1)}, bf16[6,16,1536]{2,1,0:T(8,128)(2,1)S(1)}, u32[]{:S(2)}, u32[]{:S(2)}) collective-permute-start(bf16[6,16,1536]{2,1,0:T(8,128)(2,1)S(1)} %get-tuple-element.8), channel_id=1, source_target_pairs={{0,16},{16,0},{1,17},{17,1},{2,18},{18,2},{3,19},{19,3},{4,20},{20... | collective-permute-start | bytes 884744 | tf_op jit(solution)/shard_map/ppermute | solution.py:471
